TPU v7x, 32 devices: a whole 2x2x4 slice. The times are simulated.
32 devices in a mesh: pipe: 4 (over y, core), expert: 8 (over z, x).
Axes of the slice: x: 2, y: 2, z: 4, core: 2. Of those that a mesh axis runs over, the one named last changes fastest.
Arguments:
- layer_input: bfloat16 [4, 512, 2880], P('pipe', 'expert'), may hold values from -6 to 6
- grad_output: bfloat16 [4, 512, 2880], P('pipe', 'expert'), may hold values from -6 to 6
- expert_ids: int32 [4, 512, 4], P('pipe', 'expert'), may hold values from 0 to 127, as said below
- gate_probs: float32 [4, 512, 4], P('pipe', 'expert'), may hold values from 0.05 to 1
- w_gate: bfloat16 [4, 2880, 2880], P('pipe', 'expert'), may hold values from -0.109375 to 0.109375
- w_up: bfloat16 [4, 2880, 2880], P('pipe', 'expert'), may hold values from -0.109375 to 0.109375
- w_down: bfloat16 [4, 2880, 2880], P('pipe', 'expert'), may hold values from -0.109375 to 0.109375
Outputs:
- grad_gate: bfloat16 [4, 2880, 2880], P('pipe', 'expert')
- grad_up: bfloat16 [4, 2880, 2880], P('pipe', 'expert')
- grad_down: bfloat16 [4, 2880, 2880], P('pipe', 'expert')
- grad_prev: bfloat16 [4, 512, 2880], P('pipe', 'expert')
Inputs may be any that keep to these rules, and one draw needn't show every extreme that they name: `expert_ids`: in each section, within the 64 tokens of one device, no expert is named by more than 4 tokens; in each section one expert below 1, the same for all devices of that section, is named by exactly 4 tokens of every device; a token names 4 different experts.
All inputs are finite; a program needn't handle non-finite values.
Results may differ from a plain program's by a relative error of at most 0.0085.
Values may be sent and summed in bfloat16 or wider, within the bound.
No kernel may reach another device: no remote copies, remote signals or barrier semaphores. Data moves between devices by JAX's collectives and lax.ppermute only.
A program may use at most 64 MiB of HBM per device.

v0:
```python
import jax
import jax.numpy as jnp
from jax import lax
from jax.sharding import PartitionSpec as P

SLICES = 8
CAP = 4


def from_behind(value, axis, steps):
    count = lax.axis_size(axis)
    leading, last = (max(0, -steps), min(count, count - steps))
    return lax.ppermute(value, axis, [(source, source + steps) for source in range(leading, last)])


def silu_parts(pre_gate):
    sigma = jax.nn.sigmoid(pre_gate)
    return (pre_gate * sigma, sigma * (1.0 + pre_gate * (1.0 - sigma)))


def contract_first(left, right):
    return lax.dot_general(
        left, right, (((0,), (0,)), ((), ())), preferred_element_type=jnp.float32
    )


def contract_last(left, right):
    return lax.dot_general(
        left, right, (((1,), (1,)), ((), ())), preferred_element_type=jnp.float32
    )


def expert_math(received_input, received_cotan, weight_gate, weight_up, weight_down):
    senders, slot_count, width = received_input.shape
    flat_input = received_input.reshape(senders * slot_count, width)
    flat_cotan = received_cotan.reshape(senders * slot_count, width)
    pre_gate = contract_last(flat_input, weight_gate)
    pre_up = contract_last(flat_input, weight_up)
    silu_val, silu_grad = silu_parts(pre_gate)
    hidden = (silu_val * pre_up).astype(jnp.bfloat16)
    hidden_grad = contract_last(flat_cotan, weight_down)
    grad_pre_gate = (hidden_grad * pre_up * silu_grad).astype(jnp.bfloat16)
    grad_pre_up = (hidden_grad * silu_val).astype(jnp.bfloat16)
    partial_value = jnp.dot(grad_pre_gate, weight_gate, preferred_element_type=jnp.float32)
    partial_value = partial_value + jnp.dot(
        grad_pre_up, weight_up, preferred_element_type=jnp.float32
    )
    partial_value = partial_value.astype(jnp.bfloat16).reshape(senders, slot_count, width)
    hidden_width = hidden.shape[1]
    return (
        partial_value,
        hidden.reshape(senders, slot_count, hidden_width),
        grad_pre_gate.reshape(senders, slot_count, hidden_width),
        grad_pre_up.reshape(senders, slot_count, hidden_width),
    )


def body(layer_input, grad_output, expert_ids, gate_probs, w_gate, w_up, w_down):
    inputs = layer_input[0]
    cotan = grad_output[0]
    chosen = expert_ids[0]
    probs = gate_probs[0]
    weight_gate = w_gate[0]
    weight_up = w_up[0]
    weight_down = w_down[0]
    peers = lax.axis_size("expert")
    flight = peers // SLICES
    token_count, top_count = chosen.shape
    width = inputs.shape[1]
    capacity = CAP
    flat_ids = chosen.reshape(token_count * top_count)
    labels = jnp.arange(flight, dtype=jnp.int32)
    matched = (flat_ids[:, None] == labels[None, :]).astype(jnp.int32)
    ranks = jnp.cumsum(matched, axis=0) - 1
    slot_ids = jnp.arange(capacity, dtype=jnp.int32)
    chooser = (matched[:, :, None] > 0) & (ranks[:, :, None] == slot_ids[None, None, :])
    chooser = chooser.reshape(token_count * top_count, flight * capacity).T.astype(jnp.bfloat16)
    token_chooser = jnp.sum(chooser.reshape(flight * capacity, token_count, top_count), axis=2)
    scaled = (probs[:, :, None] * cotan[:, None, :].astype(jnp.float32)).astype(jnp.bfloat16)
    scaled = scaled.reshape(token_count * top_count, width)
    send_input = jnp.dot(token_chooser, inputs, preferred_element_type=jnp.float32).astype(
        jnp.bfloat16
    )
    send_cotan = jnp.dot(chooser, scaled, preferred_element_type=jnp.float32).astype(jnp.bfloat16)
    send_input = jnp.repeat(send_input.reshape(flight, capacity, width), SLICES, axis=0)
    send_cotan = jnp.repeat(send_cotan.reshape(flight, capacity, width), SLICES, axis=0)
    received_input, received_cotan = (
        lax.all_to_all(send_input, "expert", split_axis=0, concat_axis=0, tiled=True),
        lax.all_to_all(send_cotan, "expert", split_axis=0, concat_axis=0, tiled=True),
    )
    partial_value, hidden, grad_pre_gate, grad_pre_up = expert_math(
        received_input, received_cotan, weight_gate, weight_up, weight_down
    )
    returned = lax.all_to_all(partial_value, "expert", split_axis=0, concat_axis=0, tiled=True)
    slot_total = received_input.shape[0] * received_input.shape[1]
    flat_input = received_input.reshape(slot_total, width)
    flat_cotan = received_cotan.reshape(slot_total, width)
    hidden_width = hidden.shape[2]
    grad_down = contract_first(hidden.reshape(slot_total, hidden_width), flat_cotan).astype(
        jnp.bfloat16
    )
    grad_gate = contract_first(grad_pre_gate.reshape(slot_total, hidden_width), flat_input).astype(
        jnp.bfloat16
    )
    grad_up = contract_first(grad_pre_up.reshape(slot_total, hidden_width), flat_input).astype(
        jnp.bfloat16
    )
    combined = jnp.sum(
        returned.astype(jnp.float32).reshape(flight, SLICES, capacity, width), axis=1
    )
    combined = combined.reshape(flight * capacity, width)
    input_grad = jnp.dot(
        token_chooser.T.astype(jnp.float32),
        combined,
        precision=lax.Precision.HIGHEST,
        preferred_element_type=jnp.float32,
    )
    shifted = from_behind(input_grad.astype(jnp.bfloat16)[None], "pipe", -1)
    return (grad_gate[None], grad_up[None], grad_down[None], shifted)


def solution(mesh):
    return jax.shard_map(
        body,
        mesh=mesh,
        in_specs=(
            P("pipe", "expert", None),
            P("pipe", "expert", None),
            P("pipe", "expert", None),
            P("pipe", "expert", None),
            P("pipe", "expert", None),
            P("pipe", "expert", None),
            P("pipe", "expert", None),
        ),
        out_specs=(
            P("pipe", "expert", None),
            P("pipe", "expert", None),
            P("pipe", "expert", None),
            P("pipe", "expert", None),
        ),
        check_vma=False,
    )
```

profile of v0, /device:TPU:1, one launch (start us, length us, event | category | flops | bytes accessed | tf_op | source)
XLA Modules:
  0.0 58.9 jit_solution(13846318058327578023)
XLA Ops:
  0.6 0.0 copy-start
  0.6 0.8 %broadcast_compare_fusion = (pred[1,64,4]{1,2,0:T(4,128)(4,1)S(1)}, s32[1,64,4]{1,2,0:T(4,128)S(1)}) fusion(s32[1,64,4]{1,2,0:T(4,128)} %param.9), kind=kLoop, calls=%fused_computation.44 | loop fusion | flops 768 | bytes 2304 | tf_op jit(solution)/shard_map/gt | solution.py:76
  1.5 0.1 copy.18
  1.6 0.1 reshape.258
  1.7 0.3 reduce-window.6
  2.0 0.2 slice_reduce_fusion
  2.2 0.1 reshape.253
  2.3 0.2 reduce-window.9
  2.5 0.1 broadcast.121
  2.6 0.1 reshape.254
  2.7 0.1 copy.20
  2.8 1.1 %convolution_convert_fusion.4 = bf16[4,2880]{1,0:T(4,128)(2,1)S(1)} fusion(bf16[4,64]{1,0:T(4,128)(2,1)S(1)} %fusion.19, bf16[1,64,2880]{2,1,0:T(8,128)(2,1)} %param.7), kind=kOutput, calls=%fused_computation.10 | convolution fusion | flops 1486080 | bytes 392192 | tf_op jit(solution)/shard_map/dot_general | solution.py:81
  3.9 0.7 %reshape.255 = bf16[8,4,2880]{2,1,0:T(4,128)(2,1)} broadcast(bf16[4,2880]{1,0:T(4,128)(2,1)S(1)} %convolution_convert_fusion.4), dimensions={1,2} | broadcast | bytes 207360 | tf_op jit(solution)/shard_map/reshape | solution.py:85
  4.7 6.3 %all-to-all-start.1 = ((bf16[8,4,2880]{2,1,0:T(4,128)(2,1)}), bf16[8,4,2880]{2,1,0:T(4,128)(2,1)S(1)}, u32[]{:S(2)}, u32[]{:S(2)}) async-start(bf16[8,4,2880]{2,1,0:T(4,128)(2,1)} %reshape.255), calls=%async_computation.1 | async-start | bytes 376832 | tf_op jit(solution)/shard_map/all_to_all | solution.py:88
  11.0 0.8 %copy.19 = f32[64,4]{1,0:T(8,128)S(1)} copy(f32[64,4]{0,1:T(4,128)} %bitcast.60) | data formatting | bytes 2048 | tf_op jit(solution)/shard_map/mul | solution.py:79
  11.8 1.0 %bitcast_convert_fusion = f32[64,2880]{1,0:T(8,128)S(1)} fusion(bf16[1,64,2880]{2,1,0:T(8,128)(2,1)} %param.8), kind=kLoop, calls=%fused_computation.22 | loop fusion | flops 184320 | bytes 1105920 | tf_op jit(solution)/shard_map/convert_element_type | solution.py:79
  12.8 1.7 %multiply_convert_fusion = bf16[64,4,2880]{2,1,0:T(4,128)(2,1)} fusion(f32[64,2880]{1,0:T(8,128)S(1)} %bitcast_convert_fusion, f32[64,4]{1,0:T(8,128)S(1)} %copy.19), kind=kLoop, calls=%fused_computation.12 | loop fusion | flops 1474560 | bytes 2212864 | tf_op jit(solution)/shard_map/convert_element_type | solution.py:79
  14.6 0.1 fusion.25
  14.6 0.1 copy.17
  14.8 0.1 gt.17
  14.9 3.6 %convert_element_type.95 = bf16[256,2880]{1,0:T(8,128)(2,1)} reshape(bf16[64,4,2880]{2,1,0:T(4,128)(2,1)} %multiply_convert_fusion) | data formatting | bytes 2949120 | tf_op jit(solution)/shard_map/convert_element_type | solution.py:79
  18.5 1.7 %convolution_convert_fusion.5 = bf16[4,2880]{1,0:T(4,128)(2,1)S(1)} fusion(bf16[256,2880]{1,0:T(8,128)(2,1)} %convert_element_type.95, s32[256]{0:T(256)S(1)} %fusion.25, pred[256]{0:T(512)(128)(4,1)S(1)} %gt.17), kind=kOutput, calls=%fused_computation.11 | convolution fusion | flops 5911808 | bytes 1498880 | tf_op jit(solution)/shard_map/dot_general | solution.py:84
  20.2 0.0 all-to-all-done.1
  20.2 0.7 %reshape.251 = bf16[8,4,2880]{2,1,0:T(4,128)(2,1)} broadcast(bf16[4,2880]{1,0:T(4,128)(2,1)S(1)} %convolution_convert_fusion.5), dimensions={1,2} | broadcast | bytes 207360 | tf_op jit(solution)/shard_map/reshape | solution.py:86
  20.9 5.4 %all-to-all-start = ((bf16[8,4,2880]{2,1,0:T(4,128)(2,1)}), bf16[8,4,2880]{2,1,0:T(4,128)(2,1)S(1)}, u32[]{:S(2)}, u32[]{:S(2)}) async-start(bf16[8,4,2880]{2,1,0:T(4,128)(2,1)} %reshape.251), calls=%async_computation | async-start | bytes 376832 | tf_op jit(solution)/shard_map/all_to_all | solution.py:89
  26.3 0.1 reshape.256
  26.4 0.0 copy-done
  26.4 0.0 copy-start.1
  26.4 0.7 %fusion.7 = f32[32,360]{1,0:T(8,128)S(1)} fusion(bf16[32,2880]{1,0:T(8,128)(2,1)S(1)} %reshape.256, bf16[1,360,2880]{2,1,0:T(8,128)(2,1)S(1)} %copy-done), kind=kOutput, calls=%fused_computation.15 | convolution fusion | flops 66355200 | bytes 2304000 | tf_op jit(solution)/shard_map/dot_general | solution.py:28
  27.2 0.9 %copy-done.1 = bf16[1,360,2880]{2,1,0:T(8,128)(2,1)S(1)} copy-done((bf16[1,360,2880]{2,1,0:T(8,128)(2,1)S(1)}, bf16[1,360,2880]{2,1,0:T(8,128)(2,1)}, u32[]{:S(2)}) %copy-start.1) | copy-done | bytes 2073624
  28.0 0.7 %fusion.10 = f32[32,360]{1,0:T(8,128)S(1)} fusion(bf16[32,2880]{1,0:T(8,128)(2,1)S(1)} %reshape.256, bf16[1,360,2880]{2,1,0:T(8,128)(2,1)S(1)} %copy-done.1), kind=kOutput, calls=%fused_computation.18 | convolution fusion | flops 66355200 | bytes 2304000 | tf_op jit(solution)/shard_map/dot_general | solution.py:28
  28.7 4.2 %all-to-all-done = bf16[8,4,2880]{2,1,0:T(4,128)(2,1)S(1)} async-done(((bf16[8,4,2880]{2,1,0:T(4,128)(2,1)}), bf16[8,4,2880]{2,1,0:T(4,128)(2,1)S(1)}, u32[]{:S(2)}, u32[]{:S(2)}) %all-to-all-start) | async-done | bytes 184352 | tf_op jit(solution)/shard_map/all_to_all | solution.py:89
  32.9 0.1 reshape.252
  33.0 0.0 copy-start.2
  33.0 2.5 %multiply_convert_fusion.2 = (bf16[32,360]{1,0:T(8,128)(2,1)S(1)}, bf16[32,360]{1,0:T(8,128)(2,1)S(1)}) fusion(f32[32,360]{1,0:T(8,128)S(1)} %fusion.7, f32[32,360]{1,0:T(8,128)S(1)} %fusion.10, bf16[32,2880]{1,0:T(8,128)(2,1)S(1)} %reshape.252, bf16[1,360,2880]{2,1,0:T(8,128)(2,1)} %param.13), kind=kOutput, calls=%fused_computation.26 | convolution fusion | flops 66504960 | bytes 2396160 | tf_op jit(solution)/shard_map/dot_general | solution.py:28
  35.5 0.4 fusion.5
  35.9 0.0 copy-done.2
  35.9 0.4 fusion.4
  36.3 0.1 reshape.257
  36.4 9.0 %all_to_all.15 = bf16[8,4,2880]{2,1,0:T(4,128)(2,1)S(1)} all-to-all(bf16[8,4,2880]{2,1,0:T(4,128)(2,1)S(1)} %reshape.257), channel_id=1, replica_groups=mesh['pipe'=4,'expert'=8] {'expert'}, dimensions={0} | all-to-all | bytes 368640 | tf_op jit(solution)/shard_map/all_to_all | solution.py:94
  45.4 0.1 convert_reduce_fusion
  45.5 0.5 fusion.3
  46.0 5.7 %collective-permute-start = (bf16[1,64,2880]{2,1,0:T(8,128)(2,1)S(1)}, bf16[1,64,2880]{2,1,0:T(8,128)(2,1)S(1)}, u32[]{:S(2)}, u32[]{:S(2)}) collective-permute-start(bf16[1,64,2880]{2,1,0:T(8,128)(2,1)S(1)} %fusion.3), channel_id=1, source_target_pairs={{8,0},{16,8},{24,16},{9,1},{17,9},{25,17},{10,2},{18,10},{26,18},{... | collective-permute-start | bytes 1105928 | tf_op jit(solution)/shard_map/ppermute | solution.py:13
  51.7 2.1 %fusion.1 = bf16[1,360,2880]{2,1,0:T(8,128)(2,1)} fusion(bf16[32,360]{1,0:T(8,128)(2,1)S(1)} %get-tuple-element.4, bf16[32,2880]{1,0:T(8,128)(2,1)S(1)} %reshape.256), kind=kOutput, calls=%fused_computation.4 | convolution fusion | flops 67392000 | bytes 2280960 | tf_op jit(solution)/shard_map/dot_general | solution.py:22
  53.8 2.1 %fusion = bf16[1,360,2880]{2,1,0:T(8,128)(2,1)} fusion(bf16[32,360]{1,0:T(8,128)(2,1)S(1)} %get-tuple-element.5, bf16[32,2880]{1,0:T(8,128)(2,1)S(1)} %reshape.256), kind=kOutput, calls=%fused_computation.3 | convolution fusion | flops 67392000 | bytes 2280960 | tf_op jit(solution)/shard_map/dot_general | solution.py:22
  55.9 2.1 %fusion.2 = bf16[1,360,2880]{2,1,0:T(8,128)(2,1)} fusion(bf16[32,2880]{1,0:T(8,128)(2,1)S(1)} %reshape.252, f32[32,360]{1,0:T(8,128)S(1)} %fusion.10, f32[32,360]{1,0:T(8,128)S(1)} %fusion.7), kind=kOutput, calls=%fused_computation.5 | convolution fusion | flops 67461120 | bytes 2350080 | tf_op jit(solution)/shard_map/dot_general | solution.py:22
  58.0 0.1 collective-permute-done
  58.1 0.7 %copy.22 = bf16[1,64,2880]{2,1,0:T(8,128)(2,1)} copy(bf16[1,64,2880]{2,1,0:T(8,128)(2,1)S(1)} %collective-permute-done) | data formatting | bytes 737280
  (3 shorter events, 0.0 us)
Async XLA Ops:
  0.6 25.8 %copy-start = (bf16[1,360,2880]{2,1,0:T(8,128)(2,1)S(1)}, bf16[1,360,2880]{2,1,0:T(8,128)(2,1)}, u32[]{:S(2)}) copy-start(bf16[1,360,2880]{2,1,0:T(8,128)(2,1)} %param.11) | copy-start | bytes 6220804
  4.7 15.5 %all-to-all-start.1 = ((bf16[8,4,2880]{2,1,0:T(4,128)(2,1)}), bf16[8,4,2880]{2,1,0:T(4,128)(2,1)S(1)}, u32[]{:S(2)}, u32[]{:S(2)}) async-start(bf16[8,4,2880]{2,1,0:T(4,128)(2,1)} %reshape.255), calls=%async_computation.1 | async-start | bytes 376832 | tf_op jit(solution)/shard_map/all_to_all | solution.py:88
  20.9 12.0 %all-to-all-start = ((bf16[8,4,2880]{2,1,0:T(4,128)(2,1)}), bf16[8,4,2880]{2,1,0:T(4,128)(2,1)S(1)}, u32[]{:S(2)}, u32[]{:S(2)}) async-start(bf16[8,4,2880]{2,1,0:T(4,128)(2,1)} %reshape.251), calls=%async_computation | async-start | bytes 376832 | tf_op jit(solution)/shard_map/all_to_all | solution.py:89
  26.4 1.6 %copy-start.1 = (bf16[1,360,2880]{2,1,0:T(8,128)(2,1)S(1)}, bf16[1,360,2880]{2,1,0:T(8,128)(2,1)}, u32[]{:S(2)}) copy-start(bf16[1,360,2880]{2,1,0:T(8,128)(2,1)} %param.12) | copy-start | bytes 6220804
  33.0 2.9 %copy-start.2 = (bf16[1,360,2880]{2,1,0:T(8,128)(2,1)S(1)}, bf16[1,360,2880]{2,1,0:T(8,128)(2,1)}, u32[]{:S(2)}) copy-start(bf16[1,360,2880]{2,1,0:T(8,128)(2,1)} %param.12) | copy-start | bytes 6220804
  46.0 12.1 %collective-permute-start = (bf16[1,64,2880]{2,1,0:T(8,128)(2,1)S(1)}, bf16[1,64,2880]{2,1,0:T(8,128)(2,1)S(1)}, u32[]{:S(2)}, u32[]{:S(2)}) collective-permute-start(bf16[1,64,2880]{2,1,0:T(8,128)(2,1)S(1)} %fusion.3), channel_id=1, source_target_pairs={{8,0},{16,8},{24,16},{9,1},{17,9},{25,17},{10,2},{18,10},{26,18},{... | collective-permute-start | bytes 1105928 | tf_op jit(solution)/shard_map/ppermute | solution.py:13
where the time goes:
time: 59.5 us; the launch traced here: 58.9 us
  starting transfers between devices  17.5 us (29%)
  matrix products  14.3 us (24%)
  blocking collectives  9.03 us (15%)
  local copies, waits for them, and re-layouts  8.66 us (15%)
  waiting for transfers between devices  4.31 us (7%)
  other arithmetic  4.3 us (7%)
  between operations  0.77 us (1%)
    all_to_all x1, blocking collectives, body(): lax.all_to_all(partial_value, 'expert', split_axis=0, concat_axis=0, tile...  9.03 us
    all_to_all x1, starting transfers between devices, body(): lax.all_to_all(send_input, 'expert', split_axis=0, concat_axis=0, tiled=T...  6.34 us
    dot_general x3, matrix products, contract_first(): lax.dot_general(left, right, (((0,), (0,)), ((), ())), preferred_element_...  6.26 us
    ppermute x1, starting transfers between devices, from_behind(): lax.ppermute(value, axis, [(source, source + steps) for source in range(l...  5.7 us
    all_to_all x1, starting transfers between devices, body(): lax.all_to_all(send_cotan, 'expert', split_axis=0, concat_axis=0, tiled=T...  5.44 us
    all_to_all x1, waiting for transfers between devices, body(): lax.all_to_all(send_cotan, 'expert', split_axis=0, concat_axis=0, tiled=T...  4.17 us
    dot_general x3, matrix products, contract_last(): lax.dot_general(left, right, (((1,), (1,)), ((), ())), preferred_element_...  3.88 us
    convert_element_type x1, local copies, waits for them, and re-layouts, body(): (probs[:, :, None] * cotan[:, None, :].astype(jnp.float32)).astype(jnp.bf...  3.59 us
  transfers between devices with their start and end apart: 3, of which 2 were waited for; matrix products, arithmetic and copies ran while one was open for 29% of the time, Pallas kernels for 0%

commit v1 on v0

v1 whole, which is shorter than its diff:
```python
import functools

import jax
import jax.numpy as jnp
from jax import lax
from jax.experimental import pallas as pl
from jax.experimental.pallas import tpu as pltpu
from jax.sharding import PartitionSpec as P

SLICES = 8
CAP = 4
PAIR = 2 * CAP
LANES = 128

VMEM = pl.BlockSpec(memory_space=pltpu.VMEM)


def contract_last(left, right):
    return lax.dot_general(
        left, right, (((1,), (1,)), ((), ())), preferred_element_type=jnp.float32
    )


def contract_first(left, right):
    return lax.dot_general(
        left, right, (((0,), (0,)), ((), ())), preferred_element_type=jnp.float32
    )


def select_kernel(flight, ids_ref, probs_ref, input_ref, cotan_ref, rows_ref, slots_ref):
    ids = ids_ref[...]
    probs = probs_ref[...]
    tokens = ids.shape[1]
    before = lax.broadcasted_iota(jnp.int32, (tokens, tokens), 0) < lax.broadcasted_iota(
        jnp.int32, (tokens, tokens), 1
    )
    before = before.astype(jnp.float32).astype(jnp.bfloat16)
    row = lax.broadcasted_iota(jnp.int32, (PAIR, tokens), 0)
    token = lax.broadcasted_iota(jnp.int32, (PAIR, tokens), 1).astype(jnp.float32)
    slot = lax.rem(row, CAP)
    for expert in range(flight):
        matched = ids == expert
        hit = jnp.sum(jnp.where(matched, 1.0, 0.0), axis=0, keepdims=True)
        prob = jnp.sum(jnp.where(matched, probs, 0.0), axis=0, keepdims=True)
        hits = jnp.broadcast_to(hit, (PAIR, tokens))
        ranks = jnp.dot(hits.astype(jnp.bfloat16), before, preferred_element_type=jnp.float32)
        chosen = jnp.where((hits > 0.5) & (ranks.astype(jnp.int32) == slot), 1.0, 0.0)
        scale = jnp.sum(chosen * prob, axis=1, keepdims=True)
        number = jnp.sum(chosen * token, axis=1, keepdims=True)
        chooser = chosen.astype(jnp.bfloat16)
        taken = jnp.dot(chooser, input_ref[...], preferred_element_type=jnp.float32)
        cotan = jnp.dot(chooser, cotan_ref[...], preferred_element_type=jnp.float32) * scale
        wide = lax.broadcasted_iota(jnp.int32, taken.shape, 0) < CAP
        rows_ref[pl.ds(expert * PAIR, PAIR), :] = jnp.where(wide, taken, cotan).astype(
            jnp.bfloat16
        )
        slots_ref[pl.ds(expert * PAIR, PAIR), :] = jnp.broadcast_to(number, (PAIR, LANES))


def select_rows(ids, probs, inputs, cotan, flight):
    width = inputs.shape[1]
    return pl.pallas_call(
        functools.partial(select_kernel, flight),
        out_shape=(
            jax.ShapeDtypeStruct((flight * PAIR, width), jnp.bfloat16),
            jax.ShapeDtypeStruct((flight * PAIR, LANES), jnp.float32),
        ),
        in_specs=[VMEM] * 4,
        out_specs=(VMEM, VMEM),
        compiler_params=pltpu.CompilerParams(vmem_limit_bytes=8 << 20),
        name="select",
    )(ids, probs, inputs, cotan)


def main_kernel(pieces, split, *refs):
    row_refs, (gate_ref, up_ref, down_ref) = refs[:pieces], refs[pieces : pieces + 3]
    all_ref, gate_out, up_out, hidden_out = refs[pieces + 3 : pieces + 7]
    partial_refs = refs[pieces + 7 :]
    start = 0
    for ref in row_refs:
        all_ref[pl.ds(start, ref.shape[0]), :] = ref[...]
        start += ref.shape[0]
    rows = all_ref[...]
    total = rows.shape[0]
    pre_gate = contract_last(rows, gate_ref[...])
    pre_up = contract_last(rows, up_ref[...])
    hidden_grad = pltpu.roll(contract_last(rows, down_ref[...]), total - CAP, 0)
    sigma = jax.nn.sigmoid(pre_gate)
    silu_val = pre_gate * sigma
    silu_grad = sigma * (1.0 + pre_gate * (1.0 - sigma))
    first = lax.rem(lax.broadcasted_iota(jnp.int32, pre_gate.shape, 0), PAIR) < CAP
    hidden = jnp.where(first, silu_val * pre_up, 0.0)
    grad_gate = jnp.where(first, hidden_grad * pre_up * silu_grad, 0.0)
    grad_up = jnp.where(first, hidden_grad * silu_val, 0.0)
    gate_out[...] = grad_gate.astype(jnp.bfloat16)
    up_out[...] = grad_up.astype(jnp.bfloat16)
    hidden_out[...] = pltpu.roll(hidden, CAP, 0).astype(jnp.bfloat16)

    def packed(value):
        blocks = total // PAIR
        moved = pltpu.roll(value, CAP, 0)
        return jnp.concatenate(
            [
                value[2 * m * PAIR : (2 * m + 1) * PAIR]
                + moved[(2 * m + 1) * PAIR : (2 * m + 2) * PAIR]
                for m in range(blocks // 2)
            ],
            axis=0,
        ).astype(jnp.bfloat16)

    partial = jnp.dot(packed(grad_gate), gate_ref[...], preferred_element_type=jnp.float32)
    partial = partial + jnp.dot(
        packed(grad_up), up_ref[...], preferred_element_type=jnp.float32
    )
    if split:
        half = partial.shape[0] // 2
        partial_refs[0][...] = partial[:half]
        partial_refs[1][...] = partial[half:].astype(jnp.bfloat16)
    else:
        partial_refs[0][...] = partial.astype(jnp.bfloat16)


def expert_main(pieces, weight_gate, weight_up, weight_down, split):
    total = sum(piece.shape[0] for piece in pieces)
    units, width = weight_gate.shape
    rows = total // 2
    small = jax.ShapeDtypeStruct((total, units), jnp.bfloat16)
    if split:
        partials = (
            jax.ShapeDtypeStruct((rows // 2, width), jnp.float32),
            jax.ShapeDtypeStruct((rows // 2, width), jnp.bfloat16),
        )
    else:
        partials = (jax.ShapeDtypeStruct((rows, width), jnp.bfloat16),)
    outs = (jax.ShapeDtypeStruct((total, width), jnp.bfloat16), small, small, small) + partials
    return pl.pallas_call(
        functools.partial(main_kernel, len(pieces), split),
        out_shape=outs,
        in_specs=[VMEM] * (len(pieces) + 3),
        out_specs=(VMEM,) * len(outs),
        compiler_params=pltpu.CompilerParams(vmem_limit_bytes=32 << 20),
        cost_estimate=pl.CostEstimate(
            flops=2 * total * units * width * 5,
            bytes_accessed=3 * units * width * 2,
            transcendentals=total * units,
        ),
        name="expert_main",
    )(*pieces, weight_gate, weight_up, weight_down)


def grad_kernel(left_ref, rows_ref, out_ref, turned_ref):
    step = pl.program_id(0)
    size = out_ref.shape[0]

    @pl.when(step == 0)
    def _():
        turned_ref[...] = left_ref[...].astype(jnp.float32).T.astype(jnp.bfloat16)

    left = turned_ref[pl.ds(pl.multiple_of(step * size, 8), size), :]
    out_ref[...] = jnp.dot(left, rows_ref[...], preferred_element_type=jnp.float32).astype(
        jnp.bfloat16
    )


def weight_grad(left, rows):
    total, units = left.shape
    width = rows.shape[1]
    steps = 3 if units % 24 == 0 else 1
    return pl.pallas_call(
        grad_kernel,
        out_shape=jax.ShapeDtypeStruct((units, width), jnp.bfloat16),
        grid=(steps,),
        in_specs=[
            pl.BlockSpec((total, units), lambda i: (0, 0)),
            pl.BlockSpec((total, width), lambda i: (0, 0)),
        ],
        out_specs=pl.BlockSpec((units // steps, width), lambda i: (i, 0)),
        scratch_shapes=[pltpu.VMEM((units, total), jnp.bfloat16)],
        compiler_params=pltpu.CompilerParams(vmem_limit_bytes=16 << 20),
        cost_estimate=pl.CostEstimate(
            flops=2 * total * units * width, bytes_accessed=units * width * 2, transcendentals=0
        ),
        name="weight_grad",
    )(left, rows)


def expand_kernel(message_ref, out_ref):
    message = message_ref[...]
    width = out_ref.shape[1]
    tokens = out_ref.shape[0]
    numbers = message[:, width : width + 1].astype(jnp.float32)
    column = lax.broadcasted_iota(jnp.int32, (CAP, tokens), 1).astype(jnp.float32)
    chooser = jnp.where(column == numbers, 1.0, 0.0).astype(jnp.bfloat16)
    out_ref[...] = contract_first(chooser, message[:, :width]).astype(jnp.bfloat16)


def expand(message, tokens, width):
    return pl.pallas_call(
        expand_kernel,
        out_shape=jax.ShapeDtypeStruct((tokens, width), jnp.bfloat16),
        in_specs=[VMEM],
        out_specs=VMEM,
        compiler_params=pltpu.CompilerParams(vmem_limit_bytes=8 << 20),
        name="expand",
    )(message)


def swap(value, bits):
    peers = lax.axis_size("expert")
    return lax.ppermute(value, "expert", [(i, i ^ bits) for i in range(peers)])


def shift_back(value):
    count = lax.axis_size("pipe")
    return lax.ppermute(value, "pipe", [(source, source - 1) for source in range(1, count)])


def body(layer_input, grad_output, expert_ids, gate_probs, w_gate, w_up, w_down):
    peers = lax.axis_size("expert")
    flight = peers // SLICES
    tokens, width = layer_input.shape[1:]
    ids = expert_ids[0].T
    probs = gate_probs[0].T
    own, slots = select_rows(ids, probs, layer_input[0], grad_output[0], flight)
    weights = (w_gate[0], w_up[0], w_down[0])
    if flight == 1:
        far, near, end = swap(own, 4), swap(own, 2), swap(own, 6)
        across = swap(jnp.concatenate([own, far, near], axis=0), 1)
        across_end = swap(end, 1)
        pieces = (own, far, near, end, across, across_end)
        rows, gate, up, hidden, keep, send = expert_main(pieces, *weights, split=True)
        beside = swap(send, 1)
        grad_gate = weight_grad(gate, rows)
        grad_up = weight_grad(up, rows)
        grad_down = weight_grad(hidden, rows)
        summed = keep + beside.astype(jnp.float32)
        rounded = summed.astype(jnp.bfloat16)
        home = [
            swap(rounded[j * CAP : (j + 1) * CAP], bits).astype(jnp.float32)
            for j, bits in ((1, 4), (2, 2), (3, 6))
        ]
        combined = summed[:CAP] + home[0] + home[1] + home[2]
        message = jnp.concatenate([combined, slots[:CAP]], axis=1).astype(jnp.bfloat16)
        shifted = expand(shift_back(message), tokens, width)
    else:
        own = own.reshape(flight, PAIR, width)
        spread = jnp.repeat(own, SLICES, axis=0)
        received = lax.all_to_all(spread, "expert", split_axis=0, concat_axis=0, tiled=True)
        received = received.reshape(peers * PAIR, width)
        rows, gate, up, hidden, partial = expert_main((received,), *weights, split=False)
        partial = partial.reshape(peers, CAP, width)
        returned = lax.all_to_all(partial, "expert", split_axis=0, concat_axis=0, tiled=True)
        grad_gate = weight_grad(gate, rows)
        grad_up = weight_grad(up, rows)
        grad_down = weight_grad(hidden, rows)
        combined = jnp.sum(
            returned.astype(jnp.float32).reshape(flight, SLICES, CAP, width), axis=1
        ).reshape(flight * CAP, width)
        labels = jnp.arange(flight, dtype=jnp.int32)
        named = jnp.any(ids[None] == labels[:, None, None], axis=1)
        ranks = jnp.cumsum(named.astype(jnp.int32), axis=1) - 1
        slot = jnp.arange(CAP, dtype=jnp.int32)
        chooser = named[:, None, :] & (ranks[:, None, :] == slot[None, :, None])
        chooser = chooser.reshape(flight * CAP, tokens).astype(jnp.float32)
        input_grad = lax.dot_general(
            chooser,
            combined,
            (((0,), (0,)), ((), ())),
            precision=lax.Precision.HIGHEST,
            preferred_element_type=jnp.float32,
        )
        shifted = shift_back(input_grad.astype(jnp.bfloat16))
    return grad_gate[None], grad_up[None], grad_down[None], shifted[None]


def solution(mesh):
    spec = P("pipe", "expert", None)
    return jax.shard_map(
        body, mesh=mesh, in_specs=(spec,) * 7, out_specs=(spec,) * 4, check_vma=False
    )
```

time: 59.5 us -> 52.6 us (0.88)
  matrix products: 14.3 us -> 0 us
  Pallas kernels: 0 us -> 12.4 us
  blocking collectives: 9.03 us -> 0 us
  waiting for transfers between devices: 4.31 us -> 10.9 us
  other arithmetic: 4.3 us -> 0.15 us
  starting transfers between devices: 17.5 us -> 19.9 us
    dot_general x11 -> x0, matrix products: 14.3 us -> none  [the longest x3 6.26 us: contract_first(): lax.dot_general(left, right, (((0,), (0,)), ((), ())), preferred_element_...]
    ppermute x1 -> x10, starting transfers between devices: 5.7 us -> 19.9 us  [the longest x9 11.7 us: swap(): return lax.ppermute(value, 'expert', [(i, i ^ bits) for i in range(peers)])]
    pallas_call x0 -> x6, Pallas kernels: none -> 12.4 us  [the longest x3 7.49 us: weight_grad(): pl.pallas_call(grad_kernel, out_shape=jax.ShapeDtypeStruct((units, width)...]
    all_to_all x2 -> x0, starting transfers between devices: 11.8 us -> none  [the longest x1 6.34 us: body(): lax.all_to_all(send_input, 'expert', split_axis=0, concat_axis=0, tiled=T...]
    ppermute x1 -> x10, waiting for transfers between devices: 0.14 us -> 10.9 us  [the longest x9 10.9 us: swap(): return lax.ppermute(value, 'expert', [(i, i ^ bits) for i in range(peers)])]
    all_to_all x1 -> x0, blocking collectives: 9.03 us -> none  [body(): lax.all_to_all(partial_value, 'expert', split_axis=0, concat_axis=0, tile...]
    unnamed x7 -> x14, local copies, waits for them, and re-layouts: 1.64 us -> 8.13 us
    all_to_all x2 -> x0, waiting for transfers between devices: 4.17 us -> none  [the longest x1 4.17 us: body(): lax.all_to_all(send_cotan, 'expert', split_axis=0, concat_axis=0, tiled=T...]
  transfers between devices with their start and end apart: 3 -> 10, of which waited for: 2 -> 5; matrix products, arithmetic and copies ran while one was open for 29% -> 0% of each run, Pallas kernels for 0% -> 14%
where the time goes in v1:
time: 52.6 us; the launch traced here: 52.2 us
  starting transfers between devices  19.9 us (38%)
  Pallas kernels  12.4 us (24%)
  waiting for transfers between devices  10.9 us (21%)
  local copies, waits for them, and re-layouts  8.16 us (16%)
  between operations  0.7 us (1%)
    ppermute x9, starting transfers between devices, swap(): return lax.ppermute(value, 'expert', [(i, i ^ bits) for i in range(peers)])  11.7 us
    ppermute x9, waiting for transfers between devices, swap(): return lax.ppermute(value, 'expert', [(i, i ^ bits) for i in range(peers)])  10.9 us
    ppermute x1, starting transfers between devices, shift_back(): lax.ppermute(value, 'pipe', [(source, source - 1) for source in range(1,...  8.2 us
    unnamed x14, local copies, waits for them, and re-layouts  8.13 us
    pallas_call x3, Pallas kernels, weight_grad(): pl.pallas_call(grad_kernel, out_shape=jax.ShapeDtypeStruct((units, width)...  7.49 us
    pallas_call x1, Pallas kernels, expert_main(): pl.pallas_call(functools.partial(main_kernel, len(pieces), split), out_sh...  3.39 us
    pallas_call x1, Pallas kernels, expand(): pl.pallas_call(expand_kernel, out_shape=jax.ShapeDtypeStruct((tokens, wid...  1.17 us
  transfers between devices with their start and end apart: 10, of which 5 were waited for; matrix products, arithmetic and copies ran while one was open for 0% of the time, Pallas kernels for 14%

profile of v1, /device:TPU:1, one launch (start us, length us, event | category | flops | bytes accessed | tf_op | source)
XLA Modules:
  0.0 52.2 jit_solution(3000190911992307809)
XLA Ops:
  0.6 0.0 copy-start.3
  0.6 1.0 %copy-done.3 = bf16[1,64,2880]{2,1,0:T(8,128)(2,1)S(1)} copy-done((bf16[1,64,2880]{2,1,0:T(8,128)(2,1)S(1)}, bf16[1,64,2880]{2,1,0:T(8,128)(2,1)}, u32[]{:S(2)}) %copy-start.3) | copy-done | bytes 368664
  1.6 0.0 copy-start.4
  1.6 1.0 %copy-done.4 = bf16[1,64,2880]{2,1,0:T(8,128)(2,1)S(1)} copy-done((bf16[1,64,2880]{2,1,0:T(8,128)(2,1)S(1)}, bf16[1,64,2880]{2,1,0:T(8,128)(2,1)}, u32[]{:S(2)}) %copy-start.4) | copy-done | bytes 368664
  2.6 0.0 copy-start.5
  2.6 0.7 %copy-done.5 = s32[1,64,4]{1,2,0:T(4,128)S(1)} copy-done((s32[1,64,4]{1,2,0:T(4,128)S(1)}, s32[1,64,4]{1,2,0:T(4,128)}, u32[]{:S(2)}) %copy-start.5) | copy-done | bytes 1048
  3.3 0.0 copy-start.6
  3.3 0.7 %copy-done.6 = f32[1,64,4]{1,2,0:T(4,128)S(1)} copy-done((f32[1,64,4]{1,2,0:T(4,128)S(1)}, f32[1,64,4]{1,2,0:T(4,128)}, u32[]{:S(2)}) %copy-start.6) | copy-done | bytes 1048
  4.0 0.3 select.1
  4.3 3.2 %collective-permute-start = (bf16[8,2880]{1,0:T(8,128)(2,1)S(1)}, bf16[8,2880]{1,0:T(8,128)(2,1)S(1)}, u32[]{:S(2)}, u32[]{:S(2)}) collective-permute-start(bf16[8,2880]{1,0:T(8,128)(2,1)S(1)} %get-tuple-element.12.refs_0_), channel_id=1, source_target_pairs={{0,4},{1,5},{2,6},{3,7},{4,0},{5,1},{6,2},{7,3},{8,12},{9,13},{10,... | collective-permute-start | bytes 138248 | tf_op jit(solution)/shard_map/ppermute | solution.py:210
  7.5 1.3 %collective-permute-start.1 = (bf16[8,2880]{1,0:T(8,128)(2,1)S(1)}, bf16[8,2880]{1,0:T(8,128)(2,1)S(1)}, u32[]{:S(2)}, u32[]{:S(2)}) collective-permute-start(bf16[8,2880]{1,0:T(8,128)(2,1)S(1)} %get-tuple-element.12.refs_0_), channel_id=1, source_target_pairs={{0,2},{1,3},{2,0},{3,1},{4,6},{5,7},{6,4},{7,5},{8,10},{9,11},{10,... | collective-permute-start | bytes 138248 | tf_op jit(solution)/shard_map/ppermute | solution.py:210
  8.8 0.2 collective-permute-done.refs_1_
  9.0 1.7 %collective-permute-done.1.refs_2_ = bf16[8,2880]{1,0:T(8,128)(2,1)S(1)} collective-permute-done((bf16[8,2880]{1,0:T(8,128)(2,1)S(1)}, bf16[8,2880]{1,0:T(8,128)(2,1)S(1)}, u32[]{:S(2)}, u32[]{:S(2)}) %collective-permute-start.1) | collective-permute-done | bytes 46112 | tf_op jit(solution)/shard_map/ppermute | solution.py:210
  10.6 1.6 %collective-permute-start.3 = (bf16[24,2880]{1,0:T(8,128)(2,1)S(1)}, bf16[24,2880]{1,0:T(8,128)(2,1)S(1)}, u32[]{:S(2)}, u32[]{:S(2)}) collective-permute-start(bf16[24,2880]{1,0:T(8,128)(2,1)S(1)} %pad_maximum_fusion), channel_id=1, source_target_pairs={{0,1},{1,0},{2,3},{3,2},{4,5},{5,4},{6,7},{7,6},{8,9},{9,8},{10,11... | collective-permute-start | bytes 414728 | tf_op jit(solution)/shard_map/ppermute | solution.py:210
  12.2 1.9 %collective-permute-start.2 = (bf16[8,2880]{1,0:T(8,128)(2,1)S(1)}, bf16[8,2880]{1,0:T(8,128)(2,1)S(1)}, u32[]{:S(2)}, u32[]{:S(2)}) collective-permute-start(bf16[8,2880]{1,0:T(8,128)(2,1)S(1)} %get-tuple-element.12.refs_0_), channel_id=1, source_target_pairs={{0,6},{1,7},{2,4},{3,5},{4,2},{5,3},{6,0},{7,1},{8,14},{9,15},{10,... | collective-permute-start | bytes 138248 | tf_op jit(solution)/shard_map/ppermute | solution.py:210
  14.1 2.9 %collective-permute-done.2.refs_3_ = bf16[8,2880]{1,0:T(8,128)(2,1)S(1)} collective-permute-done((bf16[8,2880]{1,0:T(8,128)(2,1)S(1)}, bf16[8,2880]{1,0:T(8,128)(2,1)S(1)}, u32[]{:S(2)}, u32[]{:S(2)}) %collective-permute-start.2) | collective-permute-done | bytes 46112 | tf_op jit(solution)/shard_map/ppermute | solution.py:210
  16.9 0.1 collective-permute-start.4
  17.0 2.8 %collective-permute-done.4.refs_5_ = bf16[8,2880]{1,0:T(8,128)(2,1)S(1)} collective-permute-done((bf16[8,2880]{1,0:T(8,128)(2,1)S(1)}, bf16[8,2880]{1,0:T(8,128)(2,1)S(1)}, u32[]{:S(2)}, u32[]{:S(2)}) %collective-permute-start.4) | collective-permute-done | bytes 46112 | tf_op jit(solution)/shard_map/ppermute | solution.py:210
  19.8 0.0 collective-permute-done.3.refs_4_
  19.8 0.0 copy-start
  19.8 1.6 %copy-done = bf16[1,360,2880]{2,1,0:T(8,128)(2,1)S(1)} copy-done((bf16[1,360,2880]{2,1,0:T(8,128)(2,1)S(1)}, bf16[1,360,2880]{2,1,0:T(8,128)(2,1)}, u32[]{:S(2)}) %copy-start) | copy-done | bytes 2073624
  21.4 0.0 copy-start.1
  21.4 1.6 %copy-done.1 = bf16[1,360,2880]{2,1,0:T(8,128)(2,1)S(1)} copy-done((bf16[1,360,2880]{2,1,0:T(8,128)(2,1)S(1)}, bf16[1,360,2880]{2,1,0:T(8,128)(2,1)}, u32[]{:S(2)}) %copy-start.1) | copy-done | bytes 2073624
  23.0 0.0 copy-start.2
  23.0 1.6 %copy-done.2 = bf16[1,360,2880]{2,1,0:T(8,128)(2,1)S(1)} copy-done((bf16[1,360,2880]{2,1,0:T(8,128)(2,1)S(1)}, bf16[1,360,2880]{2,1,0:T(8,128)(2,1)}, u32[]{:S(2)}) %copy-start.2) | copy-done | bytes 2073624
  24.6 3.4 %expert_main.1 = (bf16[64,2880]{1,0:T(8,128)(2,1)S(1)}, bf16[64,360]{1,0:T(8,128)(2,1)S(1)}, bf16[64,360]{1,0:T(8,128)(2,1)S(1)}, bf16[64,360]{1,0:T(8,128)(2,1)...) custom-call(bf16[8,2880]{1,0:T(8,128)(2,1)S(1)} %get-tuple-element.12.refs_0_, ...), custom_call_target="tpu_custom_call" | custom-call | flops 663552000 | bytes 6220800 | tf_op jit(solution)/shard_map/expert_main/pallas_call | solution.py:136
  28.0 0.1 collective-permute-start.5
  28.2 3.4 %collective-permute-done.5 = bf16[16,2880]{1,0:T(8,128)(2,1)S(1)} collective-permute-done((bf16[16,2880]{1,0:T(8,128)(2,1)S(1)}, bf16[16,2880]{1,0:T(8,128)(2,1)S(1)}, u32[]{:S(2)}, u32[]{:S(2)}) %collective-permute-start.5) | collective-permute-done | bytes 92192 | tf_op jit(solution)/shard_map/ppermute | solution.py:210
  31.6 1.9 %collective-permute-start.8 = (bf16[4,2880]{1,0:T(4,128)(2,1)S(1)}, bf16[4,2880]{1,0:T(4,128)(2,1)S(1)}, u32[]{:S(2)}, u32[]{:S(2)}) collective-permute-start(bf16[4,2880]{1,0:T(4,128)(2,1)S(1)} %get-tuple-element.23), channel_id=1, source_target_pairs={{0,6},{1,7},{2,4},{3,5},{4,2},{5,3},{6,0},{7,1},{8,14},{9,15},{10,... | collective-permute-start | bytes 69128 | tf_op jit(solution)/shard_map/ppermute | solution.py:210
  33.5 0.0 collective-permute-start.7
  33.5 1.7 %collective-permute-start.6 = (bf16[4,2880]{1,0:T(4,128)(2,1)S(1)}, bf16[4,2880]{1,0:T(4,128)(2,1)S(1)}, u32[]{:S(2)}, u32[]{:S(2)}) collective-permute-start(bf16[4,2880]{1,0:T(4,128)(2,1)S(1)} %get-tuple-element.22), channel_id=1, source_target_pairs={{0,4},{1,5},{2,6},{3,7},{4,0},{5,1},{6,2},{7,3},{8,12},{9,13},{10,... | collective-permute-start | bytes 69128 | tf_op jit(solution)/shard_map/ppermute | solution.py:210
  35.2 2.5 %weight_grad.3 = bf16[360,2880]{1,0:T(8,128)(2,1)} custom-call(bf16[64,360]{1,0:T(8,128)(2,1)S(1)} %get-tuple-element.13.left_ref, bf16[64,2880]{1,0:T(8,128)(2,1)S(1)} %get-tuple-element.14.rows_ref), custom_call_target="tpu_custom_call" | custom-call | flops 132710400 | bytes 2073600 | tf_op jit(solution)/shard_map/weight_grad/pallas_call | solution.py:169
  37.7 0.0 collective-permute-done.8
  37.7 0.0 collective-permute-done.7
  37.7 0.0 collective-permute-done.6
  37.8 0.1 pad_maximum_fusion.1
  37.8 8.2 %collective-permute-start.9 = (bf16[4,3008]{1,0:T(4,128)(2,1)S(1)}, bf16[4,3008]{1,0:T(4,128)(2,1)S(1)}, u32[]{:S(2)}, u32[]{:S(2)}) collective-permute-start(bf16[4,3008]{1,0:T(4,128)(2,1)S(1)} %pad_maximum_fusion.1), channel_id=1, source_target_pairs={{8,0},{16,8},{24,16},{9,1},{17,9},{25,17},{10,2},{18,10},{26,18},{... | collective-permute-start | bytes 72200 | tf_op jit(solution)/shard_map/ppermute | solution.py:215
  46.0 2.5 %weight_grad.4 = bf16[360,2880]{1,0:T(8,128)(2,1)} custom-call(bf16[64,360]{1,0:T(8,128)(2,1)S(1)} %get-tuple-element.15.left_ref, bf16[64,2880]{1,0:T(8,128)(2,1)S(1)} %get-tuple-element.14.rows_ref), custom_call_target="tpu_custom_call" | custom-call | flops 132710400 | bytes 2073600 | tf_op jit(solution)/shard_map/weight_grad/pallas_call | solution.py:169
  48.6 2.5 %weight_grad.5 = bf16[360,2880]{1,0:T(8,128)(2,1)} custom-call(bf16[64,360]{1,0:T(8,128)(2,1)S(1)} %get-tuple-element.16.left_ref, bf16[64,2880]{1,0:T(8,128)(2,1)S(1)} %get-tuple-element.14.rows_ref), custom_call_target="tpu_custom_call" | custom-call | flops 132710400 | bytes 2073600 | tf_op jit(solution)/shard_map/weight_grad/pallas_call | solution.py:169
  51.0 0.0 collective-permute-done.9.message_ref
  51.1 1.2 %expand.1 = bf16[64,2880]{1,0:T(8,128)(2,1)} custom-call(bf16[4,3008]{1,0:T(4,128)(2,1)S(1)} %collective-permute-done.9.message_ref), custom_call_target="tpu_custom_call" | custom-call | tf_op jit(solution)/shard_map/expand/pallas_call | solution.py:198
  (6 shorter events, 0.1 us)
Async XLA Ops:
  0.6 1.0 %copy-start.3 = (bf16[1,64,2880]{2,1,0:T(8,128)(2,1)S(1)}, bf16[1,64,2880]{2,1,0:T(8,128)(2,1)}, u32[]{:S(2)}) copy-start(bf16[1,64,2880]{2,1,0:T(8,128)(2,1)} %param.7) | copy-start | bytes 1105924
  1.6 1.0 %copy-start.4 = (bf16[1,64,2880]{2,1,0:T(8,128)(2,1)S(1)}, bf16[1,64,2880]{2,1,0:T(8,128)(2,1)}, u32[]{:S(2)}) copy-start(bf16[1,64,2880]{2,1,0:T(8,128)(2,1)} %param.8) | copy-start | bytes 1105924
  2.6 0.7 %copy-start.5 = (s32[1,64,4]{1,2,0:T(4,128)S(1)}, s32[1,64,4]{1,2,0:T(4,128)}, u32[]{:S(2)}) copy-start(s32[1,64,4]{1,2,0:T(4,128)} %param.9) | copy-start | bytes 3076
  3.3 0.7 %copy-start.6 = (f32[1,64,4]{1,2,0:T(4,128)S(1)}, f32[1,64,4]{1,2,0:T(4,128)}, u32[]{:S(2)}) copy-start(f32[1,64,4]{1,2,0:T(4,128)} %param.10) | copy-start | bytes 3076
  4.3 4.7 %collective-permute-start = (bf16[8,2880]{1,0:T(8,128)(2,1)S(1)}, bf16[8,2880]{1,0:T(8,128)(2,1)S(1)}, u32[]{:S(2)}, u32[]{:S(2)}) collective-permute-start(bf16[8,2880]{1,0:T(8,128)(2,1)S(1)} %get-tuple-element.12.refs_0_), channel_id=1, source_target_pairs={{0,4},{1,5},{2,6},{3,7},{4,0},{5,1},{6,2},{7,3},{8,12},{9,13},{10,... | collective-permute-start | bytes 138248 | tf_op jit(solution)/shard_map/ppermute | solution.py:210
  7.5 3.1 %collective-permute-start.1 = (bf16[8,2880]{1,0:T(8,128)(2,1)S(1)}, bf16[8,2880]{1,0:T(8,128)(2,1)S(1)}, u32[]{:S(2)}, u32[]{:S(2)}) collective-permute-start(bf16[8,2880]{1,0:T(8,128)(2,1)S(1)} %get-tuple-element.12.refs_0_), channel_id=1, source_target_pairs={{0,2},{1,3},{2,0},{3,1},{4,6},{5,7},{6,4},{7,5},{8,10},{9,11},{10,... | collective-permute-start | bytes 138248 | tf_op jit(solution)/shard_map/ppermute | solution.py:210
  10.6 9.2 %collective-permute-start.3 = (bf16[24,2880]{1,0:T(8,128)(2,1)S(1)}, bf16[24,2880]{1,0:T(8,128)(2,1)S(1)}, u32[]{:S(2)}, u32[]{:S(2)}) collective-permute-start(bf16[24,2880]{1,0:T(8,128)(2,1)S(1)} %pad_maximum_fusion), channel_id=1, source_target_pairs={{0,1},{1,0},{2,3},{3,2},{4,5},{5,4},{6,7},{7,6},{8,9},{9,8},{10,11... | collective-permute-start | bytes 414728 | tf_op jit(solution)/shard_map/ppermute | solution.py:210
  12.2 4.7 %collective-permute-start.2 = (bf16[8,2880]{1,0:T(8,128)(2,1)S(1)}, bf16[8,2880]{1,0:T(8,128)(2,1)S(1)}, u32[]{:S(2)}, u32[]{:S(2)}) collective-permute-start(bf16[8,2880]{1,0:T(8,128)(2,1)S(1)} %get-tuple-element.12.refs_0_), channel_id=1, source_target_pairs={{0,6},{1,7},{2,4},{3,5},{4,2},{5,3},{6,0},{7,1},{8,14},{9,15},{10,... | collective-permute-start | bytes 138248 | tf_op jit(solution)/shard_map/ppermute | solution.py:210
  16.9 2.9 %collective-permute-start.4 = (bf16[8,2880]{1,0:T(8,128)(2,1)S(1)}, bf16[8,2880]{1,0:T(8,128)(2,1)S(1)}, u32[]{:S(2)}, u32[]{:S(2)}) collective-permute-start(bf16[8,2880]{1,0:T(8,128)(2,1)S(1)} %collective-permute-done.2.refs_3_), channel_id=1, source_target_pairs={{0,1},{1,0},{2,3},{3,2},{4,5},{5,4},{6,7},{7,6},{8,9},{9,8},{10,11... | collective-permute-start | bytes 138248 | tf_op jit(solution)/shard_map/ppermute | solution.py:210
  19.8 1.6 %copy-start = (bf16[1,360,2880]{2,1,0:T(8,128)(2,1)S(1)}, bf16[1,360,2880]{2,1,0:T(8,128)(2,1)}, u32[]{:S(2)}) copy-start(bf16[1,360,2880]{2,1,0:T(8,128)(2,1)} %param.11) | copy-start | bytes 6220804
  21.4 1.6 %copy-start.1 = (bf16[1,360,2880]{2,1,0:T(8,128)(2,1)S(1)}, bf16[1,360,2880]{2,1,0:T(8,128)(2,1)}, u32[]{:S(2)}) copy-start(bf16[1,360,2880]{2,1,0:T(8,128)(2,1)} %param.12) | copy-start | bytes 6220804
  23.0 1.6 %copy-start.2 = (bf16[1,360,2880]{2,1,0:T(8,128)(2,1)S(1)}, bf16[1,360,2880]{2,1,0:T(8,128)(2,1)}, u32[]{:S(2)}) copy-start(bf16[1,360,2880]{2,1,0:T(8,128)(2,1)} %param.13) | copy-start | bytes 6220804
  28.0 3.5 %collective-permute-start.5 = (bf16[16,2880]{1,0:T(8,128)(2,1)S(1)}, bf16[16,2880]{1,0:T(8,128)(2,1)S(1)}, u32[]{:S(2)}, u32[]{:S(2)}) collective-permute-start(bf16[16,2880]{1,0:T(8,128)(2,1)S(1)} %get-tuple-element.18), channel_id=1, source_target_pairs={{0,1},{1,0},{2,3},{3,2},{4,5},{5,4},{6,7},{7,6},{8,9},{9,8},{10,11... | collective-permute-start | bytes 276488 | tf_op jit(solution)/shard_map/ppermute | solution.py:210
  31.6 6.1 %collective-permute-start.8 = (bf16[4,2880]{1,0:T(4,128)(2,1)S(1)}, bf16[4,2880]{1,0:T(4,128)(2,1)S(1)}, u32[]{:S(2)}, u32[]{:S(2)}) collective-permute-start(bf16[4,2880]{1,0:T(4,128)(2,1)S(1)} %get-tuple-element.23), channel_id=1, source_target_pairs={{0,6},{1,7},{2,4},{3,5},{4,2},{5,3},{6,0},{7,1},{8,14},{9,15},{10,... | collective-permute-start | bytes 69128 | tf_op jit(solution)/shard_map/ppermute | solution.py:210
  33.5 4.2 %collective-permute-start.7 = (bf16[4,2880]{1,0:T(4,128)(2,1)S(1)}, bf16[4,2880]{1,0:T(4,128)(2,1)S(1)}, u32[]{:S(2)}, u32[]{:S(2)}) collective-permute-start(bf16[4,2880]{1,0:T(4,128)(2,1)S(1)} %get-tuple-element.24), channel_id=1, source_target_pairs={{0,2},{1,3},{2,0},{3,1},{4,6},{5,7},{6,4},{7,5},{8,10},{9,11},{10,... | collective-permute-start | bytes 69128 | tf_op jit(solution)/shard_map/ppermute | solution.py:210
  33.5 4.2 %collective-permute-start.6 = (bf16[4,2880]{1,0:T(4,128)(2,1)S(1)}, bf16[4,2880]{1,0:T(4,128)(2,1)S(1)}, u32[]{:S(2)}, u32[]{:S(2)}) collective-permute-start(bf16[4,2880]{1,0:T(4,128)(2,1)S(1)} %get-tuple-element.22), channel_id=1, source_target_pairs={{0,4},{1,5},{2,6},{3,7},{4,0},{5,1},{6,2},{7,3},{8,12},{9,13},{10,... | collective-permute-start | bytes 69128 | tf_op jit(solution)/shard_map/ppermute | solution.py:210
  37.8 13.2 %collective-permute-start.9 = (bf16[4,3008]{1,0:T(4,128)(2,1)S(1)}, bf16[4,3008]{1,0:T(4,128)(2,1)S(1)}, u32[]{:S(2)}, u32[]{:S(2)}) collective-permute-start(bf16[4,3008]{1,0:T(4,128)(2,1)S(1)} %pad_maximum_fusion.1), channel_id=1, source_target_pairs={{8,0},{16,8},{24,16},{9,1},{17,9},{25,17},{10,2},{18,10},{26,18},{... | collective-permute-start | bytes 72200 | tf_op jit(solution)/shard_map/ppermute | solution.py:215

commit v2 on v1

v2 whole, which is shorter than its diff:
```python
import functools

import jax
import jax.numpy as jnp
from jax import lax
from jax.experimental import pallas as pl
from jax.experimental.pallas import tpu as pltpu
from jax.sharding import PartitionSpec as P


SLICES = 8
CAP = 4
PAIR = 2 * CAP
LANES = 128
CHUNK = 1024
OUT = (6, 4, 2)
HOME = (4, 6, 2)

VMEM = pl.BlockSpec(memory_space=pltpu.VMEM)
HBM = pl.BlockSpec(memory_space=pl.ANY)


def contract_last(left, right):
    return lax.dot_general(
        left, right, (((1,), (1,)), ((), ())), preferred_element_type=jnp.float32
    )


def contract_first(left, right):
    return lax.dot_general(
        left, right, (((0,), (0,)), ((), ())), preferred_element_type=jnp.float32
    )


def select_kernel(flight, *refs):
    routes_ref, sources = refs[0], refs[1:3]
    (rows_ref, slots_ref), held, sems = refs[3:5], refs[5:7], refs[7]
    copies = [
        pltpu.make_async_copy(source, target, sems.at[i])
        for i, (source, target) in enumerate(zip(sources, held))
    ]
    for copy in copies:
        copy.start()
    ids = routes_ref[0]
    probs = routes_ref[1]
    tokens = ids.shape[1]
    before = lax.broadcasted_iota(jnp.int32, (tokens, tokens), 0) < lax.broadcasted_iota(
        jnp.int32, (tokens, tokens), 1
    )
    before = before.astype(jnp.float32).astype(jnp.bfloat16)
    row = lax.broadcasted_iota(jnp.int32, (PAIR, tokens), 0)
    token = lax.broadcasted_iota(jnp.int32, (PAIR, tokens), 1).astype(jnp.float32)
    slot = lax.rem(row, CAP)
    choosers = []
    for expert in range(flight):
        matched = ids == float(expert)
        hit = jnp.sum(jnp.where(matched, 1.0, 0.0), axis=0, keepdims=True)
        prob = jnp.sum(jnp.where(matched, probs, 0.0), axis=0, keepdims=True)
        hits = jnp.broadcast_to(hit, (PAIR, tokens))
        ranks = jnp.dot(hits.astype(jnp.bfloat16), before, preferred_element_type=jnp.float32)
        chosen = jnp.where((hits > 0.5) & (ranks.astype(jnp.int32) == slot), 1.0, 0.0)
        scale = jnp.sum(chosen * prob, axis=1, keepdims=True)
        number = jnp.sum(chosen * token, axis=1, keepdims=True)
        slots_ref[pl.ds(expert * PAIR, PAIR), :] = jnp.broadcast_to(number, (PAIR, LANES))
        choosers.append((chosen.astype(jnp.bfloat16), scale))
    for copy in copies:
        copy.wait()
    for expert, (chooser, scale) in enumerate(choosers):
        taken = jnp.dot(chooser, held[0][...], preferred_element_type=jnp.float32)
        cotan = jnp.dot(chooser, held[1][...], preferred_element_type=jnp.float32) * scale
        wide = lax.broadcasted_iota(jnp.int32, taken.shape, 0) < CAP
        rows_ref[pl.ds(expert * PAIR, PAIR), :] = jnp.where(wide, taken, cotan).astype(
            jnp.bfloat16
        )


def select_rows(ids, probs, inputs, cotan, flight):
    width = inputs.shape[1]
    plane = lax.broadcasted_iota(jnp.int32, (2, *ids.shape), 0)
    routes = jnp.where(plane == 0, ids.astype(jnp.float32)[None], probs[None])
    return pl.pallas_call(
        functools.partial(select_kernel, flight),
        out_shape=(
            jax.ShapeDtypeStruct((flight * PAIR, width), jnp.bfloat16),
            jax.ShapeDtypeStruct((flight * PAIR, LANES), jnp.float32),
        ),
        in_specs=[VMEM, HBM, HBM],
        out_specs=(VMEM, VMEM),
        scratch_shapes=[pltpu.VMEM(value.shape, value.dtype) for value in (inputs, cotan)]
        + [pltpu.SemaphoreType.DMA((2,))],
        compiler_params=pltpu.CompilerParams(vmem_limit_bytes=55000 << 10),
        name="select",
    )(routes, inputs, cotan)


def fetch_kernel(after_ref, *refs):
    del after_ref
    count = len(refs) // 2
    copies = [
        pltpu.make_async_copy(refs[i], refs[count + i], refs[-1].at[i]) for i in range(count)
    ]
    for copy in copies:
        copy.start()
    for copy in copies:
        copy.wait()


def fetch(after, *weights):
    held = sum(w.size * w.dtype.itemsize for w in weights)
    return pl.pallas_call(
        fetch_kernel,
        out_shape=tuple(jax.ShapeDtypeStruct(w.shape, w.dtype) for w in weights),
        in_specs=[HBM] * (len(weights) + 1),
        out_specs=(VMEM,) * len(weights),
        scratch_shapes=[pltpu.SemaphoreType.DMA((len(weights),))],
        compiler_params=pltpu.CompilerParams(vmem_limit_bytes=47600 << 10),
        cost_estimate=pl.CostEstimate(
            flops=0,
            bytes_accessed=sum(2 * w.size * w.dtype.itemsize for w in weights),
            transcendentals=0,
        ),
        name="fetch",
    )(after, *weights)


def main_kernel(pieces, split, *refs):
    row_refs, refs = refs[:pieces], refs[pieces:]
    slots_ref, gate_ref, up_ref, down_ref = refs[:4]
    all_ref, gate_out, up_out, hidden_out = refs[4:8]
    partial_refs = refs[8:]
    start = 0
    for ref in row_refs:
        all_ref[pl.ds(start, ref.shape[0]), :] = ref[...]
        start += ref.shape[0]
    rows = all_ref[...]
    total = rows.shape[0]
    pre_gate = contract_last(rows, gate_ref[...])
    pre_up = contract_last(rows, up_ref[...])
    hidden_grad = pltpu.roll(contract_last(rows, down_ref[...]), total - CAP, 0)
    sigma = jax.nn.sigmoid(pre_gate)
    silu_val = pre_gate * sigma
    silu_grad = sigma * (1.0 + pre_gate * (1.0 - sigma))
    first = lax.rem(lax.broadcasted_iota(jnp.int32, pre_gate.shape, 0), PAIR) < CAP
    hidden = jnp.where(first, silu_val * pre_up, 0.0)
    grad_gate = jnp.where(first, hidden_grad * pre_up * silu_grad, 0.0)
    grad_up = jnp.where(first, hidden_grad * silu_val, 0.0)
    gate_out[...] = grad_gate.astype(jnp.bfloat16)
    up_out[...] = grad_up.astype(jnp.bfloat16)
    hidden_out[...] = pltpu.roll(hidden, CAP, 0).astype(jnp.bfloat16)

    def packed(value):
        blocks = total // PAIR
        moved = pltpu.roll(value, CAP, 0)
        return jnp.concatenate(
            [
                value[2 * m * PAIR : (2 * m + 1) * PAIR]
                + moved[(2 * m + 1) * PAIR : (2 * m + 2) * PAIR]
                for m in range(blocks // 2)
            ],
            axis=0,
        ).astype(jnp.bfloat16)

    partial = jnp.dot(packed(grad_gate), gate_ref[...], preferred_element_type=jnp.float32)
    partial = partial + jnp.dot(
        packed(grad_up), up_ref[...], preferred_element_type=jnp.float32
    )
    if split:
        half, width = partial.shape[0] // 2, partial.shape[1]
        keep_ref, send_ref = partial_refs
        send_ref[...] = partial[half:].astype(jnp.bfloat16)
        keep_ref[:, :width] = partial[:half].astype(jnp.bfloat16)
        keep_ref[:PAIR, width:] = slots_ref[...].astype(jnp.bfloat16)
        keep_ref[PAIR:, width:] = jnp.zeros((half - PAIR, LANES), jnp.bfloat16)
    else:
        partial_refs[0][...] = partial.astype(jnp.bfloat16)


def expert_main(pieces, slots, weight_gate, weight_up, weight_down, split):
    total = sum(piece.shape[0] for piece in pieces)
    units, width = weight_gate.shape
    rows = total // 2
    small = jax.ShapeDtypeStruct((total, units), jnp.bfloat16)
    if split:
        partials = (
            jax.ShapeDtypeStruct((rows // 2, width + LANES), jnp.bfloat16),
            jax.ShapeDtypeStruct((rows // 2, width), jnp.bfloat16),
        )
    else:
        partials = (jax.ShapeDtypeStruct((rows, width), jnp.bfloat16),)
    outs = (jax.ShapeDtypeStruct((total, width), jnp.bfloat16), small, small, small) + partials
    return pl.pallas_call(
        functools.partial(main_kernel, len(pieces), split),
        out_shape=outs,
        in_specs=[VMEM] * (len(pieces) + 4),
        out_specs=(VMEM,) * len(outs),
        compiler_params=pltpu.CompilerParams(vmem_limit_bytes=32 << 20),
        cost_estimate=pl.CostEstimate(
            flops=2 * total * units * width * 5,
            bytes_accessed=3 * units * width * 2,
            transcendentals=total * units,
        ),
        name="expert_main",
    )(*pieces, slots, weight_gate, weight_up, weight_down)


def grad_kernel(count, *refs):
    lefts, rows_ref, outs = refs[:count], refs[count], refs[count + 1 : 2 * count + 1]
    held_ref, sems = refs[2 * count + 1 :]
    width = rows_ref.shape[1]
    copies = []
    for j in range(count):
        left = lefts[j][...]
        for c, start in enumerate(range(0, width, CHUNK)):
            part = pl.ds(start, min(CHUNK, width - start))
            held_ref[j, :, part] = contract_first(left, rows_ref[:, part]).astype(jnp.bfloat16)
            copy = pltpu.make_async_copy(
                held_ref.at[j, :, part], outs[j].at[:, part], sems.at[j, c]
            )
            copy.start()
            copies.append(copy)
    for copy in copies:
        copy.wait()


def weight_grads(rows, *lefts):
    total, width = rows.shape
    units = lefts[0].shape[1]
    count = len(lefts)
    return pl.pallas_call(
        functools.partial(grad_kernel, count),
        out_shape=(jax.ShapeDtypeStruct((units, width), jnp.bfloat16),) * count,
        in_specs=[VMEM] * (count + 1),
        out_specs=(HBM,) * count,
        scratch_shapes=[
            pltpu.VMEM((count, units, width), jnp.bfloat16),
            pltpu.SemaphoreType.DMA((count, pl.cdiv(width, CHUNK))),
        ],
        compiler_params=pltpu.CompilerParams(vmem_limit_bytes=24 << 20),
        cost_estimate=pl.CostEstimate(
            flops=2 * total * units * width * count,
            bytes_accessed=units * width * 4 * count,
            transcendentals=0,
        ),
        name="weight_grads",
    )(*lefts, rows)


def expand_kernel(kept_ref, *refs):
    homes, out_ref = refs[:-1], refs[-1]
    tokens, width = out_ref.shape
    combined = kept_ref[:, :width]
    for home in homes:
        combined = combined + home[...].astype(jnp.float32)
    numbers = kept_ref[:, width : width + 1]
    column = lax.broadcasted_iota(jnp.int32, (CAP, tokens), 1).astype(jnp.float32)
    chooser = jnp.where(column == numbers, 1.0, 0.0).astype(jnp.bfloat16)
    out_ref[...] = contract_first(chooser, combined.astype(jnp.bfloat16)).astype(jnp.bfloat16)


def expand(kept, homes, tokens, width):
    return pl.pallas_call(
        expand_kernel,
        out_shape=jax.ShapeDtypeStruct((tokens, width), jnp.bfloat16),
        in_specs=[VMEM] * (len(homes) + 1),
        out_specs=VMEM,
        compiler_params=pltpu.CompilerParams(vmem_limit_bytes=8 << 20),
        name="expand",
    )(kept, *homes)


def swap(value, bits):
    peers = lax.axis_size("expert")
    return lax.ppermute(value, "expert", [(i, i ^ bits) for i in range(peers)])


def shift_back(value, bits):
    count, peers = lax.axis_size("pipe"), lax.axis_size("expert")
    pairs = [
        (section * peers + i, (section - 1) * peers + (i ^ bits))
        for section in range(1, count)
        for i in range(peers)
    ]
    return lax.ppermute(value, ("pipe", "expert"), pairs)


def one_expert(own, slots, weights, tokens, width):
    weights = fetch(own, *weights)
    first, second, third = (swap(own, bits) for bits in OUT)
    across = [swap(jnp.concatenate([own, first, second], axis=0), 1)]
    across.append(swap(third, 1))
    pieces = (own, first, second, third, *across)
    rows, gate, up, hidden, keep, send = expert_main(pieces, slots, *weights, split=True)
    beside, kept = shift_back(send, 1), shift_back(keep, 0)
    grads = weight_grads(rows, gate, up, hidden)
    kept = kept.astype(jnp.float32)
    summed = kept[:, :width] + beside.astype(jnp.float32)
    rounded = summed.astype(jnp.bfloat16)
    homes = [
        swap(rounded[(OUT.index(bits) + 1) * CAP : (OUT.index(bits) + 2) * CAP], bits)
        for bits in HOME
    ]
    kept = jnp.concatenate([summed[:CAP], kept[:CAP, width:]], axis=1)
    return grads, expand(kept, homes, tokens, width)


def many_experts(own, slots, weights, ids, peers, flight, tokens, width):
    spread = jnp.repeat(own.reshape(flight, PAIR, width), SLICES, axis=0)
    received = lax.all_to_all(spread, "expert", split_axis=0, concat_axis=0, tiled=True)
    received = received.reshape(peers * PAIR, width)
    rows, gate, up, hidden, partial = expert_main((received,), slots, *weights, split=False)
    partial = partial.reshape(peers, CAP, width)
    returned = lax.all_to_all(partial, "expert", split_axis=0, concat_axis=0, tiled=True)
    grads = weight_grads(rows, gate, up, hidden)
    combined = jnp.sum(
        returned.astype(jnp.float32).reshape(flight, SLICES, CAP, width), axis=1
    ).reshape(flight * CAP, width)
    labels = jnp.arange(flight, dtype=jnp.int32)
    named = jnp.any(ids[None] == labels[:, None, None], axis=1)
    ranks = jnp.cumsum(named.astype(jnp.int32), axis=1) - 1
    slot = jnp.arange(CAP, dtype=jnp.int32)
    chooser = named[:, None, :] & (ranks[:, None, :] == slot[None, :, None])
    chooser = chooser.reshape(flight * CAP, tokens).astype(jnp.float32)
    input_grad = lax.dot_general(
        chooser,
        combined,
        (((0,), (0,)), ((), ())),
        precision=lax.Precision.HIGHEST,
        preferred_element_type=jnp.float32,
    )
    return grads, shift_back(input_grad.astype(jnp.bfloat16), 0)


def body(layer_input, grad_output, expert_ids, gate_probs, w_gate, w_up, w_down):
    peers = lax.axis_size("expert")
    flight = peers // SLICES
    tokens, width = layer_input.shape[1:]
    ids = expert_ids[0].T
    weights = (w_gate[0], w_up[0], w_down[0])
    own, slots = select_rows(ids, gate_probs[0].T, layer_input[0], grad_output[0], flight)
    if flight == 1:
        grads, shifted = one_expert(own, slots, weights, tokens, width)
    else:
        grads, shifted = many_experts(
            own, slots, weights, ids, peers, flight, tokens, width
        )
    return tuple(grad[None] for grad in grads) + (shifted[None],)


def solution(mesh):
    spec = P("pipe", "expert", None)
    return jax.shard_map(
        body, mesh=mesh, in_specs=(spec,) * 7, out_specs=(spec,) * 4, check_vma=False
    )
```

time: 52.6 us -> 43.1 us (0.82)
  local copies, waits for them, and re-layouts: 8.16 us -> 0.11 us
  starting transfers between devices: 19.9 us -> 16.9 us
  other arithmetic: 0.15 us -> 1.58 us
  waiting for transfers between devices: 10.9 us -> 11.6 us
    unnamed x14 -> x0, local copies, waits for them, and re-layouts: 8.13 us -> none
    ppermute x9 -> x8, starting transfers between devices: 11.7 us -> 8.7 us  [swap(): return lax.ppermute(value, 'expert', [(i, i ^ bits) for i in range(peers)])]
    ppermute x1 -> x2, waiting for transfers between devices: 0.01 us -> 2.08 us  [shift_back(): return lax.ppermute(value, ('pipe', 'expert'), pairs)]
    pallas_call x3 -> x2, Pallas kernels: 7.49 us -> 6.04 us  [the longest x1 3.13 us: weight_grads(): pl.pallas_call(functools.partial(grad_kernel, count), out_shape=(jax.Shap...]
    ppermute x9 -> x8, waiting for transfers between devices: 10.9 us -> 9.52 us  [swap(): return lax.ppermute(value, 'expert', [(i, i ^ bits) for i in range(peers)])]
    pallas_call x1, Pallas kernels: 0.33 us -> 1.35 us  [select_rows(): pl.pallas_call(functools.partial(select_kernel, flight), out_shape=(jax.S...]
    select_n x0 -> x1, other arithmetic: none -> 0.75 us  [select_rows(): routes = jnp.where(plane == 0, ids.astype(jnp.float32)[None], probs[None])]
    convert_element_type x1 -> x3, other arithmetic: 0.03 us -> 0.73 us  [the longest x1 0.69 us: select_rows(): routes = jnp.where(plane == 0, ids.astype(jnp.float32)[None], probs[None])]
  transfers between devices with their start and end apart: 10 -> 10, of which waited for: 5 -> 7; matrix products, arithmetic and copies ran while one was open for 0% -> 0% of each run, Pallas kernels for 14% -> 14%
where the time goes in v2:
time: 43.1 us; the launch traced here: 42.9 us
  starting transfers between devices  16.9 us (39%)
  Pallas kernels  11.9 us (28%)
  waiting for transfers between devices  11.6 us (27%)
  other arithmetic  1.58 us (4%)
  between operations  0.74 us (2%)
    ppermute x8, waiting for transfers between devices, swap(): return lax.ppermute(value, 'expert', [(i, i ^ bits) for i in range(peers)])  9.52 us
    ppermute x8, starting transfers between devices, swap(): return lax.ppermute(value, 'expert', [(i, i ^ bits) for i in range(peers)])  8.7 us
    ppermute x2, starting transfers between devices, shift_back(): return lax.ppermute(value, ('pipe', 'expert'), pairs)  8.24 us
    pallas_call x1, Pallas kernels, expert_main(): pl.pallas_call(functools.partial(main_kernel, len(pieces), split), out_sh...  3.39 us
    pallas_call x1, Pallas kernels, weight_grads(): pl.pallas_call(functools.partial(grad_kernel, count), out_shape=(jax.Shap...  3.13 us
    pallas_call x1, Pallas kernels, fetch(): pl.pallas_call(fetch_kernel, out_shape=tuple((jax.ShapeDtypeStruct(w.shap...  2.9 us
    ppermute x2, waiting for transfers between devices, shift_back(): return lax.ppermute(value, ('pipe', 'expert'), pairs)  2.08 us
    pallas_call x1, Pallas kernels, select_rows(): pl.pallas_call(functools.partial(select_kernel, flight), out_shape=(jax.S...  1.35 us
  transfers between devices with their start and end apart: 10, of which 7 were waited for; matrix products, arithmetic and copies ran while one was open for 0% of the time, Pallas kernels for 14%

profile of v2, /device:TPU:1, one launch (start us, length us, event | category | flops | bytes accessed | tf_op | source)
XLA Modules:
  0.0 42.9 jit_solution(18065719209466305463)
XLA Ops:
  0.6 0.7 %convert_bitcast_fusion = f32[4,64]{1,0:T(4,128)S(1)} fusion(s32[1,64,4]{1,2,0:T(4,128)} %param.9), kind=kLoop, calls=%fused_computation.4 | loop fusion | flops 256 | bytes 2048 | tf_op jit(solution)/shard_map/convert_element_type | solution.py:80
  1.3 0.8 %broadcast_select_fusion.refs_0_ = f32[2,4,64]{2,1,0:T(4,128)S(1)} fusion(f32[4,64]{1,0:T(4,128)} %bitcast.22, f32[4,64]{1,0:T(4,128)S(1)} %convert_bitcast_fusion, pred[2]{0:T(512)(128)(4,1)S(1)} %iota_compare_fusion), kind=kLoop, calls=%fused_computation.3 | loop fusion | flops 512 | bytes 4098 | tf_op jit(solution)/shard_map/jit(_where)/select_n | solution.py:80
  2.1 1.4 %select.1 = (bf16[8,2880]{1,0:T(8,128)(2,1)S(1)}, f32[8,128]{1,0:T(8,128)S(1)}) custom-call(f32[2,4,64]{2,1,0:T(4,128)S(1)} %broadcast_select_fusion.refs_0_, bf16[64,2880]{1,0:T(8,128)(2,1)} %bitcast.19, bf16[64,2880]{1,0:T(8,128)(2,1)} %bitcast.20), custom_call_target="tpu_custom_call" | custom-call | tf_op jit(solution)/shard_map/select/pallas_call | solution.py:81
  3.4 3.2 %collective-permute-start.1 = (bf16[8,2880]{1,0:T(8,128)(2,1)S(1)}, bf16[8,2880]{1,0:T(8,128)(2,1)S(1)}, u32[]{:S(2)}, u32[]{:S(2)}) collective-permute-start(bf16[8,2880]{1,0:T(8,128)(2,1)S(1)} %get-tuple-element.18.after_ref.refs_0_), channel_id=1, source_target_pairs={{0,4},{1,5},{2,6},{3,7},{4,0},{5,1},{6,2},{7,3},{8,12},{9,13},{10,... | collective-permute-start | bytes 138248 | tf_op jit(solution)/shard_map/ppermute | solution.py:273
  6.6 1.1 %collective-permute-start = (bf16[8,2880]{1,0:T(8,128)(2,1)S(1)}, bf16[8,2880]{1,0:T(8,128)(2,1)S(1)}, u32[]{:S(2)}, u32[]{:S(2)}) collective-permute-start(bf16[8,2880]{1,0:T(8,128)(2,1)S(1)} %get-tuple-element.18.after_ref.refs_0_), channel_id=1, source_target_pairs={{0,6},{1,7},{2,4},{3,5},{4,2},{5,3},{6,0},{7,1},{8,14},{9,15},{10,... | collective-permute-start | bytes 138248 | tf_op jit(solution)/shard_map/ppermute | solution.py:273
  7.7 0.4 collective-permute-done.1.refs_2_
  8.1 3.3 %collective-permute-done.refs_1_ = bf16[8,2880]{1,0:T(8,128)(2,1)S(1)} collective-permute-done((bf16[8,2880]{1,0:T(8,128)(2,1)S(1)}, bf16[8,2880]{1,0:T(8,128)(2,1)S(1)}, u32[]{:S(2)}, u32[]{:S(2)}) %collective-permute-start) | collective-permute-done | bytes 46112 | tf_op jit(solution)/shard_map/ppermute | solution.py:273
  11.4 1.3 %collective-permute-start.3 = (bf16[24,2880]{1,0:T(8,128)(2,1)S(1)}, bf16[24,2880]{1,0:T(8,128)(2,1)S(1)}, u32[]{:S(2)}, u32[]{:S(2)}) collective-permute-start(bf16[24,2880]{1,0:T(8,128)(2,1)S(1)} %pad_maximum_fusion), channel_id=1, source_target_pairs={{0,1},{1,0},{2,3},{3,2},{4,5},{5,4},{6,7},{7,6},{8,9},{9,8},{10,11... | collective-permute-start | bytes 414728 | tf_op jit(solution)/shard_map/ppermute | solution.py:273
  12.6 0.2 collective-permute-start.2
  12.8 2.7 %collective-permute-done.2.refs_3_ = bf16[8,2880]{1,0:T(8,128)(2,1)S(1)} collective-permute-done((bf16[8,2880]{1,0:T(8,128)(2,1)S(1)}, bf16[8,2880]{1,0:T(8,128)(2,1)S(1)}, u32[]{:S(2)}, u32[]{:S(2)}) %collective-permute-start.2) | collective-permute-done | bytes 46112 | tf_op jit(solution)/shard_map/ppermute | solution.py:273
  15.6 0.3 collective-permute-start.4
  15.8 2.9 %fetch.1 = (bf16[360,2880]{1,0:T(8,128)(2,1)S(1)}, bf16[360,2880]{1,0:T(8,128)(2,1)S(1)}, bf16[360,2880]{1,0:T(8,128)(2,1)S(1)}) custom-call(bf16[8,2880]{1,0:T(8,128)(2,1)S(1)} %get-tuple-element.18.after_ref.refs_0_, bf16[360,2880]{1,0:T(8,128)(2,1)} %bitcast.16, bf16[360,2880]{1,0:T(8,128)(2,1)} %bitcast.17, bf16[360,2880]{1,0:T(8,128)(2,1)} %bitcast.18), custom_call_target="tpu_custom_call" | custom-call | bytes 12441600 | tf_op jit(solution)/shard_map/fetch/pallas_call | solution.py:110
  18.7 0.0 collective-permute-done.4.refs_5_
  18.7 0.0 collective-permute-done.3.refs_4_
  18.8 3.4 %expert_main.1 = (bf16[64,2880]{1,0:T(8,128)(2,1)S(1)}, bf16[64,360]{1,0:T(8,128)(2,1)S(1)}, bf16[64,360]{1,0:T(8,128)(2,1)S(1)}, bf16[64,360]{1,0:T(8,128)(2,1)...) custom-call(bf16[8,2880]{1,0:T(8,128)(2,1)S(1)} %get-tuple-element.18.after_ref.refs_0_, ...), custom_call_target="tpu_custom_call" | custom-call | flops 663552000 | bytes 6220800 | tf_op jit(solution)/shard_map/expert_main/pallas_call | solution.py:191
  22.1 6.3 %collective-permute-start.5 = (bf16[16,3008]{1,0:T(8,128)(2,1)S(1)}, bf16[16,3008]{1,0:T(8,128)(2,1)S(1)}, u32[]{:S(2)}, u32[]{:S(2)}) collective-permute-start(bf16[16,3008]{1,0:T(8,128)(2,1)S(1)} %get-tuple-element.30), channel_id=1, source_target_pairs={{8,0},{9,1},{10,2},{11,3},{12,4},{13,5},{14,6},{15,7},{16,8},{17,9... | collective-permute-start | bytes 288776 | tf_op jit(solution)/shard_map/ppermute | solution.py:283
  28.5 1.9 %collective-permute-start.6 = (bf16[16,2880]{1,0:T(8,128)(2,1)S(1)}, bf16[16,2880]{1,0:T(8,128)(2,1)S(1)}, u32[]{:S(2)}, u32[]{:S(2)}) collective-permute-start(bf16[16,2880]{1,0:T(8,128)(2,1)S(1)} %get-tuple-element.31), channel_id=1, source_target_pairs={{8,1},{9,0},{10,3},{11,2},{12,5},{13,4},{14,7},{15,6},{16,9},{17,8... | collective-permute-start | bytes 276488 | tf_op jit(solution)/shard_map/ppermute | solution.py:283
  30.4 3.1 %weight_grads.1 = (bf16[360,2880]{1,0:T(8,128)(2,1)}, bf16[360,2880]{1,0:T(8,128)(2,1)}, bf16[360,2880]{1,0:T(8,128)(2,1)}) custom-call(bf16[64,360]{1,0:T(8,128)(2,1)S(1)} %get-tuple-element.23.refs_0_, bf16[64,360]{1,0:T(8,128)(2,1)S(1)} %get-tuple-element.24.refs_1_, bf16[64,360]{1,0:T(8,128)(2,1)S(1)} %get-tuple-element.25.refs_2_, ...), custom_call_target="tpu_custom_call" | custom-call | flops 398131200 | bytes 12441600 | tf_op jit(solution)/shard_map/weight_grads/pallas_call | solution.py:229
  33.5 0.0 collective-permute-done.5
  33.6 2.1 %collective-permute-done.6 = bf16[16,2880]{1,0:T(8,128)(2,1)S(1)} collective-permute-done((bf16[16,2880]{1,0:T(8,128)(2,1)S(1)}, bf16[16,2880]{1,0:T(8,128)(2,1)S(1)}, u32[]{:S(2)}, u32[]{:S(2)}) %collective-permute-start.6) | collective-permute-done | bytes 92192 | tf_op jit(solution)/shard_map/ppermute | solution.py:283
  35.7 0.1 collective-permute-start.9
  35.8 2.4 %collective-permute-start.8 = (bf16[4,2880]{1,0:T(4,128)(2,1)S(1)}, bf16[4,2880]{1,0:T(4,128)(2,1)S(1)}, u32[]{:S(2)}, u32[]{:S(2)}) collective-permute-start(bf16[4,2880]{1,0:T(4,128)(2,1)S(1)} %get-tuple-element.35), channel_id=1, source_target_pairs={{0,6},{1,7},{2,4},{3,5},{4,2},{5,3},{6,0},{7,1},{8,14},{9,15},{10,... | collective-permute-start | bytes 69128 | tf_op jit(solution)/shard_map/ppermute | solution.py:273
  38.2 0.2 collective-permute-start.7
  38.4 0.1 slice.26
  38.5 0.1 pad_maximum_fusion.1.kept_ref
  38.6 0.2 collective-permute-done.9.refs_2_
  38.8 1.8 %collective-permute-done.8.refs_1_ = bf16[4,2880]{1,0:T(4,128)(2,1)S(1)} collective-permute-done((bf16[4,2880]{1,0:T(4,128)(2,1)S(1)}, bf16[4,2880]{1,0:T(4,128)(2,1)S(1)}, u32[]{:S(2)}, u32[]{:S(2)}) %collective-permute-start.8) | collective-permute-done | bytes 23072 | tf_op jit(solution)/shard_map/ppermute | solution.py:273
  40.5 1.2 %collective-permute-done.7.refs_0_ = bf16[4,2880]{1,0:T(4,128)(2,1)S(1)} collective-permute-done((bf16[4,2880]{1,0:T(4,128)(2,1)S(1)}, bf16[4,2880]{1,0:T(4,128)(2,1)S(1)}, u32[]{:S(2)}, u32[]{:S(2)}) %collective-permute-start.7) | collective-permute-done | bytes 23072 | tf_op jit(solution)/shard_map/ppermute | solution.py:273
  41.8 1.1 %expand.1 = bf16[64,2880]{1,0:T(8,128)(2,1)} custom-call(f32[4,3008]{1,0:T(4,128)S(1)} %pad_maximum_fusion.1.kept_ref, bf16[4,2880]{1,0:T(4,128)(2,1)S(1)} %collective-permute-done.7.refs_0_, bf16[4,2880]{1,0:T(4,128)(2,1)S(1)} %collective-permute-done.8.refs_1_, bf16[4,2880]{1,0:T(4,128)(2,1)S(1)} %collective-permute-done.9.refs_2_), custom_call_target="tpu_custom_call" | custom-call | tf_op jit(solution)/shard_map/expand/pallas_call | solution.py:261
  (6 shorter events, 0.1 us)
Async XLA Ops:
  3.4 4.7 %collective-permute-start.1 = (bf16[8,2880]{1,0:T(8,128)(2,1)S(1)}, bf16[8,2880]{1,0:T(8,128)(2,1)S(1)}, u32[]{:S(2)}, u32[]{:S(2)}) collective-permute-start(bf16[8,2880]{1,0:T(8,128)(2,1)S(1)} %get-tuple-element.18.after_ref.refs_0_), channel_id=1, source_target_pairs={{0,4},{1,5},{2,6},{3,7},{4,0},{5,1},{6,2},{7,3},{8,12},{9,13},{10,... | collective-permute-start | bytes 138248 | tf_op jit(solution)/shard_map/ppermute | solution.py:273
  6.6 4.7 %collective-permute-start = (bf16[8,2880]{1,0:T(8,128)(2,1)S(1)}, bf16[8,2880]{1,0:T(8,128)(2,1)S(1)}, u32[]{:S(2)}, u32[]{:S(2)}) collective-permute-start(bf16[8,2880]{1,0:T(8,128)(2,1)S(1)} %get-tuple-element.18.after_ref.refs_0_), channel_id=1, source_target_pairs={{0,6},{1,7},{2,4},{3,5},{4,2},{5,3},{6,0},{7,1},{8,14},{9,15},{10,... | collective-permute-start | bytes 138248 | tf_op jit(solution)/shard_map/ppermute | solution.py:273
  11.4 7.4 %collective-permute-start.3 = (bf16[24,2880]{1,0:T(8,128)(2,1)S(1)}, bf16[24,2880]{1,0:T(8,128)(2,1)S(1)}, u32[]{:S(2)}, u32[]{:S(2)}) collective-permute-start(bf16[24,2880]{1,0:T(8,128)(2,1)S(1)} %pad_maximum_fusion), channel_id=1, source_target_pairs={{0,1},{1,0},{2,3},{3,2},{4,5},{5,4},{6,7},{7,6},{8,9},{9,8},{10,11... | collective-permute-start | bytes 414728 | tf_op jit(solution)/shard_map/ppermute | solution.py:273
  12.6 2.9 %collective-permute-start.2 = (bf16[8,2880]{1,0:T(8,128)(2,1)S(1)}, bf16[8,2880]{1,0:T(8,128)(2,1)S(1)}, u32[]{:S(2)}, u32[]{:S(2)}) collective-permute-start(bf16[8,2880]{1,0:T(8,128)(2,1)S(1)} %get-tuple-element.18.after_ref.refs_0_), channel_id=1, source_target_pairs={{0,2},{1,3},{2,0},{3,1},{4,6},{5,7},{6,4},{7,5},{8,10},{9,11},{10,... | collective-permute-start | bytes 138248 | tf_op jit(solution)/shard_map/ppermute | solution.py:273
  15.6 3.2 %collective-permute-start.4 = (bf16[8,2880]{1,0:T(8,128)(2,1)S(1)}, bf16[8,2880]{1,0:T(8,128)(2,1)S(1)}, u32[]{:S(2)}, u32[]{:S(2)}) collective-permute-start(bf16[8,2880]{1,0:T(8,128)(2,1)S(1)} %collective-permute-done.2.refs_3_), channel_id=1, source_target_pairs={{0,1},{1,0},{2,3},{3,2},{4,5},{5,4},{6,7},{7,6},{8,9},{9,8},{10,11... | collective-permute-start | bytes 138248 | tf_op jit(solution)/shard_map/ppermute | solution.py:273
  22.1 11.4 %collective-permute-start.5 = (bf16[16,3008]{1,0:T(8,128)(2,1)S(1)}, bf16[16,3008]{1,0:T(8,128)(2,1)S(1)}, u32[]{:S(2)}, u32[]{:S(2)}) collective-permute-start(bf16[16,3008]{1,0:T(8,128)(2,1)S(1)} %get-tuple-element.30), channel_id=1, source_target_pairs={{8,0},{9,1},{10,2},{11,3},{12,4},{13,5},{14,6},{15,7},{16,8},{17,9... | collective-permute-start | bytes 288776 | tf_op jit(solution)/shard_map/ppermute | solution.py:283
  28.5 7.2 %collective-permute-start.6 = (bf16[16,2880]{1,0:T(8,128)(2,1)S(1)}, bf16[16,2880]{1,0:T(8,128)(2,1)S(1)}, u32[]{:S(2)}, u32[]{:S(2)}) collective-permute-start(bf16[16,2880]{1,0:T(8,128)(2,1)S(1)} %get-tuple-element.31), channel_id=1, source_target_pairs={{8,1},{9,0},{10,3},{11,2},{12,5},{13,4},{14,7},{15,6},{16,9},{17,8... | collective-permute-start | bytes 276488 | tf_op jit(solution)/shard_map/ppermute | solution.py:283
  35.7 3.0 %collective-permute-start.9 = (bf16[4,2880]{1,0:T(4,128)(2,1)S(1)}, bf16[4,2880]{1,0:T(4,128)(2,1)S(1)}, u32[]{:S(2)}, u32[]{:S(2)}) collective-permute-start(bf16[4,2880]{1,0:T(4,128)(2,1)S(1)} %get-tuple-element.34), channel_id=1, source_target_pairs={{0,2},{1,3},{2,0},{3,1},{4,6},{5,7},{6,4},{7,5},{8,10},{9,11},{10,... | collective-permute-start | bytes 69128 | tf_op jit(solution)/shard_map/ppermute | solution.py:273
  35.8 4.7 %collective-permute-start.8 = (bf16[4,2880]{1,0:T(4,128)(2,1)S(1)}, bf16[4,2880]{1,0:T(4,128)(2,1)S(1)}, u32[]{:S(2)}, u32[]{:S(2)}) collective-permute-start(bf16[4,2880]{1,0:T(4,128)(2,1)S(1)} %get-tuple-element.35), channel_id=1, source_target_pairs={{0,6},{1,7},{2,4},{3,5},{4,2},{5,3},{6,0},{7,1},{8,14},{9,15},{10,... | collective-permute-start | bytes 69128 | tf_op jit(solution)/shard_map/ppermute | solution.py:273
  38.2 3.6 %collective-permute-start.7 = (bf16[4,2880]{1,0:T(4,128)(2,1)S(1)}, bf16[4,2880]{1,0:T(4,128)(2,1)S(1)}, u32[]{:S(2)}, u32[]{:S(2)}) collective-permute-start(bf16[4,2880]{1,0:T(4,128)(2,1)S(1)} %get-tuple-element.36), channel_id=1, source_target_pairs={{0,4},{1,5},{2,6},{3,7},{4,0},{5,1},{6,2},{7,3},{8,12},{9,13},{10,... | collective-permute-start | bytes 69128 | tf_op jit(solution)/shard_map/ppermute | solution.py:273

commit v3 on v2

--- a/solution.py
+++ b/solution.py
@@ -13,7 +13,7 @@
 PAIR = 2 * CAP
 LANES = 128
 CHUNK = 1024
-OUT = (6, 4, 2)
+OUT = (4, 2, 6)
 HOME = (4, 6, 2)
 
 VMEM = pl.BlockSpec(memory_space=pltpu.VMEM)
@@ -41,9 +41,7 @@
     ]
     for copy in copies:
         copy.start()
-    ids = routes_ref[0]
-    probs = routes_ref[1]
-    tokens = ids.shape[1]
+    tokens = routes_ref.shape[2]
     before = lax.broadcasted_iota(jnp.int32, (tokens, tokens), 0) < lax.broadcasted_iota(
         jnp.int32, (tokens, tokens), 1
     )
@@ -53,10 +51,8 @@
     slot = lax.rem(row, CAP)
     choosers = []
     for expert in range(flight):
-        matched = ids == float(expert)
-        hit = jnp.sum(jnp.where(matched, 1.0, 0.0), axis=0, keepdims=True)
-        prob = jnp.sum(jnp.where(matched, probs, 0.0), axis=0, keepdims=True)
-        hits = jnp.broadcast_to(hit, (PAIR, tokens))
+        prob = jnp.sum(routes_ref[expert], axis=0, keepdims=True)
+        hits = jnp.broadcast_to(jnp.where(prob > 0.0, 1.0, 0.0), (PAIR, tokens))
         ranks = jnp.dot(hits.astype(jnp.bfloat16), before, preferred_element_type=jnp.float32)
         chosen = jnp.where((hits > 0.5) & (ranks.astype(jnp.int32) == slot), 1.0, 0.0)
         scale = jnp.sum(chosen * prob, axis=1, keepdims=True)
@@ -76,8 +72,8 @@
 
 def select_rows(ids, probs, inputs, cotan, flight):
     width = inputs.shape[1]
-    plane = lax.broadcasted_iota(jnp.int32, (2, *ids.shape), 0)
-    routes = jnp.where(plane == 0, ids.astype(jnp.float32)[None], probs[None])
+    labels = jnp.arange(flight, dtype=jnp.int32)
+    routes = jnp.where(ids[None] == labels[:, None, None], probs[None], 0.0)
     return pl.pallas_call(
         functools.partial(select_kernel, flight),
         out_shape=(
@@ -93,34 +89,24 @@
     )(routes, inputs, cotan)
 
 
-def fetch_kernel(after_ref, *refs):
-    del after_ref
-    count = len(refs) // 2
-    copies = [
-        pltpu.make_async_copy(refs[i], refs[count + i], refs[-1].at[i]) for i in range(count)
-    ]
-    for copy in copies:
-        copy.start()
-    for copy in copies:
-        copy.wait()
-
-
-def fetch(after, *weights):
-    held = sum(w.size * w.dtype.itemsize for w in weights)
-    return pl.pallas_call(
-        fetch_kernel,
-        out_shape=tuple(jax.ShapeDtypeStruct(w.shape, w.dtype) for w in weights),
-        in_specs=[HBM] * (len(weights) + 1),
-        out_specs=(VMEM,) * len(weights),
-        scratch_shapes=[pltpu.SemaphoreType.DMA((len(weights),))],
-        compiler_params=pltpu.CompilerParams(vmem_limit_bytes=47600 << 10),
-        cost_estimate=pl.CostEstimate(
-            flops=0,
-            bytes_accessed=sum(2 * w.size * w.dtype.itemsize for w in weights),
-            transcendentals=0,
-        ),
-        name="fetch",
-    )(after, *weights)
+def join_kernel(*refs):
+    out_ref, start = refs[-1], 0
+    for ref in refs[:-1]:
+        out_ref[pl.ds(start, ref.shape[0]), :] = ref[...]
+        start += ref.shape[0]
+
+
+def join(*pieces):
+    rows, width = sum(piece.shape[0] for piece in pieces), pieces[0].shape[1]
+    return pl.pallas_call(
+        join_kernel,
+        out_shape=jax.ShapeDtypeStruct((rows, width), pieces[0].dtype),
+        in_specs=[VMEM] * len(pieces),
+        out_specs=VMEM,
+        compiler_params=pltpu.CompilerParams(vmem_limit_bytes=1 << 20),
+        cost_estimate=pl.CostEstimate(flops=10**10, bytes_accessed=0, transcendentals=0),
+        name="join",
+    )(*pieces)
 
 
 def main_kernel(pieces, split, *refs):
@@ -284,9 +270,8 @@
 
 
 def one_expert(own, slots, weights, tokens, width):
-    weights = fetch(own, *weights)
     first, second, third = (swap(own, bits) for bits in OUT)
-    across = [swap(jnp.concatenate([own, first, second], axis=0), 1)]
+    across = [swap(join(own, first, second), 1)]
     across.append(swap(third, 1))
     pieces = (own, first, second, third, *across)
     rows, gate, up, hidden, keep, send = expert_main(pieces, slots, *weights, split=True)

time: 43.1 us -> 41.2 us (0.956)
  Pallas kernels: 11.9 us -> 8.97 us
  starting transfers between devices: 16.9 us -> 18.7 us
  other arithmetic: 1.58 us -> 0.82 us
    pallas_call x1, Pallas kernels: 2.9 us -> 0.01 us  [join(): pl.pallas_call(join_kernel, out_shape=jax.ShapeDtypeStruct((rows, width),...]
    ppermute x8, starting transfers between devices: 8.7 us -> 10.7 us  [swap(): return lax.ppermute(value, 'expert', [(i, i ^ bits) for i in range(peers)])]
    convert_element_type x1 -> x0, other arithmetic: 0.69 us -> none  [select_rows(): routes = jnp.where(plane == 0, ids.astype(jnp.float32)[None], probs[None])]
  transfers between devices with their start and end apart: 10 -> 10, of which waited for: 7 -> 8; matrix products, arithmetic and copies ran while one was open for 0% -> 0% of each run, Pallas kernels for 14% -> 8%
where the time goes in v3:
time: 41.2 us; the launch traced here: 41 us
  starting transfers between devices  18.7 us (45%)
  waiting for transfers between devices  11.6 us (28%)
  Pallas kernels  8.97 us (22%)
  other arithmetic  0.82 us (2%)
  between operations  0.76 us (2%)
    ppermute x8, starting transfers between devices, swap(): return lax.ppermute(value, 'expert', [(i, i ^ bits) for i in range(peers)])  10.7 us
    ppermute x8, waiting for transfers between devices, swap(): return lax.ppermute(value, 'expert', [(i, i ^ bits) for i in range(peers)])  9.52 us
    ppermute x2, starting transfers between devices, shift_back(): return lax.ppermute(value, ('pipe', 'expert'), pairs)  8.02 us
    pallas_call x1, Pallas kernels, expert_main(): pl.pallas_call(functools.partial(main_kernel, len(pieces), split), out_sh...  3.39 us
    pallas_call x1, Pallas kernels, weight_grads(): pl.pallas_call(functools.partial(grad_kernel, count), out_shape=(jax.Shap...  3.12 us
    ppermute x2, waiting for transfers between devices, shift_back(): return lax.ppermute(value, ('pipe', 'expert'), pairs)  2.09 us
    pallas_call x1, Pallas kernels, select_rows(): pl.pallas_call(functools.partial(select_kernel, flight), out_shape=(jax.S...  1.35 us
    pallas_call x1, Pallas kernels, expand(): pl.pallas_call(expand_kernel, out_shape=jax.ShapeDtypeStruct((tokens, wid...  1.1 us
  transfers between devices with their start and end apart: 10, of which 8 were waited for; matrix products, arithmetic and copies ran while one was open for 0% of the time, Pallas kernels for 8%

profile of v3, /device:TPU:1, one launch (start us, length us, event | category | flops | bytes accessed | tf_op | source)
XLA Modules:
  0.0 41.0 jit_solution(3738027471896610966)
XLA Ops:
  0.6 0.7 %select_bitcast_fusion.refs_0_ = f32[1,4,64]{2,1,0:T(4,128)S(1)} fusion(f32[1,64,4]{1,2,0:T(4,128)} %param.10, s32[1,64,4]{1,2,0:T(4,128)} %param.9), kind=kLoop, calls=%fused_computation.2 | loop fusion | flops 512 | bytes 3072 | tf_op jit(solution)/shard_map/jit(_where)/select_n | solution.py:76
  1.3 1.3 %select.1 = (bf16[8,2880]{1,0:T(8,128)(2,1)S(1)}, f32[8,128]{1,0:T(8,128)S(1)}) custom-call(f32[1,4,64]{2,1,0:T(4,128)S(1)} %select_bitcast_fusion.refs_0_, bf16[64,2880]{1,0:T(8,128)(2,1)} %bitcast.18, bf16[64,2880]{1,0:T(8,128)(2,1)} %bitcast.19), custom_call_target="tpu_custom_call" | custom-call | tf_op jit(solution)/shard_map/select/pallas_call | solution.py:77
  2.7 0.0 copy-start
  2.7 0.0 copy-start.1
  2.7 0.0 copy-start.2
  2.7 3.2 %collective-permute-start = (bf16[8,2880]{1,0:T(8,128)(2,1)S(1)}, bf16[8,2880]{1,0:T(8,128)(2,1)S(1)}, u32[]{:S(2)}, u32[]{:S(2)}) collective-permute-start(bf16[8,2880]{1,0:T(8,128)(2,1)S(1)} %get-tuple-element.15.refs_0_), channel_id=1, source_target_pairs={{0,4},{1,5},{2,6},{3,7},{4,0},{5,1},{6,2},{7,3},{8,12},{9,13},{10,... | collective-permute-start | bytes 138248 | tf_op jit(solution)/shard_map/ppermute | solution.py:259
  5.9 1.3 %collective-permute-start.1 = (bf16[8,2880]{1,0:T(8,128)(2,1)S(1)}, bf16[8,2880]{1,0:T(8,128)(2,1)S(1)}, u32[]{:S(2)}, u32[]{:S(2)}) collective-permute-start(bf16[8,2880]{1,0:T(8,128)(2,1)S(1)} %get-tuple-element.15.refs_0_), channel_id=1, source_target_pairs={{0,2},{1,3},{2,0},{3,1},{4,6},{5,7},{6,4},{7,5},{8,10},{9,11},{10,... | collective-permute-start | bytes 138248 | tf_op jit(solution)/shard_map/ppermute | solution.py:259
  7.2 0.2 collective-permute-done.refs_1_
  7.4 1.7 %collective-permute-done.1.refs_2_ = bf16[8,2880]{1,0:T(8,128)(2,1)S(1)} collective-permute-done((bf16[8,2880]{1,0:T(8,128)(2,1)S(1)}, bf16[8,2880]{1,0:T(8,128)(2,1)S(1)}, u32[]{:S(2)}, u32[]{:S(2)}) %collective-permute-start.1) | collective-permute-done | bytes 46112 | tf_op jit(solution)/shard_map/ppermute | solution.py:259
  9.1 1.6 %collective-permute-start.3 = (bf16[24,2880]{1,0:T(8,128)(2,1)S(1)}, bf16[24,2880]{1,0:T(8,128)(2,1)S(1)}, u32[]{:S(2)}, u32[]{:S(2)}) collective-permute-start(bf16[24,2880]{1,0:T(8,128)(2,1)S(1)} %join.1), channel_id=1, source_target_pairs={{0,1},{1,0},{2,3},{3,2},{4,5},{5,4},{6,7},{7,6},{8,9},{9,8},{10,11... | collective-permute-start | bytes 414728 | tf_op jit(solution)/shard_map/ppermute | solution.py:259
  10.6 1.9 %collective-permute-start.2 = (bf16[8,2880]{1,0:T(8,128)(2,1)S(1)}, bf16[8,2880]{1,0:T(8,128)(2,1)S(1)}, u32[]{:S(2)}, u32[]{:S(2)}) collective-permute-start(bf16[8,2880]{1,0:T(8,128)(2,1)S(1)} %get-tuple-element.15.refs_0_), channel_id=1, source_target_pairs={{0,6},{1,7},{2,4},{3,5},{4,2},{5,3},{6,0},{7,1},{8,14},{9,15},{10,... | collective-permute-start | bytes 138248 | tf_op jit(solution)/shard_map/ppermute | solution.py:259
  12.5 2.9 %collective-permute-done.2.refs_3_ = bf16[8,2880]{1,0:T(8,128)(2,1)S(1)} collective-permute-done((bf16[8,2880]{1,0:T(8,128)(2,1)S(1)}, bf16[8,2880]{1,0:T(8,128)(2,1)S(1)}, u32[]{:S(2)}, u32[]{:S(2)}) %collective-permute-start.2) | collective-permute-done | bytes 46112 | tf_op jit(solution)/shard_map/ppermute | solution.py:259
  15.3 0.1 collective-permute-start.4
  15.4 2.8 %collective-permute-done.4.refs_5_ = bf16[8,2880]{1,0:T(8,128)(2,1)S(1)} collective-permute-done((bf16[8,2880]{1,0:T(8,128)(2,1)S(1)}, bf16[8,2880]{1,0:T(8,128)(2,1)S(1)}, u32[]{:S(2)}, u32[]{:S(2)}) %collective-permute-start.4) | collective-permute-done | bytes 46112 | tf_op jit(solution)/shard_map/ppermute | solution.py:259
  18.2 0.0 collective-permute-done.3.refs_4_
  18.3 0.0 copy-done
  18.3 0.0 copy-done.1
  18.3 0.0 copy-done.2
  18.3 3.4 %expert_main.1 = (bf16[64,2880]{1,0:T(8,128)(2,1)S(1)}, bf16[64,360]{1,0:T(8,128)(2,1)S(1)}, bf16[64,360]{1,0:T(8,128)(2,1)S(1)}, bf16[64,360]{1,0:T(8,128)(2,1)...) custom-call(bf16[8,2880]{1,0:T(8,128)(2,1)S(1)} %get-tuple-element.15.refs_0_, ...), custom_call_target="tpu_custom_call" | custom-call | flops 663552000 | bytes 6220800 | tf_op jit(solution)/shard_map/expert_main/pallas_call | solution.py:177
  21.7 6.1 %collective-permute-start.5 = (bf16[16,3008]{1,0:T(8,128)(2,1)S(1)}, bf16[16,3008]{1,0:T(8,128)(2,1)S(1)}, u32[]{:S(2)}, u32[]{:S(2)}) collective-permute-start(bf16[16,3008]{1,0:T(8,128)(2,1)S(1)} %get-tuple-element.24), channel_id=1, source_target_pairs={{8,0},{9,1},{10,2},{11,3},{12,4},{13,5},{14,6},{15,7},{16,8},{17,9... | collective-permute-start | bytes 288776 | tf_op jit(solution)/shard_map/ppermute | solution.py:269
  27.8 1.9 %collective-permute-start.6 = (bf16[16,2880]{1,0:T(8,128)(2,1)S(1)}, bf16[16,2880]{1,0:T(8,128)(2,1)S(1)}, u32[]{:S(2)}, u32[]{:S(2)}) collective-permute-start(bf16[16,2880]{1,0:T(8,128)(2,1)S(1)} %get-tuple-element.25), channel_id=1, source_target_pairs={{8,1},{9,0},{10,3},{11,2},{12,5},{13,4},{14,7},{15,6},{16,9},{17,8... | collective-permute-start | bytes 276488 | tf_op jit(solution)/shard_map/ppermute | solution.py:269
  29.7 3.1 %weight_grads.1 = (bf16[360,2880]{1,0:T(8,128)(2,1)}, bf16[360,2880]{1,0:T(8,128)(2,1)}, bf16[360,2880]{1,0:T(8,128)(2,1)}) custom-call(bf16[64,360]{1,0:T(8,128)(2,1)S(1)} %get-tuple-element.17.refs_0_, bf16[64,360]{1,0:T(8,128)(2,1)S(1)} %get-tuple-element.18.refs_1_, bf16[64,360]{1,0:T(8,128)(2,1)S(1)} %get-tuple-element.19.refs_2_, ...), custom_call_target="tpu_custom_call" | custom-call | flops 398131200 | bytes 12441600 | tf_op jit(solution)/shard_map/weight_grads/pallas_call | solution.py:215
  32.8 0.0 collective-permute-done.5
  32.9 2.1 %collective-permute-done.6 = bf16[16,2880]{1,0:T(8,128)(2,1)S(1)} collective-permute-done((bf16[16,2880]{1,0:T(8,128)(2,1)S(1)}, bf16[16,2880]{1,0:T(8,128)(2,1)S(1)}, u32[]{:S(2)}, u32[]{:S(2)}) %collective-permute-start.6) | collective-permute-done | bytes 92192 | tf_op jit(solution)/shard_map/ppermute | solution.py:269
  35.0 0.1 collective-permute-start.7
  35.1 2.1 %collective-permute-start.8 = (bf16[4,2880]{1,0:T(4,128)(2,1)S(1)}, bf16[4,2880]{1,0:T(4,128)(2,1)S(1)}, u32[]{:S(2)}, u32[]{:S(2)}) collective-permute-start(bf16[4,2880]{1,0:T(4,128)(2,1)S(1)} %get-tuple-element.29), channel_id=1, source_target_pairs={{0,6},{1,7},{2,4},{3,5},{4,2},{5,3},{6,0},{7,1},{8,14},{9,15},{10,... | collective-permute-start | bytes 69128 | tf_op jit(solution)/shard_map/ppermute | solution.py:259
  37.2 0.5 %collective-permute-start.9 = (bf16[4,2880]{1,0:T(4,128)(2,1)S(1)}, bf16[4,2880]{1,0:T(4,128)(2,1)S(1)}, u32[]{:S(2)}, u32[]{:S(2)}) collective-permute-start(bf16[4,2880]{1,0:T(4,128)(2,1)S(1)} %get-tuple-element.28), channel_id=1, source_target_pairs={{0,2},{1,3},{2,0},{3,1},{4,6},{5,7},{6,4},{7,5},{8,10},{9,11},{10,... | collective-permute-start | bytes 69128 | tf_op jit(solution)/shard_map/ppermute | solution.py:259
  37.8 0.1 slice.26
  37.8 0.1 pad_maximum_fusion.kept_ref
  37.9 1.1 %collective-permute-done.7.refs_0_ = bf16[4,2880]{1,0:T(4,128)(2,1)S(1)} collective-permute-done((bf16[4,2880]{1,0:T(4,128)(2,1)S(1)}, bf16[4,2880]{1,0:T(4,128)(2,1)S(1)}, u32[]{:S(2)}, u32[]{:S(2)}) %collective-permute-start.7) | collective-permute-done | bytes 23072 | tf_op jit(solution)/shard_map/ppermute | solution.py:259
  39.0 0.7 %collective-permute-done.8.refs_1_ = bf16[4,2880]{1,0:T(4,128)(2,1)S(1)} collective-permute-done((bf16[4,2880]{1,0:T(4,128)(2,1)S(1)}, bf16[4,2880]{1,0:T(4,128)(2,1)S(1)}, u32[]{:S(2)}, u32[]{:S(2)}) %collective-permute-start.8) | collective-permute-done | bytes 23072 | tf_op jit(solution)/shard_map/ppermute | solution.py:259
  39.7 0.3 collective-permute-done.9.refs_2_
  39.9 1.1 %expand.1 = bf16[64,2880]{1,0:T(8,128)(2,1)} custom-call(f32[4,3008]{1,0:T(4,128)S(1)} %pad_maximum_fusion.kept_ref, bf16[4,2880]{1,0:T(4,128)(2,1)S(1)} %collective-permute-done.7.refs_0_, bf16[4,2880]{1,0:T(4,128)(2,1)S(1)} %collective-permute-done.8.refs_1_, bf16[4,2880]{1,0:T(4,128)(2,1)S(1)} %collective-permute-done.9.refs_2_), custom_call_target="tpu_custom_call" | custom-call | tf_op jit(solution)/shard_map/expand/pallas_call | solution.py:247
  (5 shorter events, 0.1 us)
Async XLA Ops:
  2.7 15.6 %copy-start = (bf16[1,360,2880]{2,1,0:T(8,128)(2,1)S(1)}, bf16[1,360,2880]{2,1,0:T(8,128)(2,1)}, u32[]{:S(2)}) copy-start(bf16[1,360,2880]{2,1,0:T(8,128)(2,1)} %param.11) | copy-start | bytes 6220804
  2.7 15.6 %copy-start.1 = (bf16[1,360,2880]{2,1,0:T(8,128)(2,1)S(1)}, bf16[1,360,2880]{2,1,0:T(8,128)(2,1)}, u32[]{:S(2)}) copy-start(bf16[1,360,2880]{2,1,0:T(8,128)(2,1)} %param.12) | copy-start | bytes 6220804
  2.7 15.5 %copy-start.2 = (bf16[1,360,2880]{2,1,0:T(8,128)(2,1)S(1)}, bf16[1,360,2880]{2,1,0:T(8,128)(2,1)}, u32[]{:S(2)}) copy-start(bf16[1,360,2880]{2,1,0:T(8,128)(2,1)} %param.13) | copy-start | bytes 6220804
  2.7 4.7 %collective-permute-start = (bf16[8,2880]{1,0:T(8,128)(2,1)S(1)}, bf16[8,2880]{1,0:T(8,128)(2,1)S(1)}, u32[]{:S(2)}, u32[]{:S(2)}) collective-permute-start(bf16[8,2880]{1,0:T(8,128)(2,1)S(1)} %get-tuple-element.15.refs_0_), channel_id=1, source_target_pairs={{0,4},{1,5},{2,6},{3,7},{4,0},{5,1},{6,2},{7,3},{8,12},{9,13},{10,... | collective-permute-start | bytes 138248 | tf_op jit(solution)/shard_map/ppermute | solution.py:259
  5.9 3.1 %collective-permute-start.1 = (bf16[8,2880]{1,0:T(8,128)(2,1)S(1)}, bf16[8,2880]{1,0:T(8,128)(2,1)S(1)}, u32[]{:S(2)}, u32[]{:S(2)}) collective-permute-start(bf16[8,2880]{1,0:T(8,128)(2,1)S(1)} %get-tuple-element.15.refs_0_), channel_id=1, source_target_pairs={{0,2},{1,3},{2,0},{3,1},{4,6},{5,7},{6,4},{7,5},{8,10},{9,11},{10,... | collective-permute-start | bytes 138248 | tf_op jit(solution)/shard_map/ppermute | solution.py:259
  9.1 9.2 %collective-permute-start.3 = (bf16[24,2880]{1,0:T(8,128)(2,1)S(1)}, bf16[24,2880]{1,0:T(8,128)(2,1)S(1)}, u32[]{:S(2)}, u32[]{:S(2)}) collective-permute-start(bf16[24,2880]{1,0:T(8,128)(2,1)S(1)} %join.1), channel_id=1, source_target_pairs={{0,1},{1,0},{2,3},{3,2},{4,5},{5,4},{6,7},{7,6},{8,9},{9,8},{10,11... | collective-permute-start | bytes 414728 | tf_op jit(solution)/shard_map/ppermute | solution.py:259
  10.6 4.7 %collective-permute-start.2 = (bf16[8,2880]{1,0:T(8,128)(2,1)S(1)}, bf16[8,2880]{1,0:T(8,128)(2,1)S(1)}, u32[]{:S(2)}, u32[]{:S(2)}) collective-permute-start(bf16[8,2880]{1,0:T(8,128)(2,1)S(1)} %get-tuple-element.15.refs_0_), channel_id=1, source_target_pairs={{0,6},{1,7},{2,4},{3,5},{4,2},{5,3},{6,0},{7,1},{8,14},{9,15},{10,... | collective-permute-start | bytes 138248 | tf_op jit(solution)/shard_map/ppermute | solution.py:259
  15.3 2.9 %collective-permute-start.4 = (bf16[8,2880]{1,0:T(8,128)(2,1)S(1)}, bf16[8,2880]{1,0:T(8,128)(2,1)S(1)}, u32[]{:S(2)}, u32[]{:S(2)}) collective-permute-start(bf16[8,2880]{1,0:T(8,128)(2,1)S(1)} %collective-permute-done.2.refs_3_), channel_id=1, source_target_pairs={{0,1},{1,0},{2,3},{3,2},{4,5},{5,4},{6,7},{7,6},{8,9},{9,8},{10,11... | collective-permute-start | bytes 138248 | tf_op jit(solution)/shard_map/ppermute | solution.py:259
  21.7 11.2 %collective-permute-start.5 = (bf16[16,3008]{1,0:T(8,128)(2,1)S(1)}, bf16[16,3008]{1,0:T(8,128)(2,1)S(1)}, u32[]{:S(2)}, u32[]{:S(2)}) collective-permute-start(bf16[16,3008]{1,0:T(8,128)(2,1)S(1)} %get-tuple-element.24), channel_id=1, source_target_pairs={{8,0},{9,1},{10,2},{11,3},{12,4},{13,5},{14,6},{15,7},{16,8},{17,9... | collective-permute-start | bytes 288776 | tf_op jit(solution)/shard_map/ppermute | solution.py:269
  27.8 7.2 %collective-permute-start.6 = (bf16[16,2880]{1,0:T(8,128)(2,1)S(1)}, bf16[16,2880]{1,0:T(8,128)(2,1)S(1)}, u32[]{:S(2)}, u32[]{:S(2)}) collective-permute-start(bf16[16,2880]{1,0:T(8,128)(2,1)S(1)} %get-tuple-element.25), channel_id=1, source_target_pairs={{8,1},{9,0},{10,3},{11,2},{12,5},{13,4},{14,7},{15,6},{16,9},{17,8... | collective-permute-start | bytes 276488 | tf_op jit(solution)/shard_map/ppermute | solution.py:269
  35.0 3.9 %collective-permute-start.7 = (bf16[4,2880]{1,0:T(4,128)(2,1)S(1)}, bf16[4,2880]{1,0:T(4,128)(2,1)S(1)}, u32[]{:S(2)}, u32[]{:S(2)}) collective-permute-start(bf16[4,2880]{1,0:T(4,128)(2,1)S(1)} %get-tuple-element.30), channel_id=1, source_target_pairs={{0,4},{1,5},{2,6},{3,7},{4,0},{5,1},{6,2},{7,3},{8,12},{9,13},{10,... | collective-permute-start | bytes 69128 | tf_op jit(solution)/shard_map/ppermute | solution.py:259
  35.1 4.5 %collective-permute-start.8 = (bf16[4,2880]{1,0:T(4,128)(2,1)S(1)}, bf16[4,2880]{1,0:T(4,128)(2,1)S(1)}, u32[]{:S(2)}, u32[]{:S(2)}) collective-permute-start(bf16[4,2880]{1,0:T(4,128)(2,1)S(1)} %get-tuple-element.29), channel_id=1, source_target_pairs={{0,6},{1,7},{2,4},{3,5},{4,2},{5,3},{6,0},{7,1},{8,14},{9,15},{10,... | collective-permute-start | bytes 69128 | tf_op jit(solution)/shard_map/ppermute | solution.py:259
  37.2 2.7 %collective-permute-start.9 = (bf16[4,2880]{1,0:T(4,128)(2,1)S(1)}, bf16[4,2880]{1,0:T(4,128)(2,1)S(1)}, u32[]{:S(2)}, u32[]{:S(2)}) collective-permute-start(bf16[4,2880]{1,0:T(4,128)(2,1)S(1)} %get-tuple-element.28), channel_id=1, source_target_pairs={{0,2},{1,3},{2,0},{3,1},{4,6},{5,7},{6,4},{7,5},{8,10},{9,11},{10,... | collective-permute-start | bytes 69128 | tf_op jit(solution)/shard_map/ppermute | solution.py:259

commit v4 on v3

--- a/solution.py
+++ b/solution.py
@@ -32,15 +32,7 @@
     )
 
 
-def select_kernel(flight, *refs):
-    routes_ref, sources = refs[0], refs[1:3]
-    (rows_ref, slots_ref), held, sems = refs[3:5], refs[5:7], refs[7]
-    copies = [
-        pltpu.make_async_copy(source, target, sems.at[i])
-        for i, (source, target) in enumerate(zip(sources, held))
-    ]
-    for copy in copies:
-        copy.start()
+def route_kernel(flight, routes_ref, chooser_ref, scale_ref, slots_ref):
     tokens = routes_ref.shape[2]
     before = lax.broadcasted_iota(jnp.int32, (tokens, tokens), 0) < lax.broadcasted_iota(
         jnp.int32, (tokens, tokens), 1
@@ -49,7 +41,6 @@
     row = lax.broadcasted_iota(jnp.int32, (PAIR, tokens), 0)
     token = lax.broadcasted_iota(jnp.int32, (PAIR, tokens), 1).astype(jnp.float32)
     slot = lax.rem(row, CAP)
-    choosers = []
     for expert in range(flight):
         prob = jnp.sum(routes_ref[expert], axis=0, keepdims=True)
         hits = jnp.broadcast_to(jnp.where(prob > 0.0, 1.0, 0.0), (PAIR, tokens))
@@ -57,15 +48,20 @@
         chosen = jnp.where((hits > 0.5) & (ranks.astype(jnp.int32) == slot), 1.0, 0.0)
         scale = jnp.sum(chosen * prob, axis=1, keepdims=True)
         number = jnp.sum(chosen * token, axis=1, keepdims=True)
-        slots_ref[pl.ds(expert * PAIR, PAIR), :] = jnp.broadcast_to(number, (PAIR, LANES))
-        choosers.append((chosen.astype(jnp.bfloat16), scale))
-    for copy in copies:
-        copy.wait()
-    for expert, (chooser, scale) in enumerate(choosers):
-        taken = jnp.dot(chooser, held[0][...], preferred_element_type=jnp.float32)
-        cotan = jnp.dot(chooser, held[1][...], preferred_element_type=jnp.float32) * scale
+        part = pl.ds(expert * PAIR, PAIR)
+        slots_ref[part, :] = jnp.broadcast_to(number, (PAIR, LANES))
+        scale_ref[part, :] = jnp.broadcast_to(scale, (PAIR, LANES))
+        chooser_ref[part, :] = chosen.astype(jnp.bfloat16)
+
+
+def select_kernel(chooser_ref, scale_ref, input_ref, cotan_ref, rows_ref):
+    for start in range(0, rows_ref.shape[0], PAIR):
+        part = pl.ds(start, PAIR)
+        chooser = chooser_ref[part, :]
+        taken = jnp.dot(chooser, input_ref[...], preferred_element_type=jnp.float32)
+        cotan = jnp.dot(chooser, cotan_ref[...], preferred_element_type=jnp.float32)
         wide = lax.broadcasted_iota(jnp.int32, taken.shape, 0) < CAP
-        rows_ref[pl.ds(expert * PAIR, PAIR), :] = jnp.where(wide, taken, cotan).astype(
+        rows_ref[part, :] = jnp.where(wide, taken, cotan * scale_ref[part, :1]).astype(
             jnp.bfloat16
         )
 
@@ -74,19 +70,29 @@
     width = inputs.shape[1]
     labels = jnp.arange(flight, dtype=jnp.int32)
     routes = jnp.where(ids[None] == labels[:, None, None], probs[None], 0.0)
-    return pl.pallas_call(
-        functools.partial(select_kernel, flight),
+    rows = flight * PAIR
+    chooser, scale, slots = pl.pallas_call(
+        functools.partial(route_kernel, flight),
         out_shape=(
-            jax.ShapeDtypeStruct((flight * PAIR, width), jnp.bfloat16),
-            jax.ShapeDtypeStruct((flight * PAIR, LANES), jnp.float32),
+            jax.ShapeDtypeStruct((rows, ids.shape[1]), jnp.bfloat16),
+            jax.ShapeDtypeStruct((rows, LANES), jnp.float32),
+            jax.ShapeDtypeStruct((rows, LANES), jnp.float32),
         ),
-        in_specs=[VMEM, HBM, HBM],
-        out_specs=(VMEM, VMEM),
-        scratch_shapes=[pltpu.VMEM(value.shape, value.dtype) for value in (inputs, cotan)]
-        + [pltpu.SemaphoreType.DMA((2,))],
-        compiler_params=pltpu.CompilerParams(vmem_limit_bytes=55000 << 10),
+        in_specs=[VMEM],
+        out_specs=(VMEM,) * 3,
+        compiler_params=pltpu.CompilerParams(vmem_limit_bytes=2 << 20),
+        cost_estimate=pl.CostEstimate(flops=10**9, bytes_accessed=0, transcendentals=0),
+        name="route",
+    )(routes)
+    taken = pl.pallas_call(
+        select_kernel,
+        out_shape=jax.ShapeDtypeStruct((rows, width), jnp.bfloat16),
+        in_specs=[VMEM] * 4,
+        out_specs=VMEM,
+        compiler_params=pltpu.CompilerParams(vmem_limit_bytes=2 << 20),
         name="select",
-    )(routes, inputs, cotan)
+    )(chooser, scale, inputs, cotan)
+    return taken, slots
 
 
 def join_kernel(*refs):

time: 41.2 us -> 40.5 us (0.983)
  Pallas kernels: 8.97 us -> 8.04 us
    pallas_call x1 -> x2, Pallas kernels: 1.35 us -> 0.42 us  [the longest x1 0.21 us: select_rows(): pl.pallas_call(select_kernel, out_shape=jax.ShapeDtypeStruct((rows, width...]
where the time goes in v4:
time: 40.5 us; the launch traced here: 40.3 us
  starting transfers between devices  18.7 us (46%)
  waiting for transfers between devices  11.6 us (29%)
  Pallas kernels  8.04 us (20%)
  other arithmetic  0.89 us (2%)
  between operations  0.78 us (2%)
    ppermute x8, starting transfers between devices, swap(): return lax.ppermute(value, 'expert', [(i, i ^ bits) for i in range(peers)])  10.7 us
    ppermute x8, waiting for transfers between devices, swap(): return lax.ppermute(value, 'expert', [(i, i ^ bits) for i in range(peers)])  9.52 us
    ppermute x2, starting transfers between devices, shift_back(): return lax.ppermute(value, ('pipe', 'expert'), pairs)  8.03 us
    pallas_call x1, Pallas kernels, expert_main(): pl.pallas_call(functools.partial(main_kernel, len(pieces), split), out_sh...  3.39 us
    pallas_call x1, Pallas kernels, weight_grads(): pl.pallas_call(functools.partial(grad_kernel, count), out_shape=(jax.Shap...  3.12 us
    ppermute x2, waiting for transfers between devices, shift_back(): return lax.ppermute(value, ('pipe', 'expert'), pairs)  2.09 us
    pallas_call x1, Pallas kernels, expand(): pl.pallas_call(expand_kernel, out_shape=jax.ShapeDtypeStruct((tokens, wid...  1.1 us
  transfers between devices with their start and end apart: 10, of which 8 were waited for; matrix products, arithmetic and copies ran while one was open for 0% of the time, Pallas kernels for 8%

profile of v4, /device:TPU:1, one launch (start us, length us, event | category | flops | bytes accessed | tf_op | source)
XLA Modules:
  0.0 40.3 jit_solution(18067257081323471027)
XLA Ops:
  0.6 0.0 copy-start.3
  0.6 0.0 copy-start.4
  0.7 0.8 %select_bitcast_fusion.routes_ref = f32[1,4,64]{2,1,0:T(4,128)S(1)} fusion(f32[1,64,4]{1,2,0:T(4,128)} %param.10, s32[1,64,4]{1,2,0:T(4,128)} %param.9), kind=kLoop, calls=%fused_computation.2 | loop fusion | flops 512 | bytes 3072 | tf_op jit(solution)/shard_map/jit(_where)/select_n | solution.py:72
  1.4 0.2 route.1
  1.6 0.0 copy-done.3
  1.7 0.1 copy-done.4
  1.8 0.2 select.1.refs_0_
  2.0 0.0 copy-start
  2.0 0.0 copy-start.1
  2.0 0.0 copy-start.2
  2.0 3.2 %collective-permute-start = (bf16[8,2880]{1,0:T(8,128)(2,1)S(1)}, bf16[8,2880]{1,0:T(8,128)(2,1)S(1)}, u32[]{:S(2)}, u32[]{:S(2)}) collective-permute-start(bf16[8,2880]{1,0:T(8,128)(2,1)S(1)} %select.1.refs_0_), channel_id=1, source_target_pairs={{0,4},{1,5},{2,6},{3,7},{4,0},{5,1},{6,2},{7,3},{8,12},{9,13},{10,... | collective-permute-start | bytes 138248 | tf_op jit(solution)/shard_map/ppermute | solution.py:265
  5.2 1.3 %collective-permute-start.1 = (bf16[8,2880]{1,0:T(8,128)(2,1)S(1)}, bf16[8,2880]{1,0:T(8,128)(2,1)S(1)}, u32[]{:S(2)}, u32[]{:S(2)}) collective-permute-start(bf16[8,2880]{1,0:T(8,128)(2,1)S(1)} %select.1.refs_0_), channel_id=1, source_target_pairs={{0,2},{1,3},{2,0},{3,1},{4,6},{5,7},{6,4},{7,5},{8,10},{9,11},{10,... | collective-permute-start | bytes 138248 | tf_op jit(solution)/shard_map/ppermute | solution.py:265
  6.5 0.2 collective-permute-done.refs_1_
  6.7 1.7 %collective-permute-done.1.refs_2_ = bf16[8,2880]{1,0:T(8,128)(2,1)S(1)} collective-permute-done((bf16[8,2880]{1,0:T(8,128)(2,1)S(1)}, bf16[8,2880]{1,0:T(8,128)(2,1)S(1)}, u32[]{:S(2)}, u32[]{:S(2)}) %collective-permute-start.1) | collective-permute-done | bytes 46112 | tf_op jit(solution)/shard_map/ppermute | solution.py:265
  8.4 1.6 %collective-permute-start.3 = (bf16[24,2880]{1,0:T(8,128)(2,1)S(1)}, bf16[24,2880]{1,0:T(8,128)(2,1)S(1)}, u32[]{:S(2)}, u32[]{:S(2)}) collective-permute-start(bf16[24,2880]{1,0:T(8,128)(2,1)S(1)} %join.1), channel_id=1, source_target_pairs={{0,1},{1,0},{2,3},{3,2},{4,5},{5,4},{6,7},{7,6},{8,9},{9,8},{10,11... | collective-permute-start | bytes 414728 | tf_op jit(solution)/shard_map/ppermute | solution.py:265
  9.9 1.9 %collective-permute-start.2 = (bf16[8,2880]{1,0:T(8,128)(2,1)S(1)}, bf16[8,2880]{1,0:T(8,128)(2,1)S(1)}, u32[]{:S(2)}, u32[]{:S(2)}) collective-permute-start(bf16[8,2880]{1,0:T(8,128)(2,1)S(1)} %select.1.refs_0_), channel_id=1, source_target_pairs={{0,6},{1,7},{2,4},{3,5},{4,2},{5,3},{6,0},{7,1},{8,14},{9,15},{10,... | collective-permute-start | bytes 138248 | tf_op jit(solution)/shard_map/ppermute | solution.py:265
  11.8 2.9 %collective-permute-done.2.refs_3_ = bf16[8,2880]{1,0:T(8,128)(2,1)S(1)} collective-permute-done((bf16[8,2880]{1,0:T(8,128)(2,1)S(1)}, bf16[8,2880]{1,0:T(8,128)(2,1)S(1)}, u32[]{:S(2)}, u32[]{:S(2)}) %collective-permute-start.2) | collective-permute-done | bytes 46112 | tf_op jit(solution)/shard_map/ppermute | solution.py:265
  14.6 0.1 collective-permute-start.4
  14.7 2.8 %collective-permute-done.4.refs_5_ = bf16[8,2880]{1,0:T(8,128)(2,1)S(1)} collective-permute-done((bf16[8,2880]{1,0:T(8,128)(2,1)S(1)}, bf16[8,2880]{1,0:T(8,128)(2,1)S(1)}, u32[]{:S(2)}, u32[]{:S(2)}) %collective-permute-start.4) | collective-permute-done | bytes 46112 | tf_op jit(solution)/shard_map/ppermute | solution.py:265
  17.6 0.0 collective-permute-done.3.refs_4_
  17.6 0.0 copy-done
  17.6 0.0 copy-done.1
  17.6 0.0 copy-done.2
  17.6 3.4 %expert_main.1 = (bf16[64,2880]{1,0:T(8,128)(2,1)S(1)}, bf16[64,360]{1,0:T(8,128)(2,1)S(1)}, bf16[64,360]{1,0:T(8,128)(2,1)S(1)}, bf16[64,360]{1,0:T(8,128)(2,1)...) custom-call(bf16[8,2880]{1,0:T(8,128)(2,1)S(1)} %select.1.refs_0_, ...), custom_call_target="tpu_custom_call" | custom-call | flops 663552000 | bytes 6220800 | tf_op jit(solution)/shard_map/expert_main/pallas_call | solution.py:183
  21.0 6.1 %collective-permute-start.5 = (bf16[16,3008]{1,0:T(8,128)(2,1)S(1)}, bf16[16,3008]{1,0:T(8,128)(2,1)S(1)}, u32[]{:S(2)}, u32[]{:S(2)}) collective-permute-start(bf16[16,3008]{1,0:T(8,128)(2,1)S(1)} %get-tuple-element.26), channel_id=1, source_target_pairs={{8,0},{9,1},{10,2},{11,3},{12,4},{13,5},{14,6},{15,7},{16,8},{17,9... | collective-permute-start | bytes 288776 | tf_op jit(solution)/shard_map/ppermute | solution.py:275
  27.1 1.9 %collective-permute-start.6 = (bf16[16,2880]{1,0:T(8,128)(2,1)S(1)}, bf16[16,2880]{1,0:T(8,128)(2,1)S(1)}, u32[]{:S(2)}, u32[]{:S(2)}) collective-permute-start(bf16[16,2880]{1,0:T(8,128)(2,1)S(1)} %get-tuple-element.27), channel_id=1, source_target_pairs={{8,1},{9,0},{10,3},{11,2},{12,5},{13,4},{14,7},{15,6},{16,9},{17,8... | collective-permute-start | bytes 276488 | tf_op jit(solution)/shard_map/ppermute | solution.py:275
  29.0 3.1 %weight_grads.1 = (bf16[360,2880]{1,0:T(8,128)(2,1)}, bf16[360,2880]{1,0:T(8,128)(2,1)}, bf16[360,2880]{1,0:T(8,128)(2,1)}) custom-call(bf16[64,360]{1,0:T(8,128)(2,1)S(1)} %get-tuple-element.19.refs_0_, bf16[64,360]{1,0:T(8,128)(2,1)S(1)} %get-tuple-element.20.refs_1_, bf16[64,360]{1,0:T(8,128)(2,1)S(1)} %get-tuple-element.21.refs_2_, ...), custom_call_target="tpu_custom_call" | custom-call | flops 398131200 | bytes 12441600 | tf_op jit(solution)/shard_map/weight_grads/pallas_call | solution.py:221
  32.1 0.0 collective-permute-done.5
  32.2 2.1 %collective-permute-done.6 = bf16[16,2880]{1,0:T(8,128)(2,1)S(1)} collective-permute-done((bf16[16,2880]{1,0:T(8,128)(2,1)S(1)}, bf16[16,2880]{1,0:T(8,128)(2,1)S(1)}, u32[]{:S(2)}, u32[]{:S(2)}) %collective-permute-start.6) | collective-permute-done | bytes 92192 | tf_op jit(solution)/shard_map/ppermute | solution.py:275
  34.4 0.1 collective-permute-start.7
  34.4 2.1 %collective-permute-start.8 = (bf16[4,2880]{1,0:T(4,128)(2,1)S(1)}, bf16[4,2880]{1,0:T(4,128)(2,1)S(1)}, u32[]{:S(2)}, u32[]{:S(2)}) collective-permute-start(bf16[4,2880]{1,0:T(4,128)(2,1)S(1)} %get-tuple-element.31), channel_id=1, source_target_pairs={{0,6},{1,7},{2,4},{3,5},{4,2},{5,3},{6,0},{7,1},{8,14},{9,15},{10,... | collective-permute-start | bytes 69128 | tf_op jit(solution)/shard_map/ppermute | solution.py:265
  36.5 0.5 %collective-permute-start.9 = (bf16[4,2880]{1,0:T(4,128)(2,1)S(1)}, bf16[4,2880]{1,0:T(4,128)(2,1)S(1)}, u32[]{:S(2)}, u32[]{:S(2)}) collective-permute-start(bf16[4,2880]{1,0:T(4,128)(2,1)S(1)} %get-tuple-element.30), channel_id=1, source_target_pairs={{0,2},{1,3},{2,0},{3,1},{4,6},{5,7},{6,4},{7,5},{8,10},{9,11},{10,... | collective-permute-start | bytes 69128 | tf_op jit(solution)/shard_map/ppermute | solution.py:265
  37.1 0.1 slice.26
  37.1 0.1 pad_maximum_fusion.kept_ref
  37.2 1.1 %collective-permute-done.7.refs_0_ = bf16[4,2880]{1,0:T(4,128)(2,1)S(1)} collective-permute-done((bf16[4,2880]{1,0:T(4,128)(2,1)S(1)}, bf16[4,2880]{1,0:T(4,128)(2,1)S(1)}, u32[]{:S(2)}, u32[]{:S(2)}) %collective-permute-start.7) | collective-permute-done | bytes 23072 | tf_op jit(solution)/shard_map/ppermute | solution.py:265
  38.3 0.7 %collective-permute-done.8.refs_1_ = bf16[4,2880]{1,0:T(4,128)(2,1)S(1)} collective-permute-done((bf16[4,2880]{1,0:T(4,128)(2,1)S(1)}, bf16[4,2880]{1,0:T(4,128)(2,1)S(1)}, u32[]{:S(2)}, u32[]{:S(2)}) %collective-permute-start.8) | collective-permute-done | bytes 23072 | tf_op jit(solution)/shard_map/ppermute | solution.py:265
  39.0 0.3 collective-permute-done.9.refs_2_
  39.2 1.1 %expand.1 = bf16[64,2880]{1,0:T(8,128)(2,1)} custom-call(f32[4,3008]{1,0:T(4,128)S(1)} %pad_maximum_fusion.kept_ref, bf16[4,2880]{1,0:T(4,128)(2,1)S(1)} %collective-permute-done.7.refs_0_, bf16[4,2880]{1,0:T(4,128)(2,1)S(1)} %collective-permute-done.8.refs_1_, bf16[4,2880]{1,0:T(4,128)(2,1)S(1)} %collective-permute-done.9.refs_2_), custom_call_target="tpu_custom_call" | custom-call | tf_op jit(solution)/shard_map/expand/pallas_call | solution.py:253
  (5 shorter events, 0.1 us)
Async XLA Ops:
  0.6 1.0 %copy-start.3 = (bf16[1,64,2880]{2,1,0:T(8,128)(2,1)S(1)}, bf16[1,64,2880]{2,1,0:T(8,128)(2,1)}, u32[]{:S(2)}) copy-start(bf16[1,64,2880]{2,1,0:T(8,128)(2,1)} %param.7) | copy-start | bytes 1105924
  0.6 1.1 %copy-start.4 = (bf16[1,64,2880]{2,1,0:T(8,128)(2,1)S(1)}, bf16[1,64,2880]{2,1,0:T(8,128)(2,1)}, u32[]{:S(2)}) copy-start(bf16[1,64,2880]{2,1,0:T(8,128)(2,1)} %param.8) | copy-start | bytes 1105924
  2.0 15.6 %copy-start = (bf16[1,360,2880]{2,1,0:T(8,128)(2,1)S(1)}, bf16[1,360,2880]{2,1,0:T(8,128)(2,1)}, u32[]{:S(2)}) copy-start(bf16[1,360,2880]{2,1,0:T(8,128)(2,1)} %param.11) | copy-start | bytes 6220804
  2.0 15.6 %copy-start.1 = (bf16[1,360,2880]{2,1,0:T(8,128)(2,1)S(1)}, bf16[1,360,2880]{2,1,0:T(8,128)(2,1)}, u32[]{:S(2)}) copy-start(bf16[1,360,2880]{2,1,0:T(8,128)(2,1)} %param.12) | copy-start | bytes 6220804
  2.0 15.5 %copy-start.2 = (bf16[1,360,2880]{2,1,0:T(8,128)(2,1)S(1)}, bf16[1,360,2880]{2,1,0:T(8,128)(2,1)}, u32[]{:S(2)}) copy-start(bf16[1,360,2880]{2,1,0:T(8,128)(2,1)} %param.13) | copy-start | bytes 6220804
  2.0 4.7 %collective-permute-start = (bf16[8,2880]{1,0:T(8,128)(2,1)S(1)}, bf16[8,2880]{1,0:T(8,128)(2,1)S(1)}, u32[]{:S(2)}, u32[]{:S(2)}) collective-permute-start(bf16[8,2880]{1,0:T(8,128)(2,1)S(1)} %select.1.refs_0_), channel_id=1, source_target_pairs={{0,4},{1,5},{2,6},{3,7},{4,0},{5,1},{6,2},{7,3},{8,12},{9,13},{10,... | collective-permute-start | bytes 138248 | tf_op jit(solution)/shard_map/ppermute | solution.py:265
  5.2 3.1 %collective-permute-start.1 = (bf16[8,2880]{1,0:T(8,128)(2,1)S(1)}, bf16[8,2880]{1,0:T(8,128)(2,1)S(1)}, u32[]{:S(2)}, u32[]{:S(2)}) collective-permute-start(bf16[8,2880]{1,0:T(8,128)(2,1)S(1)} %select.1.refs_0_), channel_id=1, source_target_pairs={{0,2},{1,3},{2,0},{3,1},{4,6},{5,7},{6,4},{7,5},{8,10},{9,11},{10,... | collective-permute-start | bytes 138248 | tf_op jit(solution)/shard_map/ppermute | solution.py:265
  8.4 9.2 %collective-permute-start.3 = (bf16[24,2880]{1,0:T(8,128)(2,1)S(1)}, bf16[24,2880]{1,0:T(8,128)(2,1)S(1)}, u32[]{:S(2)}, u32[]{:S(2)}) collective-permute-start(bf16[24,2880]{1,0:T(8,128)(2,1)S(1)} %join.1), channel_id=1, source_target_pairs={{0,1},{1,0},{2,3},{3,2},{4,5},{5,4},{6,7},{7,6},{8,9},{9,8},{10,11... | collective-permute-start | bytes 414728 | tf_op jit(solution)/shard_map/ppermute | solution.py:265
  9.9 4.7 %collective-permute-start.2 = (bf16[8,2880]{1,0:T(8,128)(2,1)S(1)}, bf16[8,2880]{1,0:T(8,128)(2,1)S(1)}, u32[]{:S(2)}, u32[]{:S(2)}) collective-permute-start(bf16[8,2880]{1,0:T(8,128)(2,1)S(1)} %select.1.refs_0_), channel_id=1, source_target_pairs={{0,6},{1,7},{2,4},{3,5},{4,2},{5,3},{6,0},{7,1},{8,14},{9,15},{10,... | collective-permute-start | bytes 138248 | tf_op jit(solution)/shard_map/ppermute | solution.py:265
  14.6 2.9 %collective-permute-start.4 = (bf16[8,2880]{1,0:T(8,128)(2,1)S(1)}, bf16[8,2880]{1,0:T(8,128)(2,1)S(1)}, u32[]{:S(2)}, u32[]{:S(2)}) collective-permute-start(bf16[8,2880]{1,0:T(8,128)(2,1)S(1)} %collective-permute-done.2.refs_3_), channel_id=1, source_target_pairs={{0,1},{1,0},{2,3},{3,2},{4,5},{5,4},{6,7},{7,6},{8,9},{9,8},{10,11... | collective-permute-start | bytes 138248 | tf_op jit(solution)/shard_map/ppermute | solution.py:265
  21.0 11.2 %collective-permute-start.5 = (bf16[16,3008]{1,0:T(8,128)(2,1)S(1)}, bf16[16,3008]{1,0:T(8,128)(2,1)S(1)}, u32[]{:S(2)}, u32[]{:S(2)}) collective-permute-start(bf16[16,3008]{1,0:T(8,128)(2,1)S(1)} %get-tuple-element.26), channel_id=1, source_target_pairs={{8,0},{9,1},{10,2},{11,3},{12,4},{13,5},{14,6},{15,7},{16,8},{17,9... | collective-permute-start | bytes 288776 | tf_op jit(solution)/shard_map/ppermute | solution.py:275
  27.1 7.2 %collective-permute-start.6 = (bf16[16,2880]{1,0:T(8,128)(2,1)S(1)}, bf16[16,2880]{1,0:T(8,128)(2,1)S(1)}, u32[]{:S(2)}, u32[]{:S(2)}) collective-permute-start(bf16[16,2880]{1,0:T(8,128)(2,1)S(1)} %get-tuple-element.27), channel_id=1, source_target_pairs={{8,1},{9,0},{10,3},{11,2},{12,5},{13,4},{14,7},{15,6},{16,9},{17,8... | collective-permute-start | bytes 276488 | tf_op jit(solution)/shard_map/ppermute | solution.py:275
  34.4 3.9 %collective-permute-start.7 = (bf16[4,2880]{1,0:T(4,128)(2,1)S(1)}, bf16[4,2880]{1,0:T(4,128)(2,1)S(1)}, u32[]{:S(2)}, u32[]{:S(2)}) collective-permute-start(bf16[4,2880]{1,0:T(4,128)(2,1)S(1)} %get-tuple-element.32), channel_id=1, source_target_pairs={{0,4},{1,5},{2,6},{3,7},{4,0},{5,1},{6,2},{7,3},{8,12},{9,13},{10,... | collective-permute-start | bytes 69128 | tf_op jit(solution)/shard_map/ppermute | solution.py:265
  34.4 4.5 %collective-permute-start.8 = (bf16[4,2880]{1,0:T(4,128)(2,1)S(1)}, bf16[4,2880]{1,0:T(4,128)(2,1)S(1)}, u32[]{:S(2)}, u32[]{:S(2)}) collective-permute-start(bf16[4,2880]{1,0:T(4,128)(2,1)S(1)} %get-tuple-element.31), channel_id=1, source_target_pairs={{0,6},{1,7},{2,4},{3,5},{4,2},{5,3},{6,0},{7,1},{8,14},{9,15},{10,... | collective-permute-start | bytes 69128 | tf_op jit(solution)/shard_map/ppermute | solution.py:265
  36.5 2.7 %collective-permute-start.9 = (bf16[4,2880]{1,0:T(4,128)(2,1)S(1)}, bf16[4,2880]{1,0:T(4,128)(2,1)S(1)}, u32[]{:S(2)}, u32[]{:S(2)}) collective-permute-start(bf16[4,2880]{1,0:T(4,128)(2,1)S(1)} %get-tuple-element.30), channel_id=1, source_target_pairs={{0,2},{1,3},{2,0},{3,1},{4,6},{5,7},{6,4},{7,5},{8,10},{9,11},{10,... | collective-permute-start | bytes 69128 | tf_op jit(solution)/shard_map/ppermute | solution.py:265

commit v5 on v4

--- a/solution.py
+++ b/solution.py
@@ -13,6 +13,8 @@
 PAIR = 2 * CAP
 LANES = 128
 CHUNK = 1024
+UNIT_CHUNK = 256
+WIDTH_CHUNK = 1536
 OUT = (4, 2, 6)
 HOME = (4, 6, 2)
 
@@ -126,45 +128,55 @@
         start += ref.shape[0]
     rows = all_ref[...]
     total = rows.shape[0]
-    pre_gate = contract_last(rows, gate_ref[...])
-    pre_up = contract_last(rows, up_ref[...])
-    hidden_grad = pltpu.roll(contract_last(rows, down_ref[...]), total - CAP, 0)
-    sigma = jax.nn.sigmoid(pre_gate)
-    silu_val = pre_gate * sigma
-    silu_grad = sigma * (1.0 + pre_gate * (1.0 - sigma))
-    first = lax.rem(lax.broadcasted_iota(jnp.int32, pre_gate.shape, 0), PAIR) < CAP
-    hidden = jnp.where(first, silu_val * pre_up, 0.0)
-    grad_gate = jnp.where(first, hidden_grad * pre_up * silu_grad, 0.0)
-    grad_up = jnp.where(first, hidden_grad * silu_val, 0.0)
-    gate_out[...] = grad_gate.astype(jnp.bfloat16)
-    up_out[...] = grad_up.astype(jnp.bfloat16)
-    hidden_out[...] = pltpu.roll(hidden, CAP, 0).astype(jnp.bfloat16)
 
     def packed(value):
-        blocks = total // PAIR
         moved = pltpu.roll(value, CAP, 0)
         return jnp.concatenate(
             [
                 value[2 * m * PAIR : (2 * m + 1) * PAIR]
                 + moved[(2 * m + 1) * PAIR : (2 * m + 2) * PAIR]
-                for m in range(blocks // 2)
+                for m in range(total // PAIR // 2)
             ],
             axis=0,
         ).astype(jnp.bfloat16)
 
-    partial = jnp.dot(packed(grad_gate), gate_ref[...], preferred_element_type=jnp.float32)
-    partial = partial + jnp.dot(
-        packed(grad_up), up_ref[...], preferred_element_type=jnp.float32
-    )
+    units, width = gate_ref.shape
+    lefts = []
+    for start in range(0, units, UNIT_CHUNK):
+        part = slice(start, min(start + UNIT_CHUNK, units))
+        pre_gate = contract_last(rows, gate_ref[part])
+        pre_up = contract_last(rows, up_ref[part])
+        hidden_grad = pltpu.roll(contract_last(rows, down_ref[part]), total - CAP, 0)
+        sigma = jax.nn.sigmoid(pre_gate)
+        silu_val = pre_gate * sigma
+        silu_grad = sigma * (1.0 + pre_gate * (1.0 - sigma))
+        first = lax.rem(lax.broadcasted_iota(jnp.int32, pre_gate.shape, 0), PAIR) < CAP
+        hidden = jnp.where(first, silu_val * pre_up, 0.0)
+        grad_gate = jnp.where(first, hidden_grad * pre_up * silu_grad, 0.0)
+        grad_up = jnp.where(first, hidden_grad * silu_val, 0.0)
+        gate_out[:, part] = grad_gate.astype(jnp.bfloat16)
+        up_out[:, part] = grad_up.astype(jnp.bfloat16)
+        hidden_out[:, part] = pltpu.roll(hidden, CAP, 0).astype(jnp.bfloat16)
+        lefts.append((part, packed(grad_gate), packed(grad_up)))
+    for start in range(0, width, WIDTH_CHUNK):
+        columns = slice(start, min(start + WIDTH_CHUNK, width))
+        partial = jnp.zeros((total // 2, columns.stop - start), jnp.float32)
+        for part, gate_rows, up_rows in lefts:
+            for left, weight_ref in ((gate_rows, gate_ref), (up_rows, up_ref)):
+                partial = partial + jnp.dot(
+                    left, weight_ref[part, columns], preferred_element_type=jnp.float32
+                )
+        partial = partial.astype(jnp.bfloat16)
+        if split:
+            half = total // 4
+            partial_refs[0][:, columns] = partial[:half]
+            partial_refs[1][:, columns] = partial[half:]
+        else:
+            partial_refs[0][:, columns] = partial
     if split:
-        half, width = partial.shape[0] // 2, partial.shape[1]
-        keep_ref, send_ref = partial_refs
-        send_ref[...] = partial[half:].astype(jnp.bfloat16)
-        keep_ref[:, :width] = partial[:half].astype(jnp.bfloat16)
+        keep_ref = partial_refs[0]
         keep_ref[:PAIR, width:] = slots_ref[...].astype(jnp.bfloat16)
         keep_ref[PAIR:, width:] = jnp.zeros((half - PAIR, LANES), jnp.bfloat16)
-    else:
-        partial_refs[0][...] = partial.astype(jnp.bfloat16)
 
 
 def expert_main(pieces, slots, weight_gate, weight_up, weight_down, split):

time: 40.5 us -> 39.8 us (0.983)
  Pallas kernels: 8.04 us -> 7.37 us
    pallas_call x1, Pallas kernels: 3.39 us -> 2.72 us  [expert_main(): pl.pallas_call(functools.partial(main_kernel, len(pieces), split), out_sh...]
where the time goes in v5:
time: 39.8 us; the launch traced here: 39.6 us
  starting transfers between devices  18.7 us (47%)
  waiting for transfers between devices  11.6 us (29%)
  Pallas kernels  7.37 us (19%)
  other arithmetic  0.89 us (2%)
  between operations  0.78 us (2%)
    ppermute x8, starting transfers between devices, swap(): return lax.ppermute(value, 'expert', [(i, i ^ bits) for i in range(peers)])  10.7 us
    ppermute x8, waiting for transfers between devices, swap(): return lax.ppermute(value, 'expert', [(i, i ^ bits) for i in range(peers)])  9.52 us
    ppermute x2, starting transfers between devices, shift_back(): return lax.ppermute(value, ('pipe', 'expert'), pairs)  8.03 us
    pallas_call x1, Pallas kernels, weight_grads(): pl.pallas_call(functools.partial(grad_kernel, count), out_shape=(jax.Shap...  3.12 us
    pallas_call x1, Pallas kernels, expert_main(): pl.pallas_call(functools.partial(main_kernel, len(pieces), split), out_sh...  2.72 us
    ppermute x2, waiting for transfers between devices, shift_back(): return lax.ppermute(value, ('pipe', 'expert'), pairs)  2.09 us
    pallas_call x1, Pallas kernels, expand(): pl.pallas_call(expand_kernel, out_shape=jax.ShapeDtypeStruct((tokens, wid...  1.09 us
  transfers between devices with their start and end apart: 10, of which 8 were waited for; matrix products, arithmetic and copies ran while one was open for 0% of the time, Pallas kernels for 8%

profile of v5, /device:TPU:1, one launch (start us, length us, event | category | flops | bytes accessed | tf_op | source)
XLA Modules:
  0.0 39.6 jit_solution(8653015540827248691)
XLA Ops:
  0.6 0.0 copy-start.3
  0.6 0.0 copy-start.4
  0.7 0.8 %select_bitcast_fusion.routes_ref = f32[1,4,64]{2,1,0:T(4,128)S(1)} fusion(f32[1,64,4]{1,2,0:T(4,128)} %param.10, s32[1,64,4]{1,2,0:T(4,128)} %param.9), kind=kLoop, calls=%fused_computation.2 | loop fusion | flops 512 | bytes 3072 | tf_op jit(solution)/shard_map/jit(_where)/select_n | solution.py:74
  1.4 0.2 route.1
  1.6 0.0 copy-done.3
  1.7 0.1 copy-done.4
  1.8 0.2 select.1.refs_0_
  2.0 0.0 copy-start
  2.0 0.0 copy-start.1
  2.0 0.0 copy-start.2
  2.0 3.2 %collective-permute-start = (bf16[8,2880]{1,0:T(8,128)(2,1)S(1)}, bf16[8,2880]{1,0:T(8,128)(2,1)S(1)}, u32[]{:S(2)}, u32[]{:S(2)}) collective-permute-start(bf16[8,2880]{1,0:T(8,128)(2,1)S(1)} %select.1.refs_0_), channel_id=1, source_target_pairs={{0,4},{1,5},{2,6},{3,7},{4,0},{5,1},{6,2},{7,3},{8,12},{9,13},{10,... | collective-permute-start | bytes 138248 | tf_op jit(solution)/shard_map/ppermute | solution.py:277
  5.2 1.3 %collective-permute-start.1 = (bf16[8,2880]{1,0:T(8,128)(2,1)S(1)}, bf16[8,2880]{1,0:T(8,128)(2,1)S(1)}, u32[]{:S(2)}, u32[]{:S(2)}) collective-permute-start(bf16[8,2880]{1,0:T(8,128)(2,1)S(1)} %select.1.refs_0_), channel_id=1, source_target_pairs={{0,2},{1,3},{2,0},{3,1},{4,6},{5,7},{6,4},{7,5},{8,10},{9,11},{10,... | collective-permute-start | bytes 138248 | tf_op jit(solution)/shard_map/ppermute | solution.py:277
  6.5 0.2 collective-permute-done.refs_1_
  6.7 1.7 %collective-permute-done.1.refs_2_ = bf16[8,2880]{1,0:T(8,128)(2,1)S(1)} collective-permute-done((bf16[8,2880]{1,0:T(8,128)(2,1)S(1)}, bf16[8,2880]{1,0:T(8,128)(2,1)S(1)}, u32[]{:S(2)}, u32[]{:S(2)}) %collective-permute-start.1) | collective-permute-done | bytes 46112 | tf_op jit(solution)/shard_map/ppermute | solution.py:277
  8.4 1.6 %collective-permute-start.3 = (bf16[24,2880]{1,0:T(8,128)(2,1)S(1)}, bf16[24,2880]{1,0:T(8,128)(2,1)S(1)}, u32[]{:S(2)}, u32[]{:S(2)}) collective-permute-start(bf16[24,2880]{1,0:T(8,128)(2,1)S(1)} %join.1), channel_id=1, source_target_pairs={{0,1},{1,0},{2,3},{3,2},{4,5},{5,4},{6,7},{7,6},{8,9},{9,8},{10,11... | collective-permute-start | bytes 414728 | tf_op jit(solution)/shard_map/ppermute | solution.py:277
  9.9 1.9 %collective-permute-start.2 = (bf16[8,2880]{1,0:T(8,128)(2,1)S(1)}, bf16[8,2880]{1,0:T(8,128)(2,1)S(1)}, u32[]{:S(2)}, u32[]{:S(2)}) collective-permute-start(bf16[8,2880]{1,0:T(8,128)(2,1)S(1)} %select.1.refs_0_), channel_id=1, source_target_pairs={{0,6},{1,7},{2,4},{3,5},{4,2},{5,3},{6,0},{7,1},{8,14},{9,15},{10,... | collective-permute-start | bytes 138248 | tf_op jit(solution)/shard_map/ppermute | solution.py:277
  11.8 2.9 %collective-permute-done.2.refs_3_ = bf16[8,2880]{1,0:T(8,128)(2,1)S(1)} collective-permute-done((bf16[8,2880]{1,0:T(8,128)(2,1)S(1)}, bf16[8,2880]{1,0:T(8,128)(2,1)S(1)}, u32[]{:S(2)}, u32[]{:S(2)}) %collective-permute-start.2) | collective-permute-done | bytes 46112 | tf_op jit(solution)/shard_map/ppermute | solution.py:277
  14.6 0.1 collective-permute-start.4
  14.7 2.8 %collective-permute-done.4.refs_5_ = bf16[8,2880]{1,0:T(8,128)(2,1)S(1)} collective-permute-done((bf16[8,2880]{1,0:T(8,128)(2,1)S(1)}, bf16[8,2880]{1,0:T(8,128)(2,1)S(1)}, u32[]{:S(2)}, u32[]{:S(2)}) %collective-permute-start.4) | collective-permute-done | bytes 46112 | tf_op jit(solution)/shard_map/ppermute | solution.py:277
  17.6 0.0 collective-permute-done.3.refs_4_
  17.6 0.0 copy-done
  17.6 0.0 copy-done.1
  17.6 0.0 copy-done.2
  17.6 2.7 %expert_main.1 = (bf16[64,2880]{1,0:T(8,128)(2,1)S(1)}, bf16[64,360]{1,0:T(8,128)(2,1)S(1)}, bf16[64,360]{1,0:T(8,128)(2,1)S(1)}, bf16[64,360]{1,0:T(8,128)(2,1)...) custom-call(bf16[8,2880]{1,0:T(8,128)(2,1)S(1)} %select.1.refs_0_, ...), custom_call_target="tpu_custom_call" | custom-call | flops 663552000 | bytes 6220800 | tf_op jit(solution)/shard_map/expert_main/pallas_call | solution.py:195
  20.3 6.1 %collective-permute-start.5 = (bf16[16,3008]{1,0:T(8,128)(2,1)S(1)}, bf16[16,3008]{1,0:T(8,128)(2,1)S(1)}, u32[]{:S(2)}, u32[]{:S(2)}) collective-permute-start(bf16[16,3008]{1,0:T(8,128)(2,1)S(1)} %get-tuple-element.26), channel_id=1, source_target_pairs={{8,0},{9,1},{10,2},{11,3},{12,4},{13,5},{14,6},{15,7},{16,8},{17,9... | collective-permute-start | bytes 288776 | tf_op jit(solution)/shard_map/ppermute | solution.py:287
  26.4 1.9 %collective-permute-start.6 = (bf16[16,2880]{1,0:T(8,128)(2,1)S(1)}, bf16[16,2880]{1,0:T(8,128)(2,1)S(1)}, u32[]{:S(2)}, u32[]{:S(2)}) collective-permute-start(bf16[16,2880]{1,0:T(8,128)(2,1)S(1)} %get-tuple-element.27), channel_id=1, source_target_pairs={{8,1},{9,0},{10,3},{11,2},{12,5},{13,4},{14,7},{15,6},{16,9},{17,8... | collective-permute-start | bytes 276488 | tf_op jit(solution)/shard_map/ppermute | solution.py:287
  28.3 3.1 %weight_grads.1 = (bf16[360,2880]{1,0:T(8,128)(2,1)}, bf16[360,2880]{1,0:T(8,128)(2,1)}, bf16[360,2880]{1,0:T(8,128)(2,1)}) custom-call(bf16[64,360]{1,0:T(8,128)(2,1)S(1)} %get-tuple-element.19.refs_0_, bf16[64,360]{1,0:T(8,128)(2,1)S(1)} %get-tuple-element.20.refs_1_, bf16[64,360]{1,0:T(8,128)(2,1)S(1)} %get-tuple-element.21.refs_2_, ...), custom_call_target="tpu_custom_call" | custom-call | flops 398131200 | bytes 12441600 | tf_op jit(solution)/shard_map/weight_grads/pallas_call | solution.py:233
  31.5 0.0 collective-permute-done.5
  31.5 2.1 %collective-permute-done.6 = bf16[16,2880]{1,0:T(8,128)(2,1)S(1)} collective-permute-done((bf16[16,2880]{1,0:T(8,128)(2,1)S(1)}, bf16[16,2880]{1,0:T(8,128)(2,1)S(1)}, u32[]{:S(2)}, u32[]{:S(2)}) %collective-permute-start.6) | collective-permute-done | bytes 92192 | tf_op jit(solution)/shard_map/ppermute | solution.py:287
  33.7 0.1 collective-permute-start.7
  33.8 2.1 %collective-permute-start.8 = (bf16[4,2880]{1,0:T(4,128)(2,1)S(1)}, bf16[4,2880]{1,0:T(4,128)(2,1)S(1)}, u32[]{:S(2)}, u32[]{:S(2)}) collective-permute-start(bf16[4,2880]{1,0:T(4,128)(2,1)S(1)} %get-tuple-element.31), channel_id=1, source_target_pairs={{0,6},{1,7},{2,4},{3,5},{4,2},{5,3},{6,0},{7,1},{8,14},{9,15},{10,... | collective-permute-start | bytes 69128 | tf_op jit(solution)/shard_map/ppermute | solution.py:277
  35.8 0.5 %collective-permute-start.9 = (bf16[4,2880]{1,0:T(4,128)(2,1)S(1)}, bf16[4,2880]{1,0:T(4,128)(2,1)S(1)}, u32[]{:S(2)}, u32[]{:S(2)}) collective-permute-start(bf16[4,2880]{1,0:T(4,128)(2,1)S(1)} %get-tuple-element.30), channel_id=1, source_target_pairs={{0,2},{1,3},{2,0},{3,1},{4,6},{5,7},{6,4},{7,5},{8,10},{9,11},{10,... | collective-permute-start | bytes 69128 | tf_op jit(solution)/shard_map/ppermute | solution.py:277
  36.4 0.1 slice.26
  36.5 0.1 pad_maximum_fusion.kept_ref
  36.5 1.1 %collective-permute-done.7.refs_0_ = bf16[4,2880]{1,0:T(4,128)(2,1)S(1)} collective-permute-done((bf16[4,2880]{1,0:T(4,128)(2,1)S(1)}, bf16[4,2880]{1,0:T(4,128)(2,1)S(1)}, u32[]{:S(2)}, u32[]{:S(2)}) %collective-permute-start.7) | collective-permute-done | bytes 23072 | tf_op jit(solution)/shard_map/ppermute | solution.py:277
  37.6 0.7 %collective-permute-done.8.refs_1_ = bf16[4,2880]{1,0:T(4,128)(2,1)S(1)} collective-permute-done((bf16[4,2880]{1,0:T(4,128)(2,1)S(1)}, bf16[4,2880]{1,0:T(4,128)(2,1)S(1)}, u32[]{:S(2)}, u32[]{:S(2)}) %collective-permute-start.8) | collective-permute-done | bytes 23072 | tf_op jit(solution)/shard_map/ppermute | solution.py:277
  38.3 0.3 collective-permute-done.9.refs_2_
  38.5 1.1 %expand.1 = bf16[64,2880]{1,0:T(8,128)(2,1)} custom-call(f32[4,3008]{1,0:T(4,128)S(1)} %pad_maximum_fusion.kept_ref, bf16[4,2880]{1,0:T(4,128)(2,1)S(1)} %collective-permute-done.7.refs_0_, bf16[4,2880]{1,0:T(4,128)(2,1)S(1)} %collective-permute-done.8.refs_1_, bf16[4,2880]{1,0:T(4,128)(2,1)S(1)} %collective-permute-done.9.refs_2_), custom_call_target="tpu_custom_call" | custom-call | tf_op jit(solution)/shard_map/expand/pallas_call | solution.py:265
  (5 shorter events, 0.1 us)
Async XLA Ops:
  0.6 1.0 %copy-start.3 = (bf16[1,64,2880]{2,1,0:T(8,128)(2,1)S(1)}, bf16[1,64,2880]{2,1,0:T(8,128)(2,1)}, u32[]{:S(2)}) copy-start(bf16[1,64,2880]{2,1,0:T(8,128)(2,1)} %param.7) | copy-start | bytes 1105924
  0.6 1.1 %copy-start.4 = (bf16[1,64,2880]{2,1,0:T(8,128)(2,1)S(1)}, bf16[1,64,2880]{2,1,0:T(8,128)(2,1)}, u32[]{:S(2)}) copy-start(bf16[1,64,2880]{2,1,0:T(8,128)(2,1)} %param.8) | copy-start | bytes 1105924
  2.0 15.6 %copy-start = (bf16[1,360,2880]{2,1,0:T(8,128)(2,1)S(1)}, bf16[1,360,2880]{2,1,0:T(8,128)(2,1)}, u32[]{:S(2)}) copy-start(bf16[1,360,2880]{2,1,0:T(8,128)(2,1)} %param.11) | copy-start | bytes 6220804
  2.0 15.6 %copy-start.1 = (bf16[1,360,2880]{2,1,0:T(8,128)(2,1)S(1)}, bf16[1,360,2880]{2,1,0:T(8,128)(2,1)}, u32[]{:S(2)}) copy-start(bf16[1,360,2880]{2,1,0:T(8,128)(2,1)} %param.12) | copy-start | bytes 6220804
  2.0 15.5 %copy-start.2 = (bf16[1,360,2880]{2,1,0:T(8,128)(2,1)S(1)}, bf16[1,360,2880]{2,1,0:T(8,128)(2,1)}, u32[]{:S(2)}) copy-start(bf16[1,360,2880]{2,1,0:T(8,128)(2,1)} %param.13) | copy-start | bytes 6220804
  2.0 4.7 %collective-permute-start = (bf16[8,2880]{1,0:T(8,128)(2,1)S(1)}, bf16[8,2880]{1,0:T(8,128)(2,1)S(1)}, u32[]{:S(2)}, u32[]{:S(2)}) collective-permute-start(bf16[8,2880]{1,0:T(8,128)(2,1)S(1)} %select.1.refs_0_), channel_id=1, source_target_pairs={{0,4},{1,5},{2,6},{3,7},{4,0},{5,1},{6,2},{7,3},{8,12},{9,13},{10,... | collective-permute-start | bytes 138248 | tf_op jit(solution)/shard_map/ppermute | solution.py:277
  5.2 3.1 %collective-permute-start.1 = (bf16[8,2880]{1,0:T(8,128)(2,1)S(1)}, bf16[8,2880]{1,0:T(8,128)(2,1)S(1)}, u32[]{:S(2)}, u32[]{:S(2)}) collective-permute-start(bf16[8,2880]{1,0:T(8,128)(2,1)S(1)} %select.1.refs_0_), channel_id=1, source_target_pairs={{0,2},{1,3},{2,0},{3,1},{4,6},{5,7},{6,4},{7,5},{8,10},{9,11},{10,... | collective-permute-start | bytes 138248 | tf_op jit(solution)/shard_map/ppermute | solution.py:277
  8.4 9.2 %collective-permute-start.3 = (bf16[24,2880]{1,0:T(8,128)(2,1)S(1)}, bf16[24,2880]{1,0:T(8,128)(2,1)S(1)}, u32[]{:S(2)}, u32[]{:S(2)}) collective-permute-start(bf16[24,2880]{1,0:T(8,128)(2,1)S(1)} %join.1), channel_id=1, source_target_pairs={{0,1},{1,0},{2,3},{3,2},{4,5},{5,4},{6,7},{7,6},{8,9},{9,8},{10,11... | collective-permute-start | bytes 414728 | tf_op jit(solution)/shard_map/ppermute | solution.py:277
  9.9 4.7 %collective-permute-start.2 = (bf16[8,2880]{1,0:T(8,128)(2,1)S(1)}, bf16[8,2880]{1,0:T(8,128)(2,1)S(1)}, u32[]{:S(2)}, u32[]{:S(2)}) collective-permute-start(bf16[8,2880]{1,0:T(8,128)(2,1)S(1)} %select.1.refs_0_), channel_id=1, source_target_pairs={{0,6},{1,7},{2,4},{3,5},{4,2},{5,3},{6,0},{7,1},{8,14},{9,15},{10,... | collective-permute-start | bytes 138248 | tf_op jit(solution)/shard_map/ppermute | solution.py:277
  14.6 2.9 %collective-permute-start.4 = (bf16[8,2880]{1,0:T(8,128)(2,1)S(1)}, bf16[8,2880]{1,0:T(8,128)(2,1)S(1)}, u32[]{:S(2)}, u32[]{:S(2)}) collective-permute-start(bf16[8,2880]{1,0:T(8,128)(2,1)S(1)} %collective-permute-done.2.refs_3_), channel_id=1, source_target_pairs={{0,1},{1,0},{2,3},{3,2},{4,5},{5,4},{6,7},{7,6},{8,9},{9,8},{10,11... | collective-permute-start | bytes 138248 | tf_op jit(solution)/shard_map/ppermute | solution.py:277
  20.3 11.2 %collective-permute-start.5 = (bf16[16,3008]{1,0:T(8,128)(2,1)S(1)}, bf16[16,3008]{1,0:T(8,128)(2,1)S(1)}, u32[]{:S(2)}, u32[]{:S(2)}) collective-permute-start(bf16[16,3008]{1,0:T(8,128)(2,1)S(1)} %get-tuple-element.26), channel_id=1, source_target_pairs={{8,0},{9,1},{10,2},{11,3},{12,4},{13,5},{14,6},{15,7},{16,8},{17,9... | collective-permute-start | bytes 288776 | tf_op jit(solution)/shard_map/ppermute | solution.py:287
  26.4 7.2 %collective-permute-start.6 = (bf16[16,2880]{1,0:T(8,128)(2,1)S(1)}, bf16[16,2880]{1,0:T(8,128)(2,1)S(1)}, u32[]{:S(2)}, u32[]{:S(2)}) collective-permute-start(bf16[16,2880]{1,0:T(8,128)(2,1)S(1)} %get-tuple-element.27), channel_id=1, source_target_pairs={{8,1},{9,0},{10,3},{11,2},{12,5},{13,4},{14,7},{15,6},{16,9},{17,8... | collective-permute-start | bytes 276488 | tf_op jit(solution)/shard_map/ppermute | solution.py:287
  33.7 3.9 %collective-permute-start.7 = (bf16[4,2880]{1,0:T(4,128)(2,1)S(1)}, bf16[4,2880]{1,0:T(4,128)(2,1)S(1)}, u32[]{:S(2)}, u32[]{:S(2)}) collective-permute-start(bf16[4,2880]{1,0:T(4,128)(2,1)S(1)} %get-tuple-element.32), channel_id=1, source_target_pairs={{0,4},{1,5},{2,6},{3,7},{4,0},{5,1},{6,2},{7,3},{8,12},{9,13},{10,... | collective-permute-start | bytes 69128 | tf_op jit(solution)/shard_map/ppermute | solution.py:277
  33.8 4.5 %collective-permute-start.8 = (bf16[4,2880]{1,0:T(4,128)(2,1)S(1)}, bf16[4,2880]{1,0:T(4,128)(2,1)S(1)}, u32[]{:S(2)}, u32[]{:S(2)}) collective-permute-start(bf16[4,2880]{1,0:T(4,128)(2,1)S(1)} %get-tuple-element.31), channel_id=1, source_target_pairs={{0,6},{1,7},{2,4},{3,5},{4,2},{5,3},{6,0},{7,1},{8,14},{9,15},{10,... | collective-permute-start | bytes 69128 | tf_op jit(solution)/shard_map/ppermute | solution.py:277
  35.8 2.7 %collective-permute-start.9 = (bf16[4,2880]{1,0:T(4,128)(2,1)S(1)}, bf16[4,2880]{1,0:T(4,128)(2,1)S(1)}, u32[]{:S(2)}, u32[]{:S(2)}) collective-permute-start(bf16[4,2880]{1,0:T(4,128)(2,1)S(1)} %get-tuple-element.30), channel_id=1, source_target_pairs={{0,2},{1,3},{2,0},{3,1},{4,6},{5,7},{6,4},{7,5},{8,10},{9,11},{10,... | collective-permute-start | bytes 69128 | tf_op jit(solution)/shard_map/ppermute | solution.py:277

commit v6 on v5

--- a/solution.py
+++ b/solution.py
@@ -288,10 +288,11 @@
 
 
 def one_expert(own, slots, weights, tokens, width):
-    first, second, third = (swap(own, bits) for bits in OUT)
-    across = [swap(join(own, first, second), 1)]
-    across.append(swap(third, 1))
-    pieces = (own, first, second, third, *across)
+    far = swap(own, 4)
+    across, along = swap(own, 1), swap(own, 2)
+    over = swap(join(own, far), 3)
+    along_far, across_far = swap(far, 2), swap(far, 1)
+    pieces = (own, far, along, along_far, across, across_far, over)
     rows, gate, up, hidden, keep, send = expert_main(pieces, slots, *weights, split=True)
     beside, kept = shift_back(send, 1), shift_back(keep, 0)
     grads = weight_grads(rows, gate, up, hidden)

time: 39.8 us -> 38.2 us (0.960)
  waiting for transfers between devices: 11.6 us -> 9.65 us
  starting transfers between devices: 18.7 us -> 19.1 us
    ppermute x8 -> x9, waiting for transfers between devices: 9.52 us -> 8.03 us  [swap(): return lax.ppermute(value, 'expert', [(i, i ^ bits) for i in range(peers)])]
    ppermute x8 -> x9, starting transfers between devices: 10.7 us -> 11.6 us  [swap(): return lax.ppermute(value, 'expert', [(i, i ^ bits) for i in range(peers)])]
    ppermute x2, starting transfers between devices: 8.03 us -> 7.44 us  [shift_back(): return lax.ppermute(value, ('pipe', 'expert'), pairs)]
    ppermute x2, waiting for transfers between devices: 2.09 us -> 1.61 us  [shift_back(): return lax.ppermute(value, ('pipe', 'expert'), pairs)]
  transfers between devices with their start and end apart: 10 -> 11, of which waited for: 8 -> 7; matrix products, arithmetic and copies ran while one was open for 0% -> 0% of each run, Pallas kernels for 8% -> 8%
where the time goes in v6:
time: 38.2 us; the launch traced here: 38 us
  starting transfers between devices  19.1 us (50%)
  waiting for transfers between devices  9.65 us (25%)
  Pallas kernels  7.37 us (19%)
  other arithmetic  0.89 us (2%)
  between operations  0.77 us (2%)
    ppermute x9, starting transfers between devices, swap(): return lax.ppermute(value, 'expert', [(i, i ^ bits) for i in range(peers)])  11.6 us
    ppermute x9, waiting for transfers between devices, swap(): return lax.ppermute(value, 'expert', [(i, i ^ bits) for i in range(peers)])  8.03 us
    ppermute x2, starting transfers between devices, shift_back(): return lax.ppermute(value, ('pipe', 'expert'), pairs)  7.44 us
    pallas_call x1, Pallas kernels, weight_grads(): pl.pallas_call(functools.partial(grad_kernel, count), out_shape=(jax.Shap...  3.13 us
    pallas_call x1, Pallas kernels, expert_main(): pl.pallas_call(functools.partial(main_kernel, len(pieces), split), out_sh...  2.71 us
    ppermute x2, waiting for transfers between devices, shift_back(): return lax.ppermute(value, ('pipe', 'expert'), pairs)  1.61 us
    pallas_call x1, Pallas kernels, expand(): pl.pallas_call(expand_kernel, out_shape=jax.ShapeDtypeStruct((tokens, wid...  1.1 us
    select_n x1, other arithmetic, select_rows(): routes = jnp.where(ids[None] == labels[:, None, None], probs[None], 0.0)  0.77 us
  transfers between devices with their start and end apart: 11, of which 7 were waited for; matrix products, arithmetic and copies ran while one was open for 0% of the time, Pallas kernels for 8%

profile of v6, /device:TPU:1, one launch (start us, length us, event | category | flops | bytes accessed | tf_op | source)
XLA Modules:
  0.0 38.0 jit_solution(2918917787039698174)
XLA Ops:
  0.6 0.0 copy-start.3
  0.6 0.0 copy-start.4
  0.7 0.8 %select_bitcast_fusion.routes_ref = f32[1,4,64]{2,1,0:T(4,128)S(1)} fusion(f32[1,64,4]{1,2,0:T(4,128)} %param.10, s32[1,64,4]{1,2,0:T(4,128)} %param.9), kind=kLoop, calls=%fused_computation.2 | loop fusion | flops 512 | bytes 3072 | tf_op jit(solution)/shard_map/jit(_where)/select_n | solution.py:74
  1.4 0.2 route.1
  1.6 0.0 copy-done.3
  1.7 0.1 copy-done.4
  1.8 0.2 select.1.refs_0_
  2.0 0.0 copy-start
  2.0 0.0 copy-start.1
  2.0 0.0 copy-start.2
  2.0 3.2 %collective-permute-start = (bf16[8,2880]{1,0:T(8,128)(2,1)S(1)}, bf16[8,2880]{1,0:T(8,128)(2,1)S(1)}, u32[]{:S(2)}, u32[]{:S(2)}) collective-permute-start(bf16[8,2880]{1,0:T(8,128)(2,1)S(1)} %select.1.refs_0_), channel_id=1, source_target_pairs={{0,4},{1,5},{2,6},{3,7},{4,0},{5,1},{6,2},{7,3},{8,12},{9,13},{10,... | collective-permute-start | bytes 138248 | tf_op jit(solution)/shard_map/ppermute | solution.py:277
  5.2 1.5 %collective-permute-done.refs_1_ = bf16[8,2880]{1,0:T(8,128)(2,1)S(1)} collective-permute-done((bf16[8,2880]{1,0:T(8,128)(2,1)S(1)}, bf16[8,2880]{1,0:T(8,128)(2,1)S(1)}, u32[]{:S(2)}, u32[]{:S(2)}) %collective-permute-start) | collective-permute-done | bytes 46112 | tf_op jit(solution)/shard_map/ppermute | solution.py:277
  6.7 2.4 %collective-permute-start.5 = (bf16[16,2880]{1,0:T(8,128)(2,1)S(1)}, bf16[16,2880]{1,0:T(8,128)(2,1)S(1)}, u32[]{:S(2)}, u32[]{:S(2)}) collective-permute-start(bf16[16,2880]{1,0:T(8,128)(2,1)S(1)} %join.1), channel_id=1, source_target_pairs={{0,3},{1,2},{2,1},{3,0},{4,7},{5,6},{6,5},{7,4},{8,11},{9,10},{10,... | collective-permute-start | bytes 276488 | tf_op jit(solution)/shard_map/ppermute | solution.py:277
  9.1 0.1 collective-permute-start.1
  9.2 0.2 collective-permute-start.3
  9.4 1.4 %collective-permute-start.2 = (bf16[8,2880]{1,0:T(8,128)(2,1)S(1)}, bf16[8,2880]{1,0:T(8,128)(2,1)S(1)}, u32[]{:S(2)}, u32[]{:S(2)}) collective-permute-start(bf16[8,2880]{1,0:T(8,128)(2,1)S(1)} %collective-permute-done.refs_1_), channel_id=1, source_target_pairs={{0,2},{1,3},{2,0},{3,1},{4,6},{5,7},{6,4},{7,5},{8,10},{9,11},{10,... | collective-permute-start | bytes 138248 | tf_op jit(solution)/shard_map/ppermute | solution.py:277
  10.9 1.1 %collective-permute-start.4 = (bf16[8,2880]{1,0:T(8,128)(2,1)S(1)}, bf16[8,2880]{1,0:T(8,128)(2,1)S(1)}, u32[]{:S(2)}, u32[]{:S(2)}) collective-permute-start(bf16[8,2880]{1,0:T(8,128)(2,1)S(1)} %collective-permute-done.refs_1_), channel_id=1, source_target_pairs={{0,1},{1,0},{2,3},{3,2},{4,5},{5,4},{6,7},{7,6},{8,9},{9,8},{10,11... | collective-permute-start | bytes 138248 | tf_op jit(solution)/shard_map/ppermute | solution.py:277
  12.0 0.0 collective-permute-done.1.refs_2_
  12.0 0.1 collective-permute-done.3.refs_4_
  12.1 0.4 collective-permute-done.2.refs_3_
  12.5 2.1 %collective-permute-done.4.refs_5_ = bf16[8,2880]{1,0:T(8,128)(2,1)S(1)} collective-permute-done((bf16[8,2880]{1,0:T(8,128)(2,1)S(1)}, bf16[8,2880]{1,0:T(8,128)(2,1)S(1)}, u32[]{:S(2)}, u32[]{:S(2)}) %collective-permute-start.4) | collective-permute-done | bytes 46112 | tf_op jit(solution)/shard_map/ppermute | solution.py:277
  14.6 0.0 collective-permute-done.5.refs_6_
  14.6 0.0 copy-done
  14.6 0.0 copy-done.1
  14.6 0.0 copy-done.2
  14.6 2.7 %expert_main.1 = (bf16[64,2880]{1,0:T(8,128)(2,1)S(1)}, bf16[64,360]{1,0:T(8,128)(2,1)S(1)}, bf16[64,360]{1,0:T(8,128)(2,1)S(1)}, bf16[64,360]{1,0:T(8,128)(2,1)...) custom-call(bf16[8,2880]{1,0:T(8,128)(2,1)S(1)} %select.1.refs_0_, ...), custom_call_target="tpu_custom_call" | custom-call | flops 663552000 | bytes 6220800 | tf_op jit(solution)/shard_map/expert_main/pallas_call | solution.py:195
  17.4 5.0 %collective-permute-start.6 = (bf16[16,3008]{1,0:T(8,128)(2,1)S(1)}, bf16[16,3008]{1,0:T(8,128)(2,1)S(1)}, u32[]{:S(2)}, u32[]{:S(2)}) collective-permute-start(bf16[16,3008]{1,0:T(8,128)(2,1)S(1)} %get-tuple-element.26), channel_id=1, source_target_pairs={{8,0},{9,1},{10,2},{11,3},{12,4},{13,5},{14,6},{15,7},{16,8},{17,9... | collective-permute-start | bytes 288776 | tf_op jit(solution)/shard_map/ppermute | solution.py:287
  22.4 2.4 %collective-permute-start.7 = (bf16[16,2880]{1,0:T(8,128)(2,1)S(1)}, bf16[16,2880]{1,0:T(8,128)(2,1)S(1)}, u32[]{:S(2)}, u32[]{:S(2)}) collective-permute-start(bf16[16,2880]{1,0:T(8,128)(2,1)S(1)} %get-tuple-element.27), channel_id=1, source_target_pairs={{8,1},{9,0},{10,3},{11,2},{12,5},{13,4},{14,7},{15,6},{16,9},{17,8... | collective-permute-start | bytes 276488 | tf_op jit(solution)/shard_map/ppermute | solution.py:287
  24.8 3.1 %weight_grads.1 = (bf16[360,2880]{1,0:T(8,128)(2,1)}, bf16[360,2880]{1,0:T(8,128)(2,1)}, bf16[360,2880]{1,0:T(8,128)(2,1)}) custom-call(bf16[64,360]{1,0:T(8,128)(2,1)S(1)} %get-tuple-element.19.refs_0_, bf16[64,360]{1,0:T(8,128)(2,1)S(1)} %get-tuple-element.20.refs_1_, bf16[64,360]{1,0:T(8,128)(2,1)S(1)} %get-tuple-element.21.refs_2_, ...), custom_call_target="tpu_custom_call" | custom-call | flops 398131200 | bytes 12441600 | tf_op jit(solution)/shard_map/weight_grads/pallas_call | solution.py:233
  28.0 0.0 collective-permute-done.6
  28.0 1.6 %collective-permute-done.7 = bf16[16,2880]{1,0:T(8,128)(2,1)S(1)} collective-permute-done((bf16[16,2880]{1,0:T(8,128)(2,1)S(1)}, bf16[16,2880]{1,0:T(8,128)(2,1)S(1)}, u32[]{:S(2)}, u32[]{:S(2)}) %collective-permute-start.7) | collective-permute-done | bytes 92192 | tf_op jit(solution)/shard_map/ppermute | solution.py:287
  29.7 2.8 %collective-permute-start.8 = (bf16[4,2880]{1,0:T(4,128)(2,1)S(1)}, bf16[4,2880]{1,0:T(4,128)(2,1)S(1)}, u32[]{:S(2)}, u32[]{:S(2)}) collective-permute-start(bf16[4,2880]{1,0:T(4,128)(2,1)S(1)} %get-tuple-element.32), channel_id=1, source_target_pairs={{0,4},{1,5},{2,6},{3,7},{4,0},{5,1},{6,2},{7,3},{8,12},{9,13},{10,... | collective-permute-start | bytes 69128 | tf_op jit(solution)/shard_map/ppermute | solution.py:277
  32.5 0.0 collective-permute-start.9
  32.5 0.4 collective-permute-start.10
  32.8 0.1 slice.26
  32.9 0.1 pad_maximum_fusion.kept_ref
  33.0 1.0 %collective-permute-done.8.refs_0_ = bf16[4,2880]{1,0:T(4,128)(2,1)S(1)} collective-permute-done((bf16[4,2880]{1,0:T(4,128)(2,1)S(1)}, bf16[4,2880]{1,0:T(4,128)(2,1)S(1)}, u32[]{:S(2)}, u32[]{:S(2)}) %collective-permute-start.8) | collective-permute-done | bytes 23072 | tf_op jit(solution)/shard_map/ppermute | solution.py:277
  33.9 3.0 %collective-permute-done.9.refs_1_ = bf16[4,2880]{1,0:T(4,128)(2,1)S(1)} collective-permute-done((bf16[4,2880]{1,0:T(4,128)(2,1)S(1)}, bf16[4,2880]{1,0:T(4,128)(2,1)S(1)}, u32[]{:S(2)}, u32[]{:S(2)}) %collective-permute-start.9) | collective-permute-done | bytes 23072 | tf_op jit(solution)/shard_map/ppermute | solution.py:277
  36.9 0.0 collective-permute-done.10.refs_2_
  36.9 1.1 %expand.1 = bf16[64,2880]{1,0:T(8,128)(2,1)} custom-call(f32[4,3008]{1,0:T(4,128)S(1)} %pad_maximum_fusion.kept_ref, bf16[4,2880]{1,0:T(4,128)(2,1)S(1)} %collective-permute-done.8.refs_0_, bf16[4,2880]{1,0:T(4,128)(2,1)S(1)} %collective-permute-done.9.refs_1_, bf16[4,2880]{1,0:T(4,128)(2,1)S(1)} %collective-permute-done.10.refs_2_), custom_call_target="tpu_custom_call" | custom-call | tf_op jit(solution)/shard_map/expand/pallas_call | solution.py:265
  (5 shorter events, 0.1 us)
Async XLA Ops:
  0.6 1.0 %copy-start.3 = (bf16[1,64,2880]{2,1,0:T(8,128)(2,1)S(1)}, bf16[1,64,2880]{2,1,0:T(8,128)(2,1)}, u32[]{:S(2)}) copy-start(bf16[1,64,2880]{2,1,0:T(8,128)(2,1)} %param.7) | copy-start | bytes 1105924
  0.6 1.1 %copy-start.4 = (bf16[1,64,2880]{2,1,0:T(8,128)(2,1)S(1)}, bf16[1,64,2880]{2,1,0:T(8,128)(2,1)}, u32[]{:S(2)}) copy-start(bf16[1,64,2880]{2,1,0:T(8,128)(2,1)} %param.8) | copy-start | bytes 1105924
  2.0 12.6 %copy-start = (bf16[1,360,2880]{2,1,0:T(8,128)(2,1)S(1)}, bf16[1,360,2880]{2,1,0:T(8,128)(2,1)}, u32[]{:S(2)}) copy-start(bf16[1,360,2880]{2,1,0:T(8,128)(2,1)} %param.11) | copy-start | bytes 6220804
  2.0 12.6 %copy-start.1 = (bf16[1,360,2880]{2,1,0:T(8,128)(2,1)S(1)}, bf16[1,360,2880]{2,1,0:T(8,128)(2,1)}, u32[]{:S(2)}) copy-start(bf16[1,360,2880]{2,1,0:T(8,128)(2,1)} %param.12) | copy-start | bytes 6220804
  2.0 12.6 %copy-start.2 = (bf16[1,360,2880]{2,1,0:T(8,128)(2,1)S(1)}, bf16[1,360,2880]{2,1,0:T(8,128)(2,1)}, u32[]{:S(2)}) copy-start(bf16[1,360,2880]{2,1,0:T(8,128)(2,1)} %param.13) | copy-start | bytes 6220804
  2.0 4.7 %collective-permute-start = (bf16[8,2880]{1,0:T(8,128)(2,1)S(1)}, bf16[8,2880]{1,0:T(8,128)(2,1)S(1)}, u32[]{:S(2)}, u32[]{:S(2)}) collective-permute-start(bf16[8,2880]{1,0:T(8,128)(2,1)S(1)} %select.1.refs_0_), channel_id=1, source_target_pairs={{0,4},{1,5},{2,6},{3,7},{4,0},{5,1},{6,2},{7,3},{8,12},{9,13},{10,... | collective-permute-start | bytes 138248 | tf_op jit(solution)/shard_map/ppermute | solution.py:277
  6.7 7.9 %collective-permute-start.5 = (bf16[16,2880]{1,0:T(8,128)(2,1)S(1)}, bf16[16,2880]{1,0:T(8,128)(2,1)S(1)}, u32[]{:S(2)}, u32[]{:S(2)}) collective-permute-start(bf16[16,2880]{1,0:T(8,128)(2,1)S(1)} %join.1), channel_id=1, source_target_pairs={{0,3},{1,2},{2,1},{3,0},{4,7},{5,6},{6,5},{7,4},{8,11},{9,10},{10,... | collective-permute-start | bytes 276488 | tf_op jit(solution)/shard_map/ppermute | solution.py:277
  9.1 2.9 %collective-permute-start.1 = (bf16[8,2880]{1,0:T(8,128)(2,1)S(1)}, bf16[8,2880]{1,0:T(8,128)(2,1)S(1)}, u32[]{:S(2)}, u32[]{:S(2)}) collective-permute-start(bf16[8,2880]{1,0:T(8,128)(2,1)S(1)} %select.1.refs_0_), channel_id=1, source_target_pairs={{0,2},{1,3},{2,0},{3,1},{4,6},{5,7},{6,4},{7,5},{8,10},{9,11},{10,... | collective-permute-start | bytes 138248 | tf_op jit(solution)/shard_map/ppermute | solution.py:277
  9.2 2.9 %collective-permute-start.3 = (bf16[8,2880]{1,0:T(8,128)(2,1)S(1)}, bf16[8,2880]{1,0:T(8,128)(2,1)S(1)}, u32[]{:S(2)}, u32[]{:S(2)}) collective-permute-start(bf16[8,2880]{1,0:T(8,128)(2,1)S(1)} %select.1.refs_0_), channel_id=1, source_target_pairs={{0,1},{1,0},{2,3},{3,2},{4,5},{5,4},{6,7},{7,6},{8,9},{9,8},{10,11... | collective-permute-start | bytes 138248 | tf_op jit(solution)/shard_map/ppermute | solution.py:277
  9.4 3.1 %collective-permute-start.2 = (bf16[8,2880]{1,0:T(8,128)(2,1)S(1)}, bf16[8,2880]{1,0:T(8,128)(2,1)S(1)}, u32[]{:S(2)}, u32[]{:S(2)}) collective-permute-start(bf16[8,2880]{1,0:T(8,128)(2,1)S(1)} %collective-permute-done.refs_1_), channel_id=1, source_target_pairs={{0,2},{1,3},{2,0},{3,1},{4,6},{5,7},{6,4},{7,5},{8,10},{9,11},{10,... | collective-permute-start | bytes 138248 | tf_op jit(solution)/shard_map/ppermute | solution.py:277
  10.9 3.8 %collective-permute-start.4 = (bf16[8,2880]{1,0:T(8,128)(2,1)S(1)}, bf16[8,2880]{1,0:T(8,128)(2,1)S(1)}, u32[]{:S(2)}, u32[]{:S(2)}) collective-permute-start(bf16[8,2880]{1,0:T(8,128)(2,1)S(1)} %collective-permute-done.refs_1_), channel_id=1, source_target_pairs={{0,1},{1,0},{2,3},{3,2},{4,5},{5,4},{6,7},{7,6},{8,9},{9,8},{10,11... | collective-permute-start | bytes 138248 | tf_op jit(solution)/shard_map/ppermute | solution.py:277
  17.4 10.6 %collective-permute-start.6 = (bf16[16,3008]{1,0:T(8,128)(2,1)S(1)}, bf16[16,3008]{1,0:T(8,128)(2,1)S(1)}, u32[]{:S(2)}, u32[]{:S(2)}) collective-permute-start(bf16[16,3008]{1,0:T(8,128)(2,1)S(1)} %get-tuple-element.26), channel_id=1, source_target_pairs={{8,0},{9,1},{10,2},{11,3},{12,4},{13,5},{14,6},{15,7},{16,8},{17,9... | collective-permute-start | bytes 288776 | tf_op jit(solution)/shard_map/ppermute | solution.py:287
  22.4 7.2 %collective-permute-start.7 = (bf16[16,2880]{1,0:T(8,128)(2,1)S(1)}, bf16[16,2880]{1,0:T(8,128)(2,1)S(1)}, u32[]{:S(2)}, u32[]{:S(2)}) collective-permute-start(bf16[16,2880]{1,0:T(8,128)(2,1)S(1)} %get-tuple-element.27), channel_id=1, source_target_pairs={{8,1},{9,0},{10,3},{11,2},{12,5},{13,4},{14,7},{15,6},{16,9},{17,8... | collective-permute-start | bytes 276488 | tf_op jit(solution)/shard_map/ppermute | solution.py:287
  29.7 4.3 %collective-permute-start.8 = (bf16[4,2880]{1,0:T(4,128)(2,1)S(1)}, bf16[4,2880]{1,0:T(4,128)(2,1)S(1)}, u32[]{:S(2)}, u32[]{:S(2)}) collective-permute-start(bf16[4,2880]{1,0:T(4,128)(2,1)S(1)} %get-tuple-element.32), channel_id=1, source_target_pairs={{0,4},{1,5},{2,6},{3,7},{4,0},{5,1},{6,2},{7,3},{8,12},{9,13},{10,... | collective-permute-start | bytes 69128 | tf_op jit(solution)/shard_map/ppermute | solution.py:277
  32.5 4.5 %collective-permute-start.9 = (bf16[4,2880]{1,0:T(4,128)(2,1)S(1)}, bf16[4,2880]{1,0:T(4,128)(2,1)S(1)}, u32[]{:S(2)}, u32[]{:S(2)}) collective-permute-start(bf16[4,2880]{1,0:T(4,128)(2,1)S(1)} %get-tuple-element.31), channel_id=1, source_target_pairs={{0,6},{1,7},{2,4},{3,5},{4,2},{5,3},{6,0},{7,1},{8,14},{9,15},{10,... | collective-permute-start | bytes 69128 | tf_op jit(solution)/shard_map/ppermute | solution.py:277
  32.5 4.5 %collective-permute-start.10 = (bf16[4,2880]{1,0:T(4,128)(2,1)S(1)}, bf16[4,2880]{1,0:T(4,128)(2,1)S(1)}, u32[]{:S(2)}, u32[]{:S(2)}) collective-permute-start(bf16[4,2880]{1,0:T(4,128)(2,1)S(1)} %get-tuple-element.30), channel_id=1, source_target_pairs={{0,2},{1,3},{2,0},{3,1},{4,6},{5,7},{6,4},{7,5},{8,10},{9,11},{10,... | collective-permute-start | bytes 69128 | tf_op jit(solution)/shard_map/ppermute | solution.py:277

commit v7 on v6

--- a/solution.py
+++ b/solution.py
@@ -12,7 +12,8 @@
 CAP = 4
 PAIR = 2 * CAP
 LANES = 128
-CHUNK = 1024
+CHUNK = 512
+EXPAND_CHUNK = 1024
 UNIT_CHUNK = 256
 WIDTH_CHUNK = 1536
 OUT = (4, 2, 6)
@@ -250,15 +251,26 @@
 
 
 def expand_kernel(kept_ref, *refs):
-    homes, out_ref = refs[:-1], refs[-1]
+    homes, (out_ref, held_ref, sems) = refs[:-3], refs[-3:]
     tokens, width = out_ref.shape
-    combined = kept_ref[:, :width]
-    for home in homes:
-        combined = combined + home[...].astype(jnp.float32)
     numbers = kept_ref[:, width : width + 1]
     column = lax.broadcasted_iota(jnp.int32, (CAP, tokens), 1).astype(jnp.float32)
     chooser = jnp.where(column == numbers, 1.0, 0.0).astype(jnp.bfloat16)
-    out_ref[...] = contract_first(chooser, combined.astype(jnp.bfloat16)).astype(jnp.bfloat16)
+    copies = []
+    for c, start in enumerate(range(0, width, EXPAND_CHUNK)):
+        part = pl.ds(start, min(EXPAND_CHUNK, width - start))
+        combined = kept_ref[:, part]
+        for home in homes:
+            combined = combined + home[:, part].astype(jnp.float32)
+        held_ref[:, part] = contract_first(chooser, combined.astype(jnp.bfloat16)).astype(
+            jnp.bfloat16
+        )
+        copies.append(
+            pltpu.make_async_copy(held_ref.at[:, part], out_ref.at[:, part], sems.at[c])
+        )
+        copies[-1].start()
+    for copy in copies:
+        copy.wait()
 
 
 def expand(kept, homes, tokens, width):
@@ -266,7 +278,11 @@
         expand_kernel,
         out_shape=jax.ShapeDtypeStruct((tokens, width), jnp.bfloat16),
         in_specs=[VMEM] * (len(homes) + 1),
-        out_specs=VMEM,
+        out_specs=HBM,
+        scratch_shapes=[
+            pltpu.VMEM((tokens, width), jnp.bfloat16),
+            pltpu.SemaphoreType.DMA((pl.cdiv(width, EXPAND_CHUNK),)),
+        ],
         compiler_params=pltpu.CompilerParams(vmem_limit_bytes=8 << 20),
         name="expand",
     )(kept, *homes)
@@ -295,7 +311,8 @@
     pieces = (own, far, along, along_far, across, across_far, over)
     rows, gate, up, hidden, keep, send = expert_main(pieces, slots, *weights, split=True)
     beside, kept = shift_back(send, 1), shift_back(keep, 0)
-    grads = weight_grads(rows, gate, up, hidden)
+    grads = weight_grads(rows, gate, up)
+    grads += weight_grads(rows, hidden)
     kept = kept.astype(jnp.float32)
     summed = kept[:, :width] + beside.astype(jnp.float32)
     rounded = summed.astype(jnp.bfloat16)

time: 38.2 us -> 38.5 us (level)
  waiting for transfers between devices: 9.65 us -> 8.73 us
  Pallas kernels: 7.37 us -> 8.23 us
    ppermute x2, waiting for transfers between devices: 1.61 us -> 0.7 us  [shift_back(): return lax.ppermute(value, ('pipe', 'expert'), pairs)]
    pallas_call x1 -> x2, Pallas kernels: 3.13 us -> 4.04 us  [weight_grads(): pl.pallas_call(functools.partial(grad_kernel, count), out_shape=(jax.Shap...]
  transfers between devices with their start and end apart: 11 -> 11, of which waited for: 7 -> 7; matrix products, arithmetic and copies ran while one was open for 0% -> 0% of each run, Pallas kernels for 8% -> 11%
where the time goes in v7:
time: 38.5 us; the launch traced here: 38 us
  starting transfers between devices  19.1 us (50%)
  waiting for transfers between devices  8.73 us (23%)
  Pallas kernels  8.23 us (21%)
  other arithmetic  0.89 us (2%)
  between operations  0.78 us (2%)
    ppermute x9, starting transfers between devices, swap(): return lax.ppermute(value, 'expert', [(i, i ^ bits) for i in range(peers)])  11.6 us
    ppermute x9, waiting for transfers between devices, swap(): return lax.ppermute(value, 'expert', [(i, i ^ bits) for i in range(peers)])  8.03 us
    ppermute x2, starting transfers between devices, shift_back(): return lax.ppermute(value, ('pipe', 'expert'), pairs)  7.44 us
    pallas_call x2, Pallas kernels, weight_grads(): pl.pallas_call(functools.partial(grad_kernel, count), out_shape=(jax.Shap...  4.04 us
    pallas_call x1, Pallas kernels, expert_main(): pl.pallas_call(functools.partial(main_kernel, len(pieces), split), out_sh...  2.71 us
    pallas_call x1, Pallas kernels, expand(): pl.pallas_call(expand_kernel, out_shape=jax.ShapeDtypeStruct((tokens, wid...  1.05 us
    select_n x1, other arithmetic, select_rows(): routes = jnp.where(ids[None] == labels[:, None, None], probs[None], 0.0)  0.77 us
  transfers between devices with their start and end apart: 11, of which 7 were waited for; matrix products, arithmetic and copies ran while one was open for 0% of the time, Pallas kernels for 11%

profile of v7, /device:TPU:1, one launch (start us, length us, event | category | flops | bytes accessed | tf_op | source)
XLA Modules:
  0.0 38.0 jit_solution(899023078075981846)
XLA Ops:
  0.6 0.0 copy-start.3
  0.6 0.0 copy-start.4
  0.7 0.8 %select_bitcast_fusion.routes_ref = f32[1,4,64]{2,1,0:T(4,128)S(1)} fusion(f32[1,64,4]{1,2,0:T(4,128)} %param.10, s32[1,64,4]{1,2,0:T(4,128)} %param.9), kind=kLoop, calls=%fused_computation.2 | loop fusion | flops 512 | bytes 3072 | tf_op jit(solution)/shard_map/jit(_where)/select_n | solution.py:75
  1.4 0.2 route.1
  1.6 0.0 copy-done.3
  1.7 0.1 copy-done.4
  1.8 0.2 select.1.refs_0_
  2.0 0.0 copy-start
  2.0 0.0 copy-start.1
  2.0 0.0 copy-start.2
  2.0 3.2 %collective-permute-start = (bf16[8,2880]{1,0:T(8,128)(2,1)S(1)}, bf16[8,2880]{1,0:T(8,128)(2,1)S(1)}, u32[]{:S(2)}, u32[]{:S(2)}) collective-permute-start(bf16[8,2880]{1,0:T(8,128)(2,1)S(1)} %select.1.refs_0_), channel_id=1, source_target_pairs={{0,4},{1,5},{2,6},{3,7},{4,0},{5,1},{6,2},{7,3},{8,12},{9,13},{10,... | collective-permute-start | bytes 138248 | tf_op jit(solution)/shard_map/ppermute | solution.py:293
  5.2 1.5 %collective-permute-done.refs_1_ = bf16[8,2880]{1,0:T(8,128)(2,1)S(1)} collective-permute-done((bf16[8,2880]{1,0:T(8,128)(2,1)S(1)}, bf16[8,2880]{1,0:T(8,128)(2,1)S(1)}, u32[]{:S(2)}, u32[]{:S(2)}) %collective-permute-start) | collective-permute-done | bytes 46112 | tf_op jit(solution)/shard_map/ppermute | solution.py:293
  6.7 2.4 %collective-permute-start.5 = (bf16[16,2880]{1,0:T(8,128)(2,1)S(1)}, bf16[16,2880]{1,0:T(8,128)(2,1)S(1)}, u32[]{:S(2)}, u32[]{:S(2)}) collective-permute-start(bf16[16,2880]{1,0:T(8,128)(2,1)S(1)} %join.1), channel_id=1, source_target_pairs={{0,3},{1,2},{2,1},{3,0},{4,7},{5,6},{6,5},{7,4},{8,11},{9,10},{10,... | collective-permute-start | bytes 276488 | tf_op jit(solution)/shard_map/ppermute | solution.py:293
  9.1 0.1 collective-permute-start.1
  9.2 0.2 collective-permute-start.3
  9.4 1.4 %collective-permute-start.2 = (bf16[8,2880]{1,0:T(8,128)(2,1)S(1)}, bf16[8,2880]{1,0:T(8,128)(2,1)S(1)}, u32[]{:S(2)}, u32[]{:S(2)}) collective-permute-start(bf16[8,2880]{1,0:T(8,128)(2,1)S(1)} %collective-permute-done.refs_1_), channel_id=1, source_target_pairs={{0,2},{1,3},{2,0},{3,1},{4,6},{5,7},{6,4},{7,5},{8,10},{9,11},{10,... | collective-permute-start | bytes 138248 | tf_op jit(solution)/shard_map/ppermute | solution.py:293
  10.9 1.1 %collective-permute-start.4 = (bf16[8,2880]{1,0:T(8,128)(2,1)S(1)}, bf16[8,2880]{1,0:T(8,128)(2,1)S(1)}, u32[]{:S(2)}, u32[]{:S(2)}) collective-permute-start(bf16[8,2880]{1,0:T(8,128)(2,1)S(1)} %collective-permute-done.refs_1_), channel_id=1, source_target_pairs={{0,1},{1,0},{2,3},{3,2},{4,5},{5,4},{6,7},{7,6},{8,9},{9,8},{10,11... | collective-permute-start | bytes 138248 | tf_op jit(solution)/shard_map/ppermute | solution.py:293
  12.0 0.0 collective-permute-done.1.refs_2_
  12.0 0.1 collective-permute-done.3.refs_4_
  12.1 0.4 collective-permute-done.2.refs_3_
  12.5 2.1 %collective-permute-done.4.refs_5_ = bf16[8,2880]{1,0:T(8,128)(2,1)S(1)} collective-permute-done((bf16[8,2880]{1,0:T(8,128)(2,1)S(1)}, bf16[8,2880]{1,0:T(8,128)(2,1)S(1)}, u32[]{:S(2)}, u32[]{:S(2)}) %collective-permute-start.4) | collective-permute-done | bytes 46112 | tf_op jit(solution)/shard_map/ppermute | solution.py:293
  14.6 0.0 collective-permute-done.5.refs_6_
  14.6 0.0 copy-done
  14.6 0.0 copy-done.1
  14.6 0.0 copy-done.2
  14.6 2.7 %expert_main.1 = (bf16[64,2880]{1,0:T(8,128)(2,1)S(1)}, bf16[64,360]{1,0:T(8,128)(2,1)S(1)}, bf16[64,360]{1,0:T(8,128)(2,1)S(1)}, bf16[64,360]{1,0:T(8,128)(2,1)...) custom-call(bf16[8,2880]{1,0:T(8,128)(2,1)S(1)} %select.1.refs_0_, ...), custom_call_target="tpu_custom_call" | custom-call | flops 663552000 | bytes 6220800 | tf_op jit(solution)/shard_map/expert_main/pallas_call | solution.py:196
  17.4 5.0 %collective-permute-start.6 = (bf16[16,3008]{1,0:T(8,128)(2,1)S(1)}, bf16[16,3008]{1,0:T(8,128)(2,1)S(1)}, u32[]{:S(2)}, u32[]{:S(2)}) collective-permute-start(bf16[16,3008]{1,0:T(8,128)(2,1)S(1)} %get-tuple-element.24), channel_id=1, source_target_pairs={{8,0},{9,1},{10,2},{11,3},{12,4},{13,5},{14,6},{15,7},{16,8},{17,9... | collective-permute-start | bytes 288776 | tf_op jit(solution)/shard_map/ppermute | solution.py:303
  22.4 2.4 %collective-permute-start.7 = (bf16[16,2880]{1,0:T(8,128)(2,1)S(1)}, bf16[16,2880]{1,0:T(8,128)(2,1)S(1)}, u32[]{:S(2)}, u32[]{:S(2)}) collective-permute-start(bf16[16,2880]{1,0:T(8,128)(2,1)S(1)} %get-tuple-element.25), channel_id=1, source_target_pairs={{8,1},{9,0},{10,3},{11,2},{12,5},{13,4},{14,7},{15,6},{16,9},{17,8... | collective-permute-start | bytes 276488 | tf_op jit(solution)/shard_map/ppermute | solution.py:303
  24.8 1.6 %weight_grads.3 = bf16[360,2880]{1,0:T(8,128)(2,1)} custom-call(bf16[64,360]{1,0:T(8,128)(2,1)S(1)} %get-tuple-element.23.refs_0_, bf16[64,2880]{1,0:T(8,128)(2,1)S(1)} %get-tuple-element.20.refs_2_.refs_1_), custom_call_target="tpu_custom_call" | custom-call | flops 132710400 | bytes 4147200 | tf_op jit(solution)/shard_map/weight_grads/pallas_call | solution.py:234
  26.5 2.4 %weight_grads.2 = (bf16[360,2880]{1,0:T(8,128)(2,1)}, bf16[360,2880]{1,0:T(8,128)(2,1)}) custom-call(bf16[64,360]{1,0:T(8,128)(2,1)S(1)} %get-tuple-element.18.refs_0_, bf16[64,360]{1,0:T(8,128)(2,1)S(1)} %get-tuple-element.19.refs_1_, bf16[64,2880]{1,0:T(8,128)(2,1)S(1)} %get-tuple-element.20.refs_2_.refs_1_), custom_call_target="tpu_custom_call" | custom-call | flops 265420800 | bytes 8294400 | tf_op jit(solution)/shard_map/weight_grads/pallas_call | solution.py:234
  28.9 0.0 collective-permute-done.6
  28.9 0.7 %collective-permute-done.7 = bf16[16,2880]{1,0:T(8,128)(2,1)S(1)} collective-permute-done((bf16[16,2880]{1,0:T(8,128)(2,1)S(1)}, bf16[16,2880]{1,0:T(8,128)(2,1)S(1)}, u32[]{:S(2)}, u32[]{:S(2)}) %collective-permute-start.7) | collective-permute-done | bytes 92192 | tf_op jit(solution)/shard_map/ppermute | solution.py:303
  29.7 2.8 %collective-permute-start.8 = (bf16[4,2880]{1,0:T(4,128)(2,1)S(1)}, bf16[4,2880]{1,0:T(4,128)(2,1)S(1)}, u32[]{:S(2)}, u32[]{:S(2)}) collective-permute-start(bf16[4,2880]{1,0:T(4,128)(2,1)S(1)} %get-tuple-element.30), channel_id=1, source_target_pairs={{0,4},{1,5},{2,6},{3,7},{4,0},{5,1},{6,2},{7,3},{8,12},{9,13},{10,... | collective-permute-start | bytes 69128 | tf_op jit(solution)/shard_map/ppermute | solution.py:293
  32.5 0.0 collective-permute-start.9
  32.5 0.4 collective-permute-start.10
  32.8 0.1 slice.26
  32.9 0.1 pad_maximum_fusion.kept_ref
  33.0 1.0 %collective-permute-done.8.refs_0_ = bf16[4,2880]{1,0:T(4,128)(2,1)S(1)} collective-permute-done((bf16[4,2880]{1,0:T(4,128)(2,1)S(1)}, bf16[4,2880]{1,0:T(4,128)(2,1)S(1)}, u32[]{:S(2)}, u32[]{:S(2)}) %collective-permute-start.8) | collective-permute-done | bytes 23072 | tf_op jit(solution)/shard_map/ppermute | solution.py:293
  33.9 3.0 %collective-permute-done.9.refs_1_ = bf16[4,2880]{1,0:T(4,128)(2,1)S(1)} collective-permute-done((bf16[4,2880]{1,0:T(4,128)(2,1)S(1)}, bf16[4,2880]{1,0:T(4,128)(2,1)S(1)}, u32[]{:S(2)}, u32[]{:S(2)}) %collective-permute-start.9) | collective-permute-done | bytes 23072 | tf_op jit(solution)/shard_map/ppermute | solution.py:293
  36.9 0.0 collective-permute-done.10.refs_2_
  36.9 1.1 %expand.1 = bf16[64,2880]{1,0:T(8,128)(2,1)} custom-call(f32[4,3008]{1,0:T(4,128)S(1)} %pad_maximum_fusion.kept_ref, bf16[4,2880]{1,0:T(4,128)(2,1)S(1)} %collective-permute-done.8.refs_0_, bf16[4,2880]{1,0:T(4,128)(2,1)S(1)} %collective-permute-done.9.refs_1_, bf16[4,2880]{1,0:T(4,128)(2,1)S(1)} %collective-permute-done.10.refs_2_), custom_call_target="tpu_custom_call" | custom-call | tf_op jit(solution)/shard_map/expand/pallas_call | solution.py:277
  (5 shorter events, 0.1 us)
Async XLA Ops:
  0.6 1.0 %copy-start.3 = (bf16[1,64,2880]{2,1,0:T(8,128)(2,1)S(1)}, bf16[1,64,2880]{2,1,0:T(8,128)(2,1)}, u32[]{:S(2)}) copy-start(bf16[1,64,2880]{2,1,0:T(8,128)(2,1)} %param.7) | copy-start | bytes 1105924
  0.6 1.1 %copy-start.4 = (bf16[1,64,2880]{2,1,0:T(8,128)(2,1)S(1)}, bf16[1,64,2880]{2,1,0:T(8,128)(2,1)}, u32[]{:S(2)}) copy-start(bf16[1,64,2880]{2,1,0:T(8,128)(2,1)} %param.8) | copy-start | bytes 1105924
  2.0 12.6 %copy-start = (bf16[1,360,2880]{2,1,0:T(8,128)(2,1)S(1)}, bf16[1,360,2880]{2,1,0:T(8,128)(2,1)}, u32[]{:S(2)}) copy-start(bf16[1,360,2880]{2,1,0:T(8,128)(2,1)} %param.11) | copy-start | bytes 6220804
  2.0 12.6 %copy-start.1 = (bf16[1,360,2880]{2,1,0:T(8,128)(2,1)S(1)}, bf16[1,360,2880]{2,1,0:T(8,128)(2,1)}, u32[]{:S(2)}) copy-start(bf16[1,360,2880]{2,1,0:T(8,128)(2,1)} %param.12) | copy-start | bytes 6220804
  2.0 12.6 %copy-start.2 = (bf16[1,360,2880]{2,1,0:T(8,128)(2,1)S(1)}, bf16[1,360,2880]{2,1,0:T(8,128)(2,1)}, u32[]{:S(2)}) copy-start(bf16[1,360,2880]{2,1,0:T(8,128)(2,1)} %param.13) | copy-start | bytes 6220804
  2.0 4.7 %collective-permute-start = (bf16[8,2880]{1,0:T(8,128)(2,1)S(1)}, bf16[8,2880]{1,0:T(8,128)(2,1)S(1)}, u32[]{:S(2)}, u32[]{:S(2)}) collective-permute-start(bf16[8,2880]{1,0:T(8,128)(2,1)S(1)} %select.1.refs_0_), channel_id=1, source_target_pairs={{0,4},{1,5},{2,6},{3,7},{4,0},{5,1},{6,2},{7,3},{8,12},{9,13},{10,... | collective-permute-start | bytes 138248 | tf_op jit(solution)/shard_map/ppermute | solution.py:293
  6.7 7.9 %collective-permute-start.5 = (bf16[16,2880]{1,0:T(8,128)(2,1)S(1)}, bf16[16,2880]{1,0:T(8,128)(2,1)S(1)}, u32[]{:S(2)}, u32[]{:S(2)}) collective-permute-start(bf16[16,2880]{1,0:T(8,128)(2,1)S(1)} %join.1), channel_id=1, source_target_pairs={{0,3},{1,2},{2,1},{3,0},{4,7},{5,6},{6,5},{7,4},{8,11},{9,10},{10,... | collective-permute-start | bytes 276488 | tf_op jit(solution)/shard_map/ppermute | solution.py:293
  9.1 2.9 %collective-permute-start.1 = (bf16[8,2880]{1,0:T(8,128)(2,1)S(1)}, bf16[8,2880]{1,0:T(8,128)(2,1)S(1)}, u32[]{:S(2)}, u32[]{:S(2)}) collective-permute-start(bf16[8,2880]{1,0:T(8,128)(2,1)S(1)} %select.1.refs_0_), channel_id=1, source_target_pairs={{0,2},{1,3},{2,0},{3,1},{4,6},{5,7},{6,4},{7,5},{8,10},{9,11},{10,... | collective-permute-start | bytes 138248 | tf_op jit(solution)/shard_map/ppermute | solution.py:293
  9.2 2.9 %collective-permute-start.3 = (bf16[8,2880]{1,0:T(8,128)(2,1)S(1)}, bf16[8,2880]{1,0:T(8,128)(2,1)S(1)}, u32[]{:S(2)}, u32[]{:S(2)}) collective-permute-start(bf16[8,2880]{1,0:T(8,128)(2,1)S(1)} %select.1.refs_0_), channel_id=1, source_target_pairs={{0,1},{1,0},{2,3},{3,2},{4,5},{5,4},{6,7},{7,6},{8,9},{9,8},{10,11... | collective-permute-start | bytes 138248 | tf_op jit(solution)/shard_map/ppermute | solution.py:293
  9.4 3.1 %collective-permute-start.2 = (bf16[8,2880]{1,0:T(8,128)(2,1)S(1)}, bf16[8,2880]{1,0:T(8,128)(2,1)S(1)}, u32[]{:S(2)}, u32[]{:S(2)}) collective-permute-start(bf16[8,2880]{1,0:T(8,128)(2,1)S(1)} %collective-permute-done.refs_1_), channel_id=1, source_target_pairs={{0,2},{1,3},{2,0},{3,1},{4,6},{5,7},{6,4},{7,5},{8,10},{9,11},{10,... | collective-permute-start | bytes 138248 | tf_op jit(solution)/shard_map/ppermute | solution.py:293
  10.9 3.8 %collective-permute-start.4 = (bf16[8,2880]{1,0:T(8,128)(2,1)S(1)}, bf16[8,2880]{1,0:T(8,128)(2,1)S(1)}, u32[]{:S(2)}, u32[]{:S(2)}) collective-permute-start(bf16[8,2880]{1,0:T(8,128)(2,1)S(1)} %collective-permute-done.refs_1_), channel_id=1, source_target_pairs={{0,1},{1,0},{2,3},{3,2},{4,5},{5,4},{6,7},{7,6},{8,9},{9,8},{10,11... | collective-permute-start | bytes 138248 | tf_op jit(solution)/shard_map/ppermute | solution.py:293
  17.4 11.5 %collective-permute-start.6 = (bf16[16,3008]{1,0:T(8,128)(2,1)S(1)}, bf16[16,3008]{1,0:T(8,128)(2,1)S(1)}, u32[]{:S(2)}, u32[]{:S(2)}) collective-permute-start(bf16[16,3008]{1,0:T(8,128)(2,1)S(1)} %get-tuple-element.24), channel_id=1, source_target_pairs={{8,0},{9,1},{10,2},{11,3},{12,4},{13,5},{14,6},{15,7},{16,8},{17,9... | collective-permute-start | bytes 288776 | tf_op jit(solution)/shard_map/ppermute | solution.py:303
  22.4 7.2 %collective-permute-start.7 = (bf16[16,2880]{1,0:T(8,128)(2,1)S(1)}, bf16[16,2880]{1,0:T(8,128)(2,1)S(1)}, u32[]{:S(2)}, u32[]{:S(2)}) collective-permute-start(bf16[16,2880]{1,0:T(8,128)(2,1)S(1)} %get-tuple-element.25), channel_id=1, source_target_pairs={{8,1},{9,0},{10,3},{11,2},{12,5},{13,4},{14,7},{15,6},{16,9},{17,8... | collective-permute-start | bytes 276488 | tf_op jit(solution)/shard_map/ppermute | solution.py:303
  29.7 4.3 %collective-permute-start.8 = (bf16[4,2880]{1,0:T(4,128)(2,1)S(1)}, bf16[4,2880]{1,0:T(4,128)(2,1)S(1)}, u32[]{:S(2)}, u32[]{:S(2)}) collective-permute-start(bf16[4,2880]{1,0:T(4,128)(2,1)S(1)} %get-tuple-element.30), channel_id=1, source_target_pairs={{0,4},{1,5},{2,6},{3,7},{4,0},{5,1},{6,2},{7,3},{8,12},{9,13},{10,... | collective-permute-start | bytes 69128 | tf_op jit(solution)/shard_map/ppermute | solution.py:293
  32.5 4.5 %collective-permute-start.9 = (bf16[4,2880]{1,0:T(4,128)(2,1)S(1)}, bf16[4,2880]{1,0:T(4,128)(2,1)S(1)}, u32[]{:S(2)}, u32[]{:S(2)}) collective-permute-start(bf16[4,2880]{1,0:T(4,128)(2,1)S(1)} %get-tuple-element.29), channel_id=1, source_target_pairs={{0,6},{1,7},{2,4},{3,5},{4,2},{5,3},{6,0},{7,1},{8,14},{9,15},{10,... | collective-permute-start | bytes 69128 | tf_op jit(solution)/shard_map/ppermute | solution.py:293
  32.5 4.5 %collective-permute-start.10 = (bf16[4,2880]{1,0:T(4,128)(2,1)S(1)}, bf16[4,2880]{1,0:T(4,128)(2,1)S(1)}, u32[]{:S(2)}, u32[]{:S(2)}) collective-permute-start(bf16[4,2880]{1,0:T(4,128)(2,1)S(1)} %get-tuple-element.28), channel_id=1, source_target_pairs={{0,2},{1,3},{2,0},{3,1},{4,6},{5,7},{6,4},{7,5},{8,10},{9,11},{10,... | collective-permute-start | bytes 69128 | tf_op jit(solution)/shard_map/ppermute | solution.py:293
